TPU v7x, 256 devices: a whole 4x4x8 slice. The times are simulated.
256 devices in a mesh: seq: 8 (over y, core), chan: 32 (over z, x).
Axes of the slice: x: 4, y: 4, z: 8, core: 2. Of those that a mesh axis runs over, the one named last changes fastest.
Arguments:
- tokens: bfloat16 [1024, 4096], P('seq', 'chan'), may hold values from -6 to 6
- in_weight: bfloat16 [4096, 3, 4096], P(None, None, 'chan'), may hold values from -0.09375 to 0.09375
- short_kernel: float32 [3, 3, 4096], P(None, None, 'chan'), may hold values from -3 to 3
- filters: float32 [2, 1024, 4096], P(None, 'seq', 'chan'), may hold values from -0.5 to 0.5
- skip_gain: float32 [2, 4096], P(None, 'chan'), may hold values from 0.5 to 1.5
- out_weight: bfloat16 [4096, 4096], P('chan'), may hold values from -0.09375 to 0.09375
- cotangent: bfloat16 [1024, 4096], P('seq', 'chan'), may hold values from -6 to 6
Outputs:
- mixed: bfloat16 [1024, 4096], P('seq', 'chan')
- token_grad: bfloat16 [1024, 4096], P('seq', 'chan')
All inputs are finite; a program needn't handle non-finite values.
Results may differ from a plain program's by a relative error of at most 0.0049.
Values may be sent and summed in bfloat16 or wider, within the bound.
No kernel may reach another device: no remote copies, remote signals or barrier semaphores. Data moves between devices by JAX's collectives and lax.ppermute only.
A program may use at most 64 MiB of HBM per device.

v0:
```python
import math

import jax
import jax.numpy as jnp
from jax import lax
from jax.sharding import PartitionSpec as P

PRECISE = lax.Precision.HIGHEST


def swapped(value, axis, apart):
    mask = 2**apart
    pairs = [(source, source ^ mask) for source in range(lax.axis_size(axis))]
    return lax.ppermute(value, axis, pairs)


def passed_along(value, axis, steps):
    count = lax.axis_size(axis)
    first, last = (max(0, -steps), min(count, count - steps))
    return lax.ppermute(value, axis, [(source, source + steps) for source in range(first, last)])


def rotate(real_part, imag_part, turn_angle):
    cosine = jnp.cos(turn_angle)
    sine_part = jnp.sin(turn_angle)
    return (real_part * cosine - imag_part * sine_part, real_part * sine_part + imag_part * cosine)


def block_dft(real_part, imag_part, flip_sign):
    full_shape = real_part.shape
    length = full_shape[-2]
    token_positions = jnp.arange(length, dtype=jnp.int32)
    table_angle = (
        2.0
        * math.pi
        / length
        * (token_positions[:, None] * token_positions[None, :] % length).astype(jnp.float32)
    )
    cosine = jnp.cos(table_angle)
    sine_part = flip_sign * jnp.sin(table_angle)
    summed = cosine + sine_part
    differ = sine_part - cosine
    flat_re = real_part.reshape((-1, length, full_shape[-1]))
    flat_im = imag_part.reshape((-1, length, full_shape[-1]))
    product_one = jnp.einsum("kn,anc->akc", cosine, flat_re + flat_im, precision=PRECISE)
    product_two = jnp.einsum("kn,anc->akc", summed, flat_im, precision=PRECISE)
    product_three = jnp.einsum("kn,anc->akc", differ, flat_re, precision=PRECISE)
    return (
        (product_one - product_two).reshape(full_shape),
        (product_one + product_three).reshape(full_shape),
    )


def twiddle(real_part, imag_part, column, full_length, flip_sign):
    row_ids = jnp.arange(real_part.shape[-2], dtype=jnp.int32)[:, None]
    turn_angle = (
        flip_sign
        * 2.0
        * math.pi
        / full_length
        * (column * row_ids % full_length).astype(jnp.float32)
    )
    return rotate(real_part, imag_part, turn_angle)


def reversed_index(seq_index, levels):
    flipped = jnp.zeros((), jnp.int32)
    for section_bit in range(levels):
        flipped = flipped + seq_index // 2**section_bit % 2 * 2 ** (levels - 1 - section_bit)
    return flipped


def spectrum(signal):
    seq_count = lax.axis_size("seq")
    levels = seq_count.bit_length() - 1
    seq_index = lax.axis_index("seq")
    blocks = signal.shape[1]
    full_length = 2 * seq_count * blocks
    quarter = jnp.arange(2, dtype=jnp.int32)
    lift_angle = -math.pi / seq_count * seq_index.astype(jnp.float32)
    real_part = jnp.stack([signal, signal * jnp.cos(lift_angle)])
    imag_part = jnp.stack([jnp.zeros_like(signal), signal * jnp.sin(lift_angle)])
    for section_bit in reversed(range(levels)):
        half_span = 2**section_bit
        other_re, other_im = swapped((real_part, imag_part), "seq", section_bit)
        is_upper = seq_index // half_span % 2 == 1
        phase_angle = -math.pi / half_span * (seq_index % half_span).astype(jnp.float32)
        diff_re, diff_im = rotate(other_re - real_part, other_im - imag_part, phase_angle)
        real_part = jnp.where(is_upper, diff_re, real_part + other_re)
        imag_part = jnp.where(is_upper, diff_im, imag_part + other_im)
    column = 2 * reversed_index(seq_index, levels) + quarter[:, None, None, None]
    real_part, imag_part = twiddle(real_part, imag_part, column, full_length, -1.0)
    return block_dft(real_part, imag_part, -1.0)


def restore(real_part, imag_part):
    seq_count = lax.axis_size("seq")
    levels = seq_count.bit_length() - 1
    seq_index = lax.axis_index("seq")
    blocks = real_part.shape[-2]
    full_length = 2 * seq_count * blocks
    quarter = jnp.arange(2, dtype=jnp.int32)
    real_part, imag_part = block_dft(real_part, imag_part, 1.0)
    real_part = real_part / blocks
    imag_part = imag_part / blocks
    column = 2 * reversed_index(seq_index, levels) + quarter[:, None, None, None]
    real_part, imag_part = twiddle(real_part, imag_part, column, full_length, 1.0)
    for section_bit in range(levels):
        half_span = 2**section_bit
        other_re, other_im = swapped((real_part, imag_part), "seq", section_bit)
        is_upper = seq_index // half_span % 2 == 1
        phase_angle = math.pi / half_span * (seq_index % half_span).astype(jnp.float32)
        turned_re, turned_im = rotate(other_re, other_im, phase_angle)
        local_rotated_real, own_turn_im = rotate(real_part, imag_part, phase_angle)
        new_re = jnp.where(is_upper, other_re - local_rotated_real, real_part + turned_re)
        new_im = jnp.where(is_upper, other_im - own_turn_im, imag_part + turned_im)
        real_part = 0.5 * new_re
        imag_part = 0.5 * new_im
    lift_angle = math.pi / seq_count * seq_index.astype(jnp.float32)
    return 0.5 * (
        real_part[0] + real_part[1] * jnp.cos(lift_angle) - imag_part[1] * jnp.sin(lift_angle)
    )


def product_of(left_pair, right_pair, conjugate):
    left_re, left_im = left_pair
    right_re, right_im = right_pair
    if conjugate:
        right_im = -right_im
    return (left_re * right_re - left_im * right_im, left_re * right_im + left_im * right_re)


def select_entry(pair, entry):
    return (pair[0][:, entry : entry + 1], pair[1][:, entry : entry + 1])


def on_device(tokens, in_weight, short_kernel, filters, skip_gain, out_weight, cotangent):
    chans = in_weight.shape[2]
    width = in_weight.shape[0]
    blocks = tokens.shape[0]
    flat_in = in_weight.reshape((width, 3 * chans))
    projected = jnp.dot(
        lax.all_gather(tokens, "chan", axis=1, tiled=True),
        flat_in,
        preferred_element_type=jnp.float32,
    )
    projected = projected.reshape((blocks, 3, chans))
    taps = short_kernel.shape[0]
    prior = passed_along(projected[blocks - (taps - 1) :], "seq", 1)
    padded = jnp.concatenate([prior, projected], axis=0)
    shorted = short_kernel[0] * projected
    for tap_index in range(1, taps):
        offset = taps - 1 - tap_index
        shorted = shorted + short_kernel[tap_index] * padded[offset : offset + blocks]
    values = shorted[:, 0]
    gate_one = shorted[:, 1]
    gate_two = shorted[:, 2]
    spectra = spectrum(jnp.stack([filters[0], filters[1], values]))
    conv_one = (
        restore(*product_of(select_entry(spectra, 2), select_entry(spectra, 0), False))[0]
        + skip_gain[0] * values
    )
    first_out = gate_one * conv_one
    first_spec = spectrum(first_out[None])
    conv_two = (
        restore(*product_of(first_spec, select_entry(spectra, 1), False))[0]
        + skip_gain[1] * first_out
    )
    second_order_output = (gate_two * conv_two).astype(jnp.bfloat16)
    picked = out_weight
    mixed = lax.psum_scatter(
        lax.dot_general(
            picked,
            second_order_output,
            (((0,), (1,)), ((), ())),
            preferred_element_type=jnp.float32,
        ),
        "chan",
        scatter_dimension=0,
        tiled=True,
    ).T.astype(jnp.bfloat16)
    grad_two = lax.dot_general(
        lax.all_gather(cotangent, "chan", axis=1, tiled=True),
        out_weight,
        (((1,), (1,)), ((), ())),
        preferred_element_type=jnp.float32,
    )
    grad_gate_two = grad_two * conv_two
    grad_conv_two = grad_two * gate_two
    grad_spec = spectrum(grad_conv_two[None])
    grad_first = (
        restore(*product_of(grad_spec, select_entry(spectra, 1), True))[0]
        + skip_gain[1] * grad_conv_two
    )
    first_gate_gradient = grad_first * conv_one
    grad_conv_one = grad_first * gate_one
    inner_spec = spectrum(grad_conv_one[None])
    grad_values = (
        restore(*product_of(inner_spec, select_entry(spectra, 0), True))[0]
        + skip_gain[0] * grad_conv_one
    )
    grad_short = jnp.stack([grad_values, first_gate_gradient, grad_gate_two], axis=1)
    later = passed_along(grad_short[: taps - 1], "seq", -1)
    padded_grad = jnp.concatenate([grad_short, later], axis=0)
    grad_proj = short_kernel[0] * grad_short
    for tap_index in range(1, taps):
        grad_proj = (
            grad_proj + short_kernel[tap_index] * padded_grad[tap_index : tap_index + blocks]
        )
    grad_proj = grad_proj.astype(jnp.bfloat16)
    grad_flat = grad_proj.reshape((blocks, 3 * chans))
    picked = flat_in
    token_grad = lax.psum_scatter(
        lax.dot_general(
            picked, grad_flat, (((1,), (1,)), ((), ())), preferred_element_type=jnp.float32
        ),
        "chan",
        scatter_dimension=0,
        tiled=True,
    ).T.astype(jnp.bfloat16)
    return (mixed, token_grad)


def solution(mesh):
    in_specs = (
        P("seq", "chan"),
        P(None, None, "chan"),
        P(None, None, "chan"),
        P(None, "seq", "chan"),
        P(None, "chan"),
        P("chan", None),
        P("seq", "chan"),
    )
    out_specs = (P("seq", "chan"), P("seq", "chan"))
    return jax.shard_map(
        on_device, mesh=mesh, in_specs=in_specs, out_specs=out_specs, check_vma=False
    )
```

profile of v0, /device:TPU:8, one launch (start us, length us, event | category | flops | bytes accessed | tf_op | source)
XLA Modules:
  0.0 760.3 jit_solution(1646638522925081413)
XLA Ops:
  8.9 4.8 copy.188
  13.7 70.3 %all-gather.3.cloned.1.call-done = bf16[128,4096]{1,0:T(8,128)(2,1)} async-done(((bf16[128,128]{1,0:T(8,128)(2,1)}), bf16[128,4096]{1,0:T(8,128)(2,1)}) %all-gather.3.cloned.1.call-update) | async-done | bytes 1048592 | tf_op jit(solution)/shard_map/all_gather | solution.py:143
  84.0 3.3 fusion.349
  87.3 1.9 collective-permute-start
  89.3 66.9 %all-gather.5.cloned.1.call-done = bf16[128,4096]{1,0:T(8,128)(2,1)} async-done(((bf16[128,128]{1,0:T(8,128)(2,1)}), bf16[128,4096]{1,0:T(8,128)(2,1)}) %all-gather.5.cloned.1.call-update) | async-done | bytes 1048592 | tf_op jit(solution)/shard_map/all_gather | solution.py:183
  156.2 1.7 fusion.350
  158.3 2.2 collective-permute-start.1
  160.6 1.5 collective-permute-start.2
  162.1 2.2 collective-permute-start.25
  164.3 1.5 collective-permute-start.26
  166.2 13.1 %collective-permute-done.25 = f32[2,1,128,128]{3,2,1,0:T(8,128)S(1)} collective-permute-done((f32[2,1,128,128]{3,2,1,0:T(8,128)S(1)}, f32[2,1,128,128]{3,2,1,0:T(8,128)S(1)}, u32[]{:S(2)}, u32[]{:S(2)}) %collective-permute-start.25) | collective-permute-done | bytes 131104 | tf_op jit(solution)/shard_map/ppermute | solution.py:14
  179.3 2.8 collective-permute-done.26
  182.7 1.5 collective-permute-start.28
  186.1 1.5 collective-permute-start.4
  188.6 2.8 collective-permute-done.28
  192.0 6.9 collective-permute-done.3
  198.9 4.2 collective-permute-done.4
  213.6 1.4 collective-permute-start.34
  215.5 3.8 collective-permute-done.33
  219.4 2.2 collective-permute-done.34
  222.0 3.3 collective-permute-start.36
  225.3 4.2 collective-permute-done.35
  229.5 1.4 collective-permute-done.36
  232.0 2.8 collective-permute-start.38
  234.8 3.3 collective-permute-done.37
  238.1 1.4 collective-permute-done.38
  240.7 1.5 collective-permute-start.40
  242.2 2.4 collective-permute-done.39
  244.6 1.6 collective-permute-done.40
  255.5 4.3 collective-permute-done.10
  259.8 2.0 collective-permute-done.9
  261.9 2.1 collective-permute-start.11
  264.0 1.5 collective-permute-start.12
  265.6 4.2 collective-permute-done.11
  269.8 1.5 collective-permute-done.12
  271.5 1.8 collective-permute-start.13
  273.3 1.9 collective-permute-start.14
  275.2 3.5 collective-permute-done.13
  278.6 1.4 collective-permute-done.14
  280.1 1.4 collective-permute-start.15
  282.8 2.3 collective-permute-done.15
  285.1 1.5 collective-permute-done.16
  294.4 1.5 collective-permute-start.21
  296.5 4.3 collective-permute-done.21
  300.9 2.0 collective-permute-done.22
  303.0 2.0 collective-permute-start.23
  305.0 1.6 collective-permute-start.24
  306.6 4.3 collective-permute-done.23
  310.9 1.4 collective-permute-done.24
  312.5 1.7 convolution_bitcast_fusion.1
  316.0 1.4 collective-permute-start.45
  318.1 4.3 collective-permute-done.45
  322.5 2.2 collective-permute-done.46
  324.8 1.8 collective-permute-start.47
  326.5 1.8 collective-permute-start.48
  328.4 4.3 collective-permute-done.47
  332.6 1.4 collective-permute-done.48
  334.2 1.9 collective-permute-start.49
  336.1 1.3 collective-permute-done.49
  337.5 2.5 convolution_bitcast_fusion
  340.0 191.6 %reduce-scatter.3.cloned.1.call-done = f32[128,128]{0,1:T(8,128)} async-done(((f32[4096,128]{0,1:T(8,128)}), f32[128,128]{0,1:T(8,128)}) %reduce-scatter.3.cloned.1.call-update) | async-done | bytes 65552 | tf_op jit(solution)/shard_map/reduce_scatter | solution.py:171
  531.5 1.5 convert_bitcast_fusion.1
  533.0 219.1 %reduce-scatter.5.cloned.1.call-done = f32[128,128]{0,1:T(8,128)} async-done(((f32[4096,128]{0,1:T(8,128)}), f32[128,128]{0,1:T(8,128)}) %reduce-scatter.5.cloned.1.call-update) | async-done | bytes 65552 | tf_op jit(solution)/shard_map/reduce_scatter | solution.py:213
  752.1 1.5 convert_bitcast_fusion
  (170 shorter events, 41.3 us)
Async XLA Ops:
  7.2 149.0 %copy-start = (bf16[128,4096]{1,0:T(8,128)(2,1)S(1)}, bf16[128,4096]{1,0:T(8,128)(2,1)}, u32[]{:S(2)}) copy-start(bf16[128,4096]{1,0:T(8,128)(2,1)} %param.12) | copy-start | bytes 3145732
  7.2 76.8 %all-gather.3.cloned.1.call-start = ((), (), s32[]{:S(2)}) async-start(), calls=%async_computation.2 | async-start | bytes 1081344 | tf_op jit(solution)/shard_map/all_gather | solution.py:143
  7.9 148.3 %all-gather.5.cloned.1.call-start = ((), (), s32[]{:S(2)}) async-start(), calls=%async_computation.4 | async-start | bytes 1081344 | tf_op jit(solution)/shard_map/all_gather | solution.py:183
  8.7 522.9 %reduce-scatter.3.cloned.1.call-start = ((), (), s32[]{:S(2)}) async-start(), calls=%async_computation.3 | async-start | bytes 2162688 | tf_op jit(solution)/shard_map/reduce_scatter | solution.py:171
  13.7 144.4 %copy-start.3 = (f32[3,128]{1,0:T(4,128)}, f32[3,128]{1,0:T(4,128)S(1)}, u32[]{:S(2)}) copy-start(f32[3,128]{1,0:T(4,128)S(1)} %get-tuple-element.98) | copy-start | bytes 4612
  84.0 74.2 %copy-start.2 = (f32[2,128,128]{2,1,0:T(8,128)S(1)}, f32[2,128,128]{2,1,0:T(8,128)}, u32[]{:S(2)}) copy-start(f32[2,128,128]{2,1,0:T(8,128)} %param.10) | copy-start | bytes 393220
  87.3 70.8 %collective-permute-start = (f32[2,3,128]{2,0,1:T(2,128)S(1)}, f32[2,3,128]{2,0,1:T(2,128)S(1)}, u32[]{:S(2)}, u32[]{:S(2)}) collective-permute-start(f32[2,3,128]{2,0,1:T(2,128)S(1)} %slice_bitcast_fusion.13), channel_id=1, source_target_pairs={{0,32},{32,64},{64,96},{96,128},{128,160},{160,192},{192,224},{1,3... | collective-permute-start | bytes 9224 | tf_op jit(solution)/shard_map/ppermute | solution.py:20
  158.3 25.9 %collective-permute-start.1 = (f32[2,3,128,128]{3,2,1,0:T(8,128)S(1)}, f32[2,3,128,128]{3,2,1,0:T(8,128)}, u32[]{:S(2)}, u32[]{:S(2)}) collective-permute-start(f32[2,3,128,128]{3,2,1,0:T(8,128)S(1)} %pad_maximum_fusion), channel_id=1, source_target_pairs={{0,128},{32,160},{64,192},{96,224},{128,0},{160,32},{192,64},{224,... | collective-permute-start | bytes 1179656 | tf_op jit(solution)/shard_map/ppermute | solution.py:14
  160.6 23.7 %collective-permute-start.2 = (f32[2,3,128,128]{3,2,1,0:T(8,128)S(1)}, f32[2,3,128,128]{3,2,1,0:T(8,128)}, u32[]{:S(2)}, u32[]{:S(2)}) collective-permute-start(f32[2,3,128,128]{3,2,1,0:T(8,128)S(1)} %stack.71), channel_id=1, source_target_pairs={{0,128},{32,160},{64,192},{96,224},{128,0},{160,32},{192,64},{224,... | collective-permute-start | bytes 1179656 | tf_op jit(solution)/shard_map/ppermute | solution.py:14
  162.1 17.1 %collective-permute-start.25 = (f32[2,1,128,128]{3,2,1,0:T(8,128)S(1)}, f32[2,1,128,128]{3,2,1,0:T(8,128)S(1)}, u32[]{:S(2)}, u32[]{:S(2)}) collective-permute-start(f32[2,1,128,128]{3,2,1,0:T(8,128)S(1)} %pad_maximum_fusion.6), channel_id=1, source_target_pairs={{0,128},{32,160},{64,192},{96,224},{128,0},{160,32},{192,64},{224,... | collective-permute-start | bytes 393224 | tf_op jit(solution)/shard_map/ppermute | solution.py:14
  164.3 17.7 %collective-permute-start.26 = (f32[2,1,128,128]{3,2,1,0:T(8,128)S(1)}, f32[2,1,128,128]{3,2,1,0:T(8,128)S(1)}, u32[]{:S(2)}, u32[]{:S(2)}) collective-permute-start(f32[2,1,128,128]{3,2,1,0:T(8,128)S(1)} %stack.77), channel_id=1, source_target_pairs={{0,128},{32,160},{64,192},{96,224},{128,0},{160,32},{192,64},{224,... | collective-permute-start | bytes 393224 | tf_op jit(solution)/shard_map/ppermute | solution.py:14
  182.1 6.5 collective-permute-start.27
  182.7 8.7 %collective-permute-start.28 = (f32[2,1,128,128]{3,2,0,1:T(8,128)S(1)}, f32[2,1,128,128]{3,2,0,1:T(8,128)S(1)}, u32[]{:S(2)}, u32[]{:S(2)}) collective-permute-start(f32[2,1,128,128]{3,2,0,1:T(8,128)S(1)} %get-tuple-element.81), channel_id=1, source_target_pairs={{0,64},{32,96},{64,0},{96,32},{128,192},{160,224},{192,128},{224,1... | collective-permute-start | bytes 393224 | tf_op jit(solution)/shard_map/ppermute | solution.py:14
  185.5 13.4 %collective-permute-start.3 = (f32[2,3,128,128]{3,2,1,0:T(8,128)S(1)}, f32[2,3,128,128]{3,2,1,0:T(8,128)S(1)}, u32[]{:S(2)}, u32[]{:S(2)}) collective-permute-start(f32[2,3,128,128]{3,2,1,0:T(8,128)S(1)} %get-tuple-element.51), channel_id=1, source_target_pairs={{0,64},{32,96},{64,0},{96,32},{128,192},{160,224},{192,128},{224,1... | collective-permute-start | bytes 1179656 | tf_op jit(solution)/shard_map/ppermute | solution.py:14
  186.1 17.0 %collective-permute-start.4 = (f32[2,3,128,128]{3,2,1,0:T(8,128)S(1)}, f32[2,3,128,128]{3,2,1,0:T(8,128)S(1)}, u32[]{:S(2)}, u32[]{:S(2)}) collective-permute-start(f32[2,3,128,128]{3,2,1,0:T(8,128)S(1)} %get-tuple-element.50), channel_id=1, source_target_pairs={{0,64},{32,96},{64,0},{96,32},{128,192},{160,224},{192,128},{224,1... | collective-permute-start | bytes 1179656 | tf_op jit(solution)/shard_map/ppermute | solution.py:14
  187.8 22.9 %copy-start.5 = (f32[2,128]{1,0:T(2,128)}, f32[2,128]{1,0:T(2,128)S(1)}, u32[]{:S(2)}) copy-start(f32[2,128]{1,0:T(2,128)S(1)} %get-tuple-element.103) | copy-start | bytes 3076
  187.8 22.9 %copy-start.7 = (f32[2,128]{1,0:T(2,128)}, f32[2,128]{1,0:T(2,128)S(1)}, u32[]{:S(2)}) copy-start(f32[2,128]{1,0:T(2,128)S(1)} %get-tuple-element.104) | copy-start | bytes 3076
  191.4 12.6 %collective-permute-start.29 = (f32[2,1,128,128]{3,2,0,1:T(8,128)S(1)}, f32[2,1,128,128]{3,2,0,1:T(8,128)S(1)}, u32[]{:S(2)}, u32[]{:S(2)}) collective-permute-start(f32[2,1,128,128]{3,2,0,1:T(8,128)S(1)} %get-tuple-element.78), channel_id=1, source_target_pairs={{0,32},{32,0},{64,96},{96,64},{128,160},{160,128},{192,224},{224,1... | collective-permute-start | bytes 393224 | tf_op jit(solution)/shard_map/ppermute | solution.py:14
  191.5 12.5 %collective-permute-start.30 = (f32[2,1,128,128]{3,2,0,1:T(8,128)S(1)}, f32[2,1,128,128]{3,2,0,1:T(8,128)S(1)}, u32[]{:S(2)}, u32[]{:S(2)}) collective-permute-start(f32[2,1,128,128]{3,2,0,1:T(8,128)S(1)} %get-tuple-element.79), channel_id=1, source_target_pairs={{0,32},{32,0},{64,96},{96,64},{128,160},{160,128},{192,224},{224,1... | collective-permute-start | bytes 393224 | tf_op jit(solution)/shard_map/ppermute | solution.py:14
  203.3 2.0 collective-permute-start.5
  203.4 2.3 collective-permute-start.6
  208.0 17.2 %copy-start.10 = (f32[2,128]{1,0:T(2,128)S(1)}, f32[2,128]{1,0:T(2,128)}, u32[]{:S(2)}) copy-start(f32[2,128]{1,0:T(2,128)} %param.11) | copy-start | bytes 3076
  211.2 1.4 collective-permute-start.31
  211.5 1.4 collective-permute-start.32
  212.9 6.5 collective-permute-start.33
  213.6 7.9 %collective-permute-start.34 = (f32[2,1,128,128]{3,2,1,0:T(8,128)S(1)}, f32[2,1,128,128]{3,2,1,0:T(8,128)S(1)}, u32[]{:S(2)}, u32[]{:S(2)}) collective-permute-start(f32[2,1,128,128]{3,2,1,0:T(8,128)S(1)} %get-tuple-element.74), channel_id=1, source_target_pairs={{0,64},{32,96},{64,0},{96,32},{128,192},{160,224},{192,128},{224,1... | collective-permute-start | bytes 393224 | tf_op jit(solution)/shard_map/ppermute | solution.py:14
  221.7 7.9 %collective-permute-start.35 = (f32[2,1,128,128]{3,2,1,0:T(8,128)S(1)}, f32[2,1,128,128]{3,2,1,0:T(8,128)S(1)}, u32[]{:S(2)}, u32[]{:S(2)}) collective-permute-start(f32[2,1,128,128]{3,2,1,0:T(8,128)S(1)} %get-tuple-element.72), channel_id=1, source_target_pairs={{0,128},{32,160},{64,192},{96,224},{128,0},{160,32},{192,64},{224,... | collective-permute-start | bytes 393224 | tf_op jit(solution)/shard_map/ppermute | solution.py:14
  222.0 8.9 %collective-permute-start.36 = (f32[2,1,128,128]{3,2,1,0:T(8,128)S(1)}, f32[2,1,128,128]{3,2,1,0:T(8,128)S(1)}, u32[]{:S(2)}, u32[]{:S(2)}) collective-permute-start(f32[2,1,128,128]{3,2,1,0:T(8,128)S(1)} %get-tuple-element.17), channel_id=1, source_target_pairs={{0,128},{32,160},{64,192},{96,224},{128,0},{160,32},{192,64},{224,... | collective-permute-start | bytes 393224 | tf_op jit(solution)/shard_map/ppermute | solution.py:14
  231.1 7.0 collective-permute-start.37
  232.0 7.5 collective-permute-start.38
  239.5 11.3 %copy-start.6 = (f32[2,128]{1,0:T(2,128)S(1)}, f32[2,128]{1,0:T(2,128)}, u32[]{:S(2)}) copy-start(f32[2,128]{1,0:T(2,128)} %copy-done.5) | copy-start | bytes 3076
  239.6 11.3 %copy-start.8 = (f32[2,128]{1,0:T(2,128)S(1)}, f32[2,128]{1,0:T(2,128)}, u32[]{:S(2)}) copy-start(f32[2,128]{1,0:T(2,128)} %copy-done.7) | copy-start | bytes 3076
  239.6 5.1 collective-permute-start.39
  240.7 5.5 collective-permute-start.40
  246.2 1.4 collective-permute-start.41
  246.4 1.6 collective-permute-start.42
  251.4 1.4 collective-permute-start.7
  251.9 1.3 collective-permute-start.8
  253.3 6.5 collective-permute-start.10
  254.4 7.4 collective-permute-start.9
  261.9 7.9 %collective-permute-start.11 = (f32[2,1,128,128]{3,2,0,1:T(8,128)S(1)}, f32[2,1,128,128]{3,2,0,1:T(8,128)S(1)}, u32[]{:S(2)}, u32[]{:S(2)}) collective-permute-start(f32[2,1,128,128]{3,2,0,1:T(8,128)S(1)} %get-tuple-element.68), channel_id=1, source_target_pairs={{0,128},{32,160},{64,192},{96,224},{128,0},{160,32},{192,64},{224,... | collective-permute-start | bytes 393224 | tf_op jit(solution)/shard_map/ppermute | solution.py:14
  264.0 7.3 collective-permute-start.12
  271.5 7.2 collective-permute-start.13
  273.3 6.7 collective-permute-start.14
  280.1 5.1 collective-permute-start.15
  281.5 5.1 collective-permute-start.16
  286.6 1.4 collective-permute-start.17
  286.8 1.7 collective-permute-start.18
  292.5 1.4 collective-permute-start.19
  293.0 1.3 collective-permute-start.20
  294.4 6.5 collective-permute-start.21
  295.9 7.0 collective-permute-start.22
  303.0 7.9 %collective-permute-start.23 = (f32[2,1,128,128]{3,2,0,1:T(8,128)S(1)}, f32[2,1,128,128]{3,2,0,1:T(8,128)S(1)}, u32[]{:S(2)}, u32[]{:S(2)}) collective-permute-start(f32[2,1,128,128]{3,2,0,1:T(8,128)S(1)} %get-tuple-element.64), channel_id=1, source_target_pairs={{0,128},{32,160},{64,192},{96,224},{128,0},{160,32},{192,64},{224,... | collective-permute-start | bytes 393224 | tf_op jit(solution)/shard_map/ppermute | solution.py:14
  305.0 7.4 collective-permute-start.24
  314.2 23.2 %copy-start.4 = (f32[3,128]{1,0:T(4,128)S(1)}, f32[3,128]{1,0:T(4,128)}, u32[]{:S(2)}) copy-start(f32[3,128]{1,0:T(4,128)} %copy-done.3) | copy-start | bytes 4612
  314.3 437.8 %reduce-scatter.5.cloned.1.call-start = ((), (), s32[]{:S(2)}) async-start(), calls=%async_computation.5 | async-start | bytes 2162688 | tf_op jit(solution)/shard_map/reduce_scatter | solution.py:213
  314.3 23.2 %copy-start.1 = (bf16[4096,3,128]{2,0,1:T(8,128)(2,1)S(1)}, bf16[4096,3,128]{2,0,1:T(8,128)(2,1)}, u32[]{:S(2)}) copy-start(bf16[4096,3,128]{2,0,1:T(8,128)(2,1)} %param.8) | copy-start | bytes 9437188
  314.3 1.4 collective-permute-start.43
  314.4 1.5 collective-permute-start.44
  316.0 6.5 collective-permute-start.45
  317.5 7.2 collective-permute-start.46
  324.8 7.9 %collective-permute-start.47 = (f32[2,1,128,128]{3,2,1,0:T(8,128)S(1)}, f32[2,1,128,128]{3,2,1,0:T(8,128)S(1)}, u32[]{:S(2)}, u32[]{:S(2)}) collective-permute-start(f32[2,1,128,128]{3,2,1,0:T(8,128)S(1)} %broadcast_multiply_fusion.4), channel_id=1, source_target_pairs={{0,128},{32,160},{64,192},{96,224},{128,0},{160,32},{192,64},{224,... | collective-permute-start | bytes 393224 | tf_op jit(solution)/shard_map/ppermute | solution.py:14
  326.5 7.5 collective-permute-start.48
  334.2 3.2 collective-permute-start.49
  (1 other events, 4.9 us)
Sparse Core Ops, SparseCore 0:
  10.4 73.5 all-gather.2
  86.5 69.6 all-gather.4
  314.4 217.0 reduce-scatter.2
  535.2 216.8 reduce-scatter.4
where the time goes:
time: 768 us; the launch traced here: 760 us
  waiting for transfers between devices  653 us (85%)
  starting transfers between devices  56 us (7%)
  matrix products  23.4 us (3%)
  between operations  15.7 us (2%)
    reduce_scatter x1, waiting for transfers between devices, on_device(): lax.psum_scatter(lax.dot_general(picked, grad_flat, (((1,), (1,)), ((), (...  219 us
    reduce_scatter x1, waiting for transfers between devices, on_device(): lax.psum_scatter(lax.dot_general(picked, second_order_output, (((0,), (1,...  192 us
    ppermute x48, waiting for transfers between devices, swapped(): return lax.ppermute(value, axis, pairs)  102 us
    all_gather x1, waiting for transfers between devices, on_device(): lax.all_gather(tokens, 'chan', axis=1, tiled=True)  70.3 us
    all_gather x1, waiting for transfers between devices, on_device(): lax.all_gather(cotangent, 'chan', axis=1, tiled=True)  66.9 us
    ppermute x48, starting transfers between devices, swapped(): return lax.ppermute(value, axis, pairs)  52 us
  transfers between devices with their start and end apart: 54, of which 47 were waited for; matrix products, arithmetic and copies ran while one was open for 2% of the time, Pallas kernels for 0%

commit v1 on v0

v1 whole, which is shorter than its diff:
```python
import functools
import math

import jax
import jax.numpy as jnp
import numpy as np
from jax import lax
from jax.experimental import pallas as pl
from jax.experimental.pallas import tpu as pltpu
from jax.sharding import Mesh, PartitionSpec as P


F32 = jnp.float32
BF16 = jnp.bfloat16
LANES = 128
BLOCKS = 8
COARSE = 2 * BLOCKS
KEPT = COARSE // 2 + 1
SEQ = ("y", "core")


def fine_table():
    ids = np.arange(LANES)
    angle = 2.0 * np.pi / LANES * (ids[:, None] * ids[None, :] % LANES)
    table = np.stack([np.cos(angle), np.sin(angle)]).astype(np.float32)
    high = table.astype(jnp.bfloat16)
    low = (table - high.astype(np.float32)).astype(jnp.bfloat16)
    return np.stack([high, low])


def fine_matrices(table_ref):
    found = []
    for part in range(2):
        cosine, sine = table_ref[part, 0], table_ref[part, 1]
        upper = jnp.concatenate([cosine, -sine], axis=1)
        found.append(jnp.concatenate([upper, jnp.concatenate([sine, cosine], axis=1)], axis=0))
    return found


def twiddle_table():
    angle = (
        2.0 * np.pi / (COARSE * LANES) * (np.arange(KEPT)[:, None] * np.arange(LANES)[None, :])
    )
    return np.stack([np.cos(angle), np.sin(angle)]).astype(np.float32)


def coarse(index):
    index = index % COARSE
    cosine = math.cos(2.0 * math.pi * index / COARSE)
    sine = math.sin(2.0 * math.pi * index / COARSE)
    return cosine, sine


def add_term(total, value, factor):
    if abs(factor) < 1e-9:
        return total
    if abs(abs(factor) - 1.0) < 1e-9:
        if total is None:
            return value if factor > 0 else -value
        return total + value if factor > 0 else total - value
    return value * factor if total is None else total + value * factor


def precise_dot(value, matrices):
    high = value.astype(BF16)
    low = (value - high.astype(F32)).astype(BF16)
    dot = functools.partial(jnp.dot, preferred_element_type=F32)
    return (dot(low, matrices[0]) + dot(high, matrices[1])) + dot(high, matrices[0])


def spectrum(signal, matrices, twiddle_ref):
    parts = []
    for freq in range(KEPT):
        real = imag = None
        for block in range(BLOCKS):
            cosine, sine = coarse(block * freq)
            real = add_term(real, signal[block], cosine)
            imag = add_term(imag, signal[block], -sine)
        cos_t = twiddle_ref[0, freq : freq + 1, :]
        sin_t = twiddle_ref[1, freq : freq + 1, :]
        if imag is None:
            turned = (real * cos_t, -real * sin_t)
        else:
            turned = (real * cos_t + imag * sin_t, imag * cos_t - real * sin_t)
        parts.append(jnp.concatenate(turned, axis=1))
    return precise_dot(jnp.concatenate(parts, axis=0), matrices)


def restore(turned_spec, matrices, twiddle_ref):
    rows = turned_spec.shape[0] // KEPT
    back = precise_dot(turned_spec, matrices)
    real, imag = [], []
    for freq in range(KEPT):
        piece = back[freq * rows : (freq + 1) * rows]
        re, minus_im = piece[:, :LANES], piece[:, LANES:]
        cos_t = twiddle_ref[0, freq : freq + 1, :]
        sin_t = twiddle_ref[1, freq : freq + 1, :]
        real.append(re * cos_t + minus_im * sin_t)
        imag.append(re * sin_t - minus_im * cos_t)
    out = []
    for block in range(BLOCKS):
        total = None
        for freq in range(1, KEPT - 1):
            cosine, sine = coarse(block * freq)
            total = add_term(total, real[freq], cosine)
            total = add_term(total, imag[freq], -sine)
        total = 2.0 * total + real[0]
        out.append(add_term(total, real[KEPT - 1], 1.0 if block % 2 == 0 else -1.0))
    return out


def turned_product(left, right, conjugate):
    left_re, left_im = left[:, :LANES], left[:, LANES:]
    right_re, right_im = right[:, :LANES], right[:, LANES:]
    straight, crossed = left_re * right_re, left_im * right_im
    if conjugate:
        real, minus_imag = straight + crossed, left_re * right_im - left_im * right_re
    else:
        real, minus_imag = straight - crossed, -(left_re * right_im + left_im * right_re)
    return jnp.concatenate([real, minus_imag], axis=1)


def lagged(blocks, steps):
    lane = lax.broadcasted_iota(jnp.int32, blocks[0].shape, 1)
    turned = [pltpu.roll(block, steps, 1) for block in blocks]
    before = [jnp.zeros_like(blocks[0])] + turned[:-1]
    return [jnp.where(lane >= steps, own, prior) for own, prior in zip(turned, before)]


def leading(blocks, steps):
    lane = lax.broadcasted_iota(jnp.int32, blocks[0].shape, 1)
    turned = [pltpu.roll(block, LANES - steps, 1) for block in blocks]
    after = turned[1:] + [jnp.zeros_like(blocks[0])]
    return [jnp.where(lane < LANES - steps, own, later) for own, later in zip(turned, after)]


def short_sum(blocks, coef_ref, which, shift):
    total = [coef_ref[which] * block for block in blocks]
    for tap in (1, 2):
        factor = coef_ref[3 * tap + which]
        total = [have + factor * block for have, block in zip(total, shift(blocks, tap))]
    return total


def operator_kernel(
    table_hbm, twiddle_hbm, given_ref, coef_ref, out_ref, table_ref, twiddle_ref, sems
):
    count = given_ref.shape[1] // 6
    tables_in = [
        *started([table_hbm], [table_ref], sems.at[0]),
        *started([twiddle_hbm], [twiddle_ref], sems.at[1]),
    ]

    def rows_of(slot):
        return [given_ref[block, slot * count : (slot + 1) * count] for block in range(BLOCKS)]

    def store(slot, blocks):
        for block, value in enumerate(blocks):
            out_ref[block, slot * count : (slot + 1) * count] = value.astype(BF16)

    def scaled(gain, blocks):
        return [coef_ref[gain] * value for value in blocks]

    def product(left, right):
        return [one * two for one, two in zip(left, right)]

    def plus(left, right):
        return [one + two for one, two in zip(left, right)]

    def filtered(blocks, order, conjugate):
        spec = turned_product(
            spectrum(blocks, matrices, twiddle_ref), filter_spec[order], conjugate
        )
        return plus(restore(spec, matrices, twiddle_ref), scaled(9 + order, blocks))

    values = short_sum(rows_of(0), coef_ref, 0, lagged)
    gate_one = short_sum(rows_of(1), coef_ref, 1, lagged)
    gate_two = short_sum(rows_of(2), coef_ref, 2, lagged)
    for copy in tables_in:
        copy.wait()
    matrices = fine_matrices(table_ref)
    filter_spec = [
        spectrum(rows_of(3 + order), matrices, twiddle_ref) * (1.0 / (COARSE * LANES))
        for order in range(2)
    ]
    conv_one = filtered(values, 0, False)
    conv_two = filtered(product(gate_one, conv_one), 1, False)
    store(0, product(gate_two, conv_two))
    grad_two = rows_of(5)
    store(3, short_sum(product(grad_two, conv_two), coef_ref, 2, leading))
    grad_first = filtered(product(grad_two, gate_two), 1, True)
    store(2, short_sum(product(grad_first, conv_one), coef_ref, 1, leading))
    grad_values = filtered(product(grad_first, gate_one), 0, True)
    store(1, short_sum(grad_values, coef_ref, 0, leading))


def started(source_refs, targets, sems):
    found = []
    for at, (source, target) in enumerate(zip(source_refs, targets)):
        copy = pltpu.make_async_copy(source, target, sems.at[at])
        copy.start()
        found.append(copy)
    return found


def weight_start(place_ref, z, apart, ring, feats):
    block = z * ring + lax.rem(place_ref[0] + apart, ring)
    return pl.multiple_of(block * feats, feats)


def chunks(ref, parts, axis):
    size = ref.shape[axis] // parts
    lead = (slice(None),) * axis
    return [ref.at[(*lead, pl.ds(part * size, size))] for part in range(parts)]


def project_kernel(
    ring,
    place_ref,
    weight_ref,
    filter_ref,
    own,
    left,
    right,
    far,
    out_ref,
    held,
    held_filter,
    sems,
):
    n_z, tokens, feats = own.shape
    (filter_copy,) = started([filter_ref], [held_filter], sems.at[1])
    copies_in = started(chunks(weight_ref, n_z, 1), chunks(held, n_z, 1), sems.at[0])
    chans = weight_ref.shape[2]
    count = chans // BLOCKS

    def store(slot, turned):
        for block in range(BLOCKS):
            out_ref[block, slot * count : (slot + 1) * count] = turned[
                block * count : (block + 1) * count
            ]

    filter_copy.wait()
    for order in range(2):
        store(3 + order, held_filter[order].T)
    total = [jnp.zeros((tokens, chans), F32)] * 3
    for z in range(n_z):
        copies_in[z].wait()
        for rows_ref, apart in ((own, 0), (right, 1), (far, 2), (left, 3)):
            start = weight_start(place_ref, z, apart, ring, feats)
            for which in range(3):
                total[which] = total[which] + jnp.dot(
                    rows_ref[z], held[which, pl.ds(start, feats), :], preferred_element_type=F32
                )
    for which in range(3):
        store(which, total[which].T)


def project_grad_kernel(
    ring, place_ref, weight_ref, own, left, right, far, given_ref, out_ref, held, sems
):
    n_z, tokens, feats = own.shape
    copies_in = started(chunks(weight_ref, n_z, 1), chunks(held, n_z, 1), sems)
    total = jnp.zeros((weight_ref.shape[0], tokens), F32)
    for z in range(n_z):
        copies_in[z].wait()
        for rows_ref, apart in ((own, 0), (right, 1), (far, 2), (left, 3)):
            start = weight_start(place_ref, z, apart, ring, feats)
            total = total + lax.dot_general(
                held[:, pl.ds(start, feats)],
                rows_ref[z],
                (((1,), (1,)), ((), ())),
                preferred_element_type=F32,
            )
    count = out_ref.shape[1] // 6
    out_ref[:, : 5 * count] = given_ref[...]
    out_ref[:, 5 * count :] = total.reshape((BLOCKS, count, tokens))


def partial_kernel(
    ring,
    place_ref,
    out_weight_ref,
    in_weight_ref,
    channels_ref,
    own_ref,
    right_ref,
    left_ref,
    keep_r_ref,
    keep_l_ref,
    held_out,
    held_in,
    sems,
):
    n_z, _, feats, tokens = own_ref.shape
    half = n_z // 2
    out_copies = started(chunks(out_weight_ref, n_z, 1), chunks(held_out, n_z, 1), sems.at[0])
    in_copies = started(chunks(in_weight_ref, n_z, 1), chunks(held_in, n_z, 1), sems.at[1])
    count = channels_ref.shape[1] // 4
    second, *grads = [
        channels_ref[:, slot * count : (slot + 1) * count].reshape((BLOCKS * count, tokens))
        for slot in range(4)
    ]
    second = second.astype(F32).T.astype(BF16)
    dot = functools.partial(jnp.dot, preferred_element_type=F32)

    def mixed(z, apart):
        start = weight_start(place_ref, z, apart, ring, feats)
        return dot(second, held_out[:, pl.ds(start, feats)])

    def token_grad(z, apart):
        start = weight_start(place_ref, z, apart, ring, feats)
        total = dot(held_in[0, pl.ds(start, feats), :], grads[0])
        for which in (1, 2):
            total = total + dot(held_in[which, pl.ds(start, feats), :], grads[which])
        return total

    for copy in out_copies + in_copies:
        copy.wait()
    for output, product in ((0, mixed), (1, token_grad)):
        for z in range(n_z):
            own_ref[z, output] = product(z, 0).astype(BF16)
            if z < half:
                right_ref[z, output] = product(z, 2).astype(BF16)
                keep_r_ref[z, output] = product(z, 1).astype(BF16)
                left_ref[z, output] = product(z, 3).astype(BF16)
            else:
                right_ref[z, output] = product(z, 1).astype(BF16)
                left_ref[z, output] = product(z, 2).astype(BF16)
                keep_l_ref[z - half, output] = product(z, 3).astype(BF16)


def merge_kernel(keep_r_ref, keep_l_ref, from_l_ref, from_r_ref, right_ref, left_ref):
    half = keep_r_ref.shape[0]
    right_ref[...] = (keep_r_ref[...].astype(F32) + from_l_ref[:half].astype(F32)).astype(BF16)
    left_ref[...] = (keep_l_ref[...].astype(F32) + from_r_ref[half:].astype(F32)).astype(BF16)


def ring_sum_kernel(own_ref, from_l_ref, from_r_ref, last_l_ref, last_r_ref, out_ref):
    half = last_l_ref.shape[0]
    own_low, own_high = own_ref[:half].astype(F32), own_ref[half:].astype(F32)
    out_ref[:half] = (
        own_low + last_l_ref[...].astype(F32) + from_r_ref[:half].astype(F32)
    ).astype(BF16)
    out_ref[half:] = (
        own_high + from_l_ref[half:].astype(F32) + last_r_ref[...].astype(F32)
    ).astype(BF16)


def last_sum_kernel(parts_ref, mixed_ref, token_grad_ref):
    totals = []
    for output in range(2):
        total = parts_ref[0, output].astype(F32)
        for part in range(1, parts_ref.shape[0]):
            total = total + parts_ref[part, output].astype(F32)
        totals.append(total)
    mixed_ref[...] = totals[0].astype(BF16)
    token_grad_ref[...] = totals[1].T.astype(BF16)


def run(kernel, out_shape, *args, flops=0, place=None, weights=()):
    single = not isinstance(out_shape, (list, tuple))
    outs = (out_shape,) if single else out_shape
    in_vmem = pl.BlockSpec(memory_space=pltpu.VMEM)
    specs, scratch = [in_vmem] * len(args), []
    if weights:
        held = (pltpu.with_memory_space_constraint(weight, pltpu.HBM) for weight in weights)
        places = () if place is None else (place,)
        args = (*places, *held, *args)
        in_hbm = [pl.BlockSpec(memory_space=pltpu.HBM)] * len(weights)
        specs = [pl.BlockSpec(memory_space=pltpu.SMEM)] * len(places) + in_hbm + specs
        scratch = [pltpu.VMEM(weight.shape, weight.dtype) for weight in weights]
        shape = (BLOCKS,) if len(weights) == 1 else (len(weights), BLOCKS)
        scratch.append(pltpu.SemaphoreType.DMA(shape))
    moved = sum(int(np.prod(a.shape)) * a.dtype.itemsize for a in (*args, *outs))
    return pl.pallas_call(
        kernel,
        out_shape=out_shape,
        in_specs=specs,
        out_specs=in_vmem if single else [in_vmem] * len(outs),
        scratch_shapes=scratch,
        compiler_params=pltpu.CompilerParams(vmem_limit_bytes=24 << 20),
        cost_estimate=pl.CostEstimate(flops=flops, bytes_accessed=moved, transcendentals=0),
    )(*args)


def shape_of(shape, dtype):
    return jax.ShapeDtypeStruct(shape, dtype)


def exchanged(value, axis):
    return lax.all_to_all(value, axis, 0, 0, tiled=True)


def copies(value, count):
    return jnp.broadcast_to(value[None], (count, *value.shape))


def shifted(value, steps):
    ring = lax.axis_size("x")
    return lax.ppermute(value, "x", [(at, (at + steps) % ring) for at in range(ring)])


def after(value, *others):
    return lax.optimization_barrier((value, *others))[0]


def gathered(own, steps):
    left, right = shifted(own, 1), shifted(own, -1)
    return left, right, shifted(left if steps > 0 else right, steps)


def on_device(tokens, in_weight, short_kernel, filters, skip_gain, out_weight, cotangent):
    width, _, chans = in_weight.shape
    rows = tokens.shape[0]
    n_z, ring = lax.axis_size("z"), lax.axis_size("x")
    half = n_z // 2
    count = chans // BLOCKS
    seq_index = lax.axis_index(SEQ)
    place = lax.axis_index("x").reshape((1,)).astype(jnp.int32)
    table = jnp.asarray(fine_table())
    twiddles = jnp.asarray(twiddle_table())
    split_in = in_weight.transpose((1, 0, 2))

    taps = lax.dynamic_slice_in_dim(short_kernel, seq_index * count, count, 2)
    gains = lax.dynamic_slice_in_dim(skip_gain, seq_index * count, count, 1)
    coef = jnp.concatenate([taps.reshape((9, count)), gains], axis=0)
    coef = jnp.broadcast_to(coef[:, :, None], (11, count, LANES))

    own_rows = exchanged(copies(tokens, n_z), "z")
    own_grads = exchanged(after(copies(cotangent, n_z), own_rows), "z")
    other_rows = gathered(own_rows, 1)
    other_grads = gathered(after(own_grads, *other_rows[:2]), -1)

    given = run(
        functools.partial(project_kernel, ring),
        shape_of((BLOCKS, 5 * count, rows), F32),
        own_rows,
        *other_rows,
        flops=2 * rows * width * 3 * chans,
        place=place,
        weights=(split_in, filters),
    )
    given = run(
        functools.partial(project_grad_kernel, ring),
        shape_of((BLOCKS, 6 * count, rows), F32),
        own_grads,
        *other_grads,
        given,
        flops=2 * rows * width * chans,
        place=place,
        weights=(out_weight,),
    )
    channels = run(
        operator_kernel,
        shape_of((BLOCKS, 4 * count, LANES), BF16),
        exchanged(given, SEQ),
        coef,
        weights=(table, twiddles),
    )
    whole, part = (n_z, 2, LANES, rows), (half, 2, LANES, rows)
    own, to_right, to_left, keep_r, keep_l = run(
        functools.partial(partial_kernel, ring),
        tuple(shape_of(shape, BF16) for shape in (whole, whole, whole, part, part)),
        exchanged(channels, SEQ),
        flops=2 * rows * width * 4 * chans,
        place=place,
        weights=(out_weight, split_in),
    )
    from_l, from_r = shifted(to_right, 1), shifted(to_left, -1)
    to_right, to_left = run(
        merge_kernel, (shape_of(part, BF16), shape_of(part, BF16)), keep_r, keep_l, from_l, from_r
    )
    last_l, last_r = shifted(to_right, 1), shifted(to_left, -1)
    parts = run(ring_sum_kernel, shape_of(whole, BF16), own, from_l, from_r, last_l, last_r)
    out = shape_of((rows, LANES), BF16)
    return run(last_sum_kernel, (out, out), exchanged(parts, "z"))


def solution(mesh):
    split = Mesh(mesh.devices.reshape((4, 2, 8, 4)), ("y", "core", "z", "x"))
    chan = ("z", "x")
    in_specs = (
        P(SEQ, chan),
        P(None, None, chan),
        P(None, None, chan),
        P(None, SEQ, chan),
        P(None, chan),
        P(chan, None),
        P(SEQ, chan),
    )
    out_specs = (P(SEQ, chan), P(SEQ, chan))

    return jax.shard_map(
        on_device, mesh=split, in_specs=in_specs, out_specs=out_specs, check_vma=False
    )
```

time: 768 us -> 131 us (0.17)
  waiting for transfers between devices: 653 us -> 36.8 us
  blocking collectives: 0 us -> 50.4 us
  starting transfers between devices: 56 us -> 24.7 us
  matrix products: 23.4 us -> 0 us
  between operations: 15.7 us -> 0.73 us
  Pallas kernels: 0 us -> 13.9 us
    reduce_scatter x2 -> x0, waiting for transfers between devices: 411 us -> none  [the longest x1 219 us: on_device(): lax.psum_scatter(lax.dot_general(picked, grad_flat, (((1,), (1,)), ((), (...]
    all_gather x2 -> x0, waiting for transfers between devices: 137 us -> none  [the longest x1 70.3 us: on_device(): lax.all_gather(tokens, 'chan', axis=1, tiled=True)]
    ppermute x50 -> x10, waiting for transfers between devices: 103 us -> 29.5 us  [shifted(): lax.ppermute(value, 'x', [(at, (at + steps) % ring) for at in range(ring)])]
    all_to_all x0 -> x3, blocking collectives: none -> 50.4 us  [exchanged(): return lax.all_to_all(value, axis, 0, 0, tiled=True)]
    ppermute x50 -> x10, starting transfers between devices: 55.8 us -> 16.4 us  [shifted(): lax.ppermute(value, 'x', [(at, (at + steps) % ring) for at in range(ring)])]
    dot_general x28 -> x0, matrix products: 23.4 us -> none  [the longest x8 4.9 us: block_dft(): jnp.einsum('kn,anc->akc', differ, flat_re, precision=PRECISE)]
    pallas_call x0 -> x7, Pallas kernels: none -> 13.9 us  [run(): pl.pallas_call(kernel, out_shape=out_shape, in_specs=specs, out_specs=in_...]
    all_to_all x0 -> x2, starting transfers between devices: none -> 8.33 us  [exchanged(): return lax.all_to_all(value, axis, 0, 0, tiled=True)]
  transfers between devices with their start and end apart: 54 -> 12, of which waited for: 47 -> 7; matrix products, arithmetic and copies ran while one was open for 2% -> 0% of each run, Pallas kernels for 0% -> 2%
where the time goes in v1:
time: 131 us; the launch traced here: 129 us
  blocking collectives  50.4 us (38%)
  waiting for transfers between devices  36.8 us (28%)
  starting transfers between devices  24.7 us (19%)
  Pallas kernels  13.9 us (11%)
  local copies, waits for them, and re-layouts  2.52 us (2%)
    all_to_all x3, blocking collectives, exchanged(): return lax.all_to_all(value, axis, 0, 0, tiled=True)  50.4 us
    ppermute x10, waiting for transfers between devices, shifted(): lax.ppermute(value, 'x', [(at, (at + steps) % ring) for at in range(ring)])  29.5 us
    ppermute x10, starting transfers between devices, shifted(): lax.ppermute(value, 'x', [(at, (at + steps) % ring) for at in range(ring)])  16.4 us
    pallas_call x7, Pallas kernels, run(): pl.pallas_call(kernel, out_shape=out_shape, in_specs=specs, out_specs=in_...  13.9 us
    all_to_all x2, starting transfers between devices, exchanged(): return lax.all_to_all(value, axis, 0, 0, tiled=True)  8.33 us
    all_to_all x2, waiting for transfers between devices, exchanged(): return lax.all_to_all(value, axis, 0, 0, tiled=True)  7.28 us
  transfers between devices with their start and end apart: 12, of which 7 were waited for; matrix products, arithmetic and copies ran while one was open for 0% of the time, Pallas kernels for 2%

profile of v1, /device:TPU:8, one launch (start us, length us, event | category | flops | bytes accessed | tf_op | source)
XLA Modules:
  0.0 129.0 jit_solution(6963250996660809933)
XLA Ops:
  0.6 0.0 copy-start
  0.6 0.8 broadcast_in_dim.7
  1.4 20.1 %all_to_all.25.own = bf16[8,128,128]{2,1,0:T(8,128)(2,1)S(1)} all-to-all(bf16[8,128,128]{2,1,0:T(8,128)(2,1)S(1)} %broadcast_in_dim.7), channel_id=1, replica_groups=mesh['y'=4,'core'=2,'z'=8,'x'=4] {'z'}, dimensions={0} | all-to-all | bytes 524288 | tf_op jit(solution)/shard_map/all_to_all | solution.py:392
  21.6 1.5 %broadcast_in_dim.6 = bf16[8,128,128]{2,1,0:T(8,128)(2,1)} broadcast(bf16[128,128]{1,0:T(8,128)(2,1)} %param.15), dimensions={1,2} | broadcast | bytes 294912 | tf_op jit(solution)/shard_map/broadcast_in_dim | solution.py:396
  23.1 3.4 %all-to-all-start.1 = ((bf16[8,128,128]{2,1,0:T(8,128)(2,1)}), bf16[8,128,128]{2,1,0:T(8,128)(2,1)S(1)}, u32[]{:S(2)}, u32[]{:S(2)}) async-start(bf16[8,128,128]{2,1,0:T(8,128)(2,1)} %broadcast_in_dim.6), calls=%async_computation.1 | async-start | bytes 524288 | tf_op jit(solution)/shard_map/all_to_all | solution.py:392
  26.5 2.8 %collective-permute-start.1 = (bf16[8,128,128]{2,1,0:T(8,128)(2,1)S(1)}, bf16[8,128,128]{2,1,0:T(8,128)(2,1)S(1)}, u32[]{:S(2)}, u32[]{:S(2)}) collective-permute-start(bf16[8,128,128]{2,1,0:T(8,128)(2,1)S(1)} %all_to_all.25.own), channel_id=1, source_target_pairs={{0,3},{1,0},{2,1},{3,2},{4,7},{5,4},{6,5},{7,6},{8,11},{9,8},{10,9... | collective-permute-start | bytes 786440 | tf_op jit(solution)/shard_map/ppermute | solution.py:401
  29.3 0.0 collective-permute-start
  29.3 3.9 %collective-permute-done.1.right = bf16[8,128,128]{2,1,0:T(8,128)(2,1)S(1)} collective-permute-done((bf16[8,128,128]{2,1,0:T(8,128)(2,1)S(1)}, bf16[8,128,128]{2,1,0:T(8,128)(2,1)S(1)}, u32[]{:S(2)}, u32[]{:S(2)}) %collective-permute-start.1) | collective-permute-done | bytes 262176 | tf_op jit(solution)/shard_map/ppermute | solution.py:401
  33.2 3.7 %collective-permute-done.left = bf16[8,128,128]{2,1,0:T(8,128)(2,1)S(1)} collective-permute-done((bf16[8,128,128]{2,1,0:T(8,128)(2,1)S(1)}, bf16[8,128,128]{2,1,0:T(8,128)(2,1)S(1)}, u32[]{:S(2)}, u32[]{:S(2)}) %collective-permute-start) | collective-permute-done | bytes 262176 | tf_op jit(solution)/shard_map/ppermute | solution.py:401
  36.9 0.0 all-to-all-done.1.own
  36.9 2.7 %collective-permute-start.3 = (bf16[8,128,128]{2,1,0:T(8,128)(2,1)S(1)}, bf16[8,128,128]{2,1,0:T(8,128)(2,1)S(1)}, u32[]{:S(2)}, u32[]{:S(2)}) collective-permute-start(bf16[8,128,128]{2,1,0:T(8,128)(2,1)S(1)} %all-to-all-done.1.own), channel_id=1, source_target_pairs={{0,3},{1,0},{2,1},{3,2},{4,7},{5,4},{6,5},{7,6},{8,11},{9,8},{10,9... | collective-permute-start | bytes 786440 | tf_op jit(solution)/shard_map/ppermute | solution.py:401
  39.7 0.0 collective-permute-start.5
  39.7 0.8 collective-permute-start.2
  40.4 3.7 %collective-permute-done.3.right = bf16[8,128,128]{2,1,0:T(8,128)(2,1)S(1)} collective-permute-done((bf16[8,128,128]{2,1,0:T(8,128)(2,1)S(1)}, bf16[8,128,128]{2,1,0:T(8,128)(2,1)S(1)}, u32[]{:S(2)}, u32[]{:S(2)}) %collective-permute-start.3) | collective-permute-done | bytes 262176 | tf_op jit(solution)/shard_map/ppermute | solution.py:401
  44.2 3.3 %collective-permute-start.4 = (bf16[8,128,128]{2,1,0:T(8,128)(2,1)S(1)}, bf16[8,128,128]{2,1,0:T(8,128)(2,1)S(1)}, u32[]{:S(2)}, u32[]{:S(2)}) collective-permute-start(bf16[8,128,128]{2,1,0:T(8,128)(2,1)S(1)} %collective-permute-done.3.right), channel_id=1, source_target_pairs={{0,3},{1,0},{2,1},{3,2},{4,7},{5,4},{6,5},{7,6},{8,11},{9,8},{10,9... | collective-permute-start | bytes 786440 | tf_op jit(solution)/shard_map/ppermute | solution.py:401
  47.5 1.3 collective-permute-done.5.far
  48.7 0.0 copy-start.1
  48.7 3.1 %shard_map.104.given_ref = f32[8,80,128]{2,1,0:T(8,128)S(1)} custom-call(s32[1]{0:T(128)} %bitcast.place_ref, bf16[3,4096,128]{2,1,0:T(8,128)(2,1)} %bitcast.2, f32[2,128,128]{2,1,0:T(8,128)} %filter_ref.1, bf16[8,128,128]{2,1,0:T(8,128)(2,1)S(1)} %all_to_all.25.own, bf16[8,128,128]{2,1,0:T(8,128)(2,1)S(1)} %collective-permute-done.left, ...), custom_call_target="tpu_custom_call" | custom-call | flops 402653184 | bytes 4653060 | tf_op jit(solution)/shard_map/pallas_call | solution.py:376
  51.8 0.0 collective-permute-done.2.left
  51.8 0.0 collective-permute-done.4.far
  51.8 3.2 %shard_map.105 = f32[8,96,128]{2,1,0:T(8,128)} custom-call(s32[1]{0:T(128)} %bitcast.place_ref, bf16[128,4096]{1,0:T(8,128)(2,1)} %out_weight_ref.1, bf16[8,128,128]{2,1,0:T(8,128)(2,1)S(1)} %all-to-all-done.1.own, bf16[8,128,128]{2,1,0:T(8,128)(2,1)S(1)} %collective-permute-done.2.left, bf16[8,128,128]{2,1,0:T(8,128)(2,1)S(1)} %collective-permute-done.3.right, ...), custom_call_target="tpu_custom_call" | custom-call | flops 134217728 | bytes 2818052 | tf_op jit(solution)/shard_map/pallas_call | solution.py:376
  55.0 4.9 %all-to-all-start.2 = ((f32[8,96,128]{2,1,0:T(8,128)}), f32[8,96,128]{2,1,0:T(8,128)S(1)}, u32[]{:S(2)}, u32[]{:S(2)}) async-start(f32[8,96,128]{2,1,0:T(8,128)} %shard_map.105), calls=%async_computation.2 | async-start | bytes 786432 | tf_op jit(solution)/shard_map/all_to_all | solution.py:392
  60.0 0.0 copy-done
  60.0 0.1 constant_dynamic-slice_fusion.1
  60.1 0.0 copy-done.1
  60.1 0.1 constant_dynamic-slice_fusion
  60.1 7.3 %all-to-all-done.2.given_ref = f32[8,96,128]{2,1,0:T(8,128)S(1)} async-done(((f32[8,96,128]{2,1,0:T(8,128)}), f32[8,96,128]{2,1,0:T(8,128)S(1)}, u32[]{:S(2)}, u32[]{:S(2)}) %all-to-all-start.2) | async-done | bytes 393248 | tf_op jit(solution)/shard_map/all_to_all | solution.py:392
  67.4 0.1 broadcast_in_dim.8.coef_ref
  67.5 2.9 %shard_map.106 = bf16[8,64,128]{2,1,0:T(8,128)(2,1)S(1)} custom-call(bf16[2,2,128,128]{3,2,1,0:T(8,128)(2,1)} %constant.26.clone.table_hbm, f32[2,9,128]{2,1,0:T(8,128)} %constant.27.clone.twiddle_hbm, f32[8,96,128]{2,1,0:T(8,128)S(1)} %all-to-all-done.2.given_ref, f32[11,16,128]{2,1,0:T(8,128)S(1)} %broadcast_in_dim.8.coef_ref), custom_call_target="tpu_custom_call" | custom-call | bytes 754688 | tf_op jit(solution)/shard_map/pallas_call | solution.py:376
  70.4 8.5 %all_to_all.26.channels_ref = bf16[8,64,128]{2,1,0:T(8,128)(2,1)S(1)} all-to-all(bf16[8,64,128]{2,1,0:T(8,128)(2,1)S(1)} %shard_map.106), channel_id=1, replica_groups=mesh['y'=4,'core'=2,'z'=8,'x'=4] {'y','core'}, dimensions={0} | all-to-all | bytes 262144 | tf_op jit(solution)/shard_map/all_to_all | solution.py:392
  78.9 3.7 %shard_map.107 = (bf16[8,2,128,128]{3,2,1,0:T(8,128)(2,1)S(1)}, bf16[8,2,128,128]{3,2,1,0:T(8,128)(2,1)S(1)}, bf16[8,2,128,128]{3,2,1,0:T(8,128)(2,1)S(1)}, bf16...) custom-call(s32[1]{0:T(128)} %bitcast.place_ref, bf16[128,4096]{1,0:T(8,128)(2,1)} %out_weight_ref.1, ...), custom_call_target="tpu_custom_call" | custom-call | flops 536870912 | bytes 6422532 | tf_op jit(solution)/shard_map/pallas_call | solution.py:376
  82.6 0.8 collective-permute-start.6
  83.4 2.6 %collective-permute-start.7 = (bf16[8,2,128,128]{3,2,1,0:T(8,128)(2,1)S(1)}, bf16[8,2,128,128]{3,2,1,0:T(8,128)(2,1)S(1)}, u32[]{:S(2)}, u32[]{:S(2)}) collective-permute-start(bf16[8,2,128,128]{3,2,1,0:T(8,128)(2,1)S(1)} %get-tuple-element.15), channel_id=1, source_target_pairs={{0,3},{1,0},{2,1},{3,2},{4,7},{5,4},{6,5},{7,6},{8,11},{9,8},{10,9... | collective-permute-start | bytes 1572872 | tf_op jit(solution)/shard_map/ppermute | solution.py:401
  86.0 11.6 %collective-permute-done.6.from_l_ref = bf16[8,2,128,128]{3,2,1,0:T(8,128)(2,1)S(1)} collective-permute-done((bf16[8,2,128,128]{3,2,1,0:T(8,128)(2,1)S(1)}, bf16[8,2,128,128]{3,2,1,0:T(8,128)(2,1)S(1)}, u32[]{:S(2)}, u32[]{:S(2)}) %collective-permute-start.6) | collective-permute-done | bytes 524320 | tf_op jit(solution)/shard_map/ppermute | solution.py:401
  97.6 0.0 collective-permute-done.7.from_r_ref
  97.6 0.1 shard_map.108
  97.7 1.2 collective-permute-start.8
  98.9 2.1 %collective-permute-start.9 = (bf16[4,2,128,128]{3,2,1,0:T(8,128)(2,1)S(1)}, bf16[4,2,128,128]{3,2,1,0:T(8,128)(2,1)S(1)}, u32[]{:S(2)}, u32[]{:S(2)}) collective-permute-start(bf16[4,2,128,128]{3,2,1,0:T(8,128)(2,1)S(1)} %get-tuple-element.19), channel_id=1, source_target_pairs={{0,3},{1,0},{2,1},{3,2},{4,7},{5,4},{6,5},{7,6},{8,11},{9,8},{10,9... | collective-permute-start | bytes 786440 | tf_op jit(solution)/shard_map/ppermute | solution.py:401
  101.1 5.3 %collective-permute-done.8.last_l_ref = bf16[4,2,128,128]{3,2,1,0:T(8,128)(2,1)S(1)} collective-permute-done((bf16[4,2,128,128]{3,2,1,0:T(8,128)(2,1)S(1)}, bf16[4,2,128,128]{3,2,1,0:T(8,128)(2,1)S(1)}, u32[]{:S(2)}, u32[]{:S(2)}) %collective-permute-start.8) | collective-permute-done | bytes 262176 | tf_op jit(solution)/shard_map/ppermute | solution.py:401
  106.3 0.0 collective-permute-done.9.last_r_ref
  106.3 0.2 shard_map.109
  106.5 21.8 %all_to_all.27.parts_ref = bf16[8,2,128,128]{3,2,1,0:T(8,128)(2,1)S(1)} all-to-all(bf16[8,2,128,128]{3,2,1,0:T(8,128)(2,1)S(1)} %shard_map.109), channel_id=1, replica_groups=mesh['y'=4,'core'=2,'z'=8,'x'=4] {'z'}, dimensions={0} | all-to-all | bytes 1048576 | tf_op jit(solution)/shard_map/all_to_all | solution.py:392
  128.3 0.7 shard_map.110
  (2 shorter events, 0.0 us)
Async XLA Ops:
  0.6 59.3 %copy-start = (f32[3,3,128]{2,1,0:T(4,128)S(1)}, f32[3,3,128]{2,1,0:T(4,128)}, u32[]{:S(2)}) copy-start(f32[3,3,128]{2,1,0:T(4,128)} %param.11) | copy-start | bytes 13828
  23.1 13.8 %all-to-all-start.1 = ((bf16[8,128,128]{2,1,0:T(8,128)(2,1)}), bf16[8,128,128]{2,1,0:T(8,128)(2,1)S(1)}, u32[]{:S(2)}, u32[]{:S(2)}) async-start(bf16[8,128,128]{2,1,0:T(8,128)(2,1)} %broadcast_in_dim.6), calls=%async_computation.1 | async-start | bytes 524288 | tf_op jit(solution)/shard_map/all_to_all | solution.py:392
  26.5 6.7 %collective-permute-start.1 = (bf16[8,128,128]{2,1,0:T(8,128)(2,1)S(1)}, bf16[8,128,128]{2,1,0:T(8,128)(2,1)S(1)}, u32[]{:S(2)}, u32[]{:S(2)}) collective-permute-start(bf16[8,128,128]{2,1,0:T(8,128)(2,1)S(1)} %all_to_all.25.own), channel_id=1, source_target_pairs={{0,3},{1,0},{2,1},{3,2},{4,7},{5,4},{6,5},{7,6},{8,11},{9,8},{10,9... | collective-permute-start | bytes 786440 | tf_op jit(solution)/shard_map/ppermute | solution.py:401
  29.3 7.6 %collective-permute-start = (bf16[8,128,128]{2,1,0:T(8,128)(2,1)S(1)}, bf16[8,128,128]{2,1,0:T(8,128)(2,1)S(1)}, u32[]{:S(2)}, u32[]{:S(2)}) collective-permute-start(bf16[8,128,128]{2,1,0:T(8,128)(2,1)S(1)} %all_to_all.25.own), channel_id=1, source_target_pairs={{0,1},{1,2},{2,3},{3,0},{4,5},{5,6},{6,7},{7,4},{8,9},{9,10},{10,1... | collective-permute-start | bytes 786440 | tf_op jit(solution)/shard_map/ppermute | solution.py:401
  36.9 7.2 %collective-permute-start.3 = (bf16[8,128,128]{2,1,0:T(8,128)(2,1)S(1)}, bf16[8,128,128]{2,1,0:T(8,128)(2,1)S(1)}, u32[]{:S(2)}, u32[]{:S(2)}) collective-permute-start(bf16[8,128,128]{2,1,0:T(8,128)(2,1)S(1)} %all-to-all-done.1.own), channel_id=1, source_target_pairs={{0,3},{1,0},{2,1},{3,2},{4,7},{5,4},{6,5},{7,6},{8,11},{9,8},{10,9... | collective-permute-start | bytes 786440 | tf_op jit(solution)/shard_map/ppermute | solution.py:401
  39.7 9.1 %collective-permute-start.5 = (bf16[8,128,128]{2,1,0:T(8,128)(2,1)S(1)}, bf16[8,128,128]{2,1,0:T(8,128)(2,1)S(1)}, u32[]{:S(2)}, u32[]{:S(2)}) collective-permute-start(bf16[8,128,128]{2,1,0:T(8,128)(2,1)S(1)} %collective-permute-done.left), channel_id=1, source_target_pairs={{0,1},{1,2},{2,3},{3,0},{4,5},{5,6},{6,7},{7,4},{8,9},{9,10},{10,1... | collective-permute-start | bytes 786440 | tf_op jit(solution)/shard_map/ppermute | solution.py:401
  39.7 12.1 %collective-permute-start.2 = (bf16[8,128,128]{2,1,0:T(8,128)(2,1)S(1)}, bf16[8,128,128]{2,1,0:T(8,128)(2,1)S(1)}, u32[]{:S(2)}, u32[]{:S(2)}) collective-permute-start(bf16[8,128,128]{2,1,0:T(8,128)(2,1)S(1)} %all-to-all-done.1.own), channel_id=1, source_target_pairs={{0,1},{1,2},{2,3},{3,0},{4,5},{5,6},{6,7},{7,4},{8,9},{9,10},{10,1... | collective-permute-start | bytes 786440 | tf_op jit(solution)/shard_map/ppermute | solution.py:401
  44.2 7.7 %collective-permute-start.4 = (bf16[8,128,128]{2,1,0:T(8,128)(2,1)S(1)}, bf16[8,128,128]{2,1,0:T(8,128)(2,1)S(1)}, u32[]{:S(2)}, u32[]{:S(2)}) collective-permute-start(bf16[8,128,128]{2,1,0:T(8,128)(2,1)S(1)} %collective-permute-done.3.right), channel_id=1, source_target_pairs={{0,3},{1,0},{2,1},{3,2},{4,7},{5,4},{6,5},{7,6},{8,11},{9,8},{10,9... | collective-permute-start | bytes 786440 | tf_op jit(solution)/shard_map/ppermute | solution.py:401
  48.7 11.3 %copy-start.1 = (f32[2,128]{1,0:T(2,128)S(1)}, f32[2,128]{1,0:T(2,128)}, u32[]{:S(2)}) copy-start(f32[2,128]{1,0:T(2,128)} %param.13) | copy-start | bytes 3076
  55.0 12.4 %all-to-all-start.2 = ((f32[8,96,128]{2,1,0:T(8,128)}), f32[8,96,128]{2,1,0:T(8,128)S(1)}, u32[]{:S(2)}, u32[]{:S(2)}) async-start(f32[8,96,128]{2,1,0:T(8,128)} %shard_map.105), calls=%async_computation.2 | async-start | bytes 786432 | tf_op jit(solution)/shard_map/all_to_all | solution.py:392
  82.6 15.0 %collective-permute-start.6 = (bf16[8,2,128,128]{3,2,1,0:T(8,128)(2,1)S(1)}, bf16[8,2,128,128]{3,2,1,0:T(8,128)(2,1)S(1)}, u32[]{:S(2)}, u32[]{:S(2)}) collective-permute-start(bf16[8,2,128,128]{3,2,1,0:T(8,128)(2,1)S(1)} %get-tuple-element.14), channel_id=1, source_target_pairs={{0,1},{1,2},{2,3},{3,0},{4,5},{5,6},{6,7},{7,4},{8,9},{9,10},{10,1... | collective-permute-start | bytes 1572872 | tf_op jit(solution)/shard_map/ppermute | solution.py:401
  83.4 14.2 %collective-permute-start.7 = (bf16[8,2,128,128]{3,2,1,0:T(8,128)(2,1)S(1)}, bf16[8,2,128,128]{3,2,1,0:T(8,128)(2,1)S(1)}, u32[]{:S(2)}, u32[]{:S(2)}) collective-permute-start(bf16[8,2,128,128]{3,2,1,0:T(8,128)(2,1)S(1)} %get-tuple-element.15), channel_id=1, source_target_pairs={{0,3},{1,0},{2,1},{3,2},{4,7},{5,4},{6,5},{7,6},{8,11},{9,8},{10,9... | collective-permute-start | bytes 1572872 | tf_op jit(solution)/shard_map/ppermute | solution.py:401
  97.7 8.6 %collective-permute-start.8 = (bf16[4,2,128,128]{3,2,1,0:T(8,128)(2,1)S(1)}, bf16[4,2,128,128]{3,2,1,0:T(8,128)(2,1)S(1)}, u32[]{:S(2)}, u32[]{:S(2)}) collective-permute-start(bf16[4,2,128,128]{3,2,1,0:T(8,128)(2,1)S(1)} %get-tuple-element.18), channel_id=1, source_target_pairs={{0,1},{1,2},{2,3},{3,0},{4,5},{5,6},{6,7},{7,4},{8,9},{9,10},{10,1... | collective-permute-start | bytes 786440 | tf_op jit(solution)/shard_map/ppermute | solution.py:401
  98.9 7.4 %collective-permute-start.9 = (bf16[4,2,128,128]{3,2,1,0:T(8,128)(2,1)S(1)}, bf16[4,2,128,128]{3,2,1,0:T(8,128)(2,1)S(1)}, u32[]{:S(2)}, u32[]{:S(2)}) collective-permute-start(bf16[4,2,128,128]{3,2,1,0:T(8,128)(2,1)S(1)} %get-tuple-element.19), channel_id=1, source_target_pairs={{0,3},{1,0},{2,1},{3,2},{4,7},{5,4},{6,5},{7,6},{8,11},{9,8},{10,9... | collective-permute-start | bytes 786440 | tf_op jit(solution)/shard_map/ppermute | solution.py:401

commit v2 on v1

--- a/solution.py
+++ b/solution.py
@@ -143,16 +143,48 @@
 
 
 def operator_kernel(
-    table_hbm, twiddle_hbm, given_ref, coef_ref, out_ref, table_ref, twiddle_ref, sems
+    place_ref,
+    table_hbm,
+    twiddle_hbm,
+    taps_hbm,
+    gains_hbm,
+    given_ref,
+    filter_ref,
+    out_ref,
+    table_ref,
+    twiddle_ref,
+    taps_ref,
+    gains_ref,
+    rows_ref,
+    turned_ref,
+    coef_ref,
+    sems,
 ):
-    count = given_ref.shape[1] // 6
+    count = given_ref.shape[1] // 4
     tables_in = [
         *started([table_hbm], [table_ref], sems.at[0]),
         *started([twiddle_hbm], [twiddle_ref], sems.at[1]),
     ]
-
-    def rows_of(slot):
-        return [given_ref[block, slot * count : (slot + 1) * count] for block in range(BLOCKS)]
+    coef_in = [
+        *started([taps_hbm], [taps_ref], sems.at[2]),
+        *started([gains_hbm], [gains_ref], sems.at[3]),
+    ]
+    for copy in coef_in:
+        copy.wait()
+    rows_ref[...] = jnp.zeros_like(rows_ref)
+    for tap in range(3):
+        for which in range(3):
+            rows_ref[3 * tap + which] = taps_ref[tap, which]
+    for order in range(2):
+        rows_ref[9 + order] = gains_ref[order]
+    turned_ref[...] = rows_ref[...].T
+    own_start = pl.multiple_of(place_ref[0] * count, count)
+    columns = turned_ref[pl.ds(own_start, count), :]
+    for at in range(coef_ref.shape[0]):
+        coef_ref[at] = jnp.broadcast_to(columns[:, at : at + 1], coef_ref.shape[1:])
+
+    def rows_of(slot, ref=given_ref):
+        return [ref[block, slot * count : (slot + 1) * count] for block in range(BLOCKS)]
 
     def store(slot, blocks):
         for block, value in enumerate(blocks):
@@ -180,13 +212,13 @@
         copy.wait()
     matrices = fine_matrices(table_ref)
     filter_spec = [
-        spectrum(rows_of(3 + order), matrices, twiddle_ref) * (1.0 / (COARSE * LANES))
+        spectrum(rows_of(order, filter_ref), matrices, twiddle_ref) * (1.0 / (COARSE * LANES))
         for order in range(2)
     ]
     conv_one = filtered(values, 0, False)
     conv_two = filtered(product(gate_one, conv_one), 1, False)
     store(0, product(gate_two, conv_two))
-    grad_two = rows_of(5)
+    grad_two = rows_of(3)
     store(3, short_sum(product(grad_two, conv_two), coef_ref, 2, leading))
     grad_first = filtered(product(grad_two, gate_two), 1, True)
     store(2, short_sum(product(grad_first, conv_one), coef_ref, 1, leading))
@@ -203,35 +235,73 @@
     return found
 
 
-def weight_start(place_ref, z, apart, ring, feats):
-    block = z * ring + lax.rem(place_ref[0] + apart, ring)
-    return pl.multiple_of(block * feats, feats)
-
-
-def chunks(ref, parts, axis):
-    size = ref.shape[axis] // parts
-    lead = (slice(None),) * axis
-    return [ref.at[(*lead, pl.ds(part * size, size))] for part in range(parts)]
-
-
-def project_kernel(
-    ring,
-    place_ref,
-    weight_ref,
-    filter_ref,
-    own,
-    left,
-    right,
-    far,
-    out_ref,
-    held,
-    held_filter,
-    sems,
-):
-    n_z, tokens, feats = own.shape
-    (filter_copy,) = started([filter_ref], [held_filter], sems.at[1])
-    copies_in = started(chunks(weight_ref, n_z, 1), chunks(held, n_z, 1), sems.at[0])
-    chans = weight_ref.shape[2]
+def copies_kernel(tokens_hbm, cotangent_hbm, out_ref, held, sems):
+    begun = started([tokens_hbm, cotangent_hbm], [held.at[0], held.at[1]], sems)
+    for copy in begun:
+        copy.wait()
+    for at in range(out_ref.shape[0]):
+        out_ref[at] = held[...]
+
+
+def apart_kernel(both_ref, rows_ref, grads_ref):
+    rows_ref[...] = both_ref[:, 0]
+    grads_ref[...] = both_ref[:, 1]
+
+
+def turned_filters_kernel(filter_ref, out_ref):
+    count = out_ref.shape[1] // 2
+    for order in range(2):
+        turned = filter_ref[order].T
+        for block in range(BLOCKS):
+            out_ref[block, order * count : (order + 1) * count] = turned[
+                block * count : (block + 1) * count
+            ]
+
+
+def out_weight_copies(place_ref, out_hbm, out_ref, sems):
+    ring, n_z = sems.shape
+    feats = out_ref.shape[1] // (ring * n_z)
+    begun = []
+    for z in range(n_z):
+        for apart in range(ring):
+            source = lax.rem(place_ref[0] + apart, ring)
+            start = pl.multiple_of((z * ring + source) * feats, feats)
+            copy = pltpu.make_async_copy(
+                out_hbm.at[:, pl.ds(start, feats)],
+                out_ref.at[:, pl.ds((z * ring + apart) * feats, feats)],
+                sems.at[apart, z],
+            )
+            copy.start()
+            begun.append(copy)
+    return begun
+
+
+def weights_kernel(place_ref, in_hbm, out_hbm, in_ref, out_ref, in_sems, out_sems):
+    parts, _, ring, _, chans = in_hbm.shape
+    begun = []
+    for apart in range(ring):
+        source = lax.rem(place_ref[0] + apart, ring)
+        for part in range(parts):
+            copy = pltpu.make_async_copy(
+                in_hbm.at[part, :, source],
+                in_ref.at[:, apart, :, pl.ds(part * chans, chans)],
+                in_sems.at[apart, part],
+            )
+            copy.start()
+            begun.append(copy)
+    begun += out_weight_copies(place_ref, out_hbm, out_ref, out_sems)
+    for copy in begun:
+        copy.wait()
+
+
+def side_by_side(own, right, far, left, z):
+    return jnp.concatenate([own[z], right[z], far, left[z]], axis=1)
+
+
+def project_kernel(weight_ref, own, left, right, far, out_ref):
+    n_z, tokens, _ = own.shape
+    columns = weight_ref.shape[3]
+    chans = columns // 3
     count = chans // BLOCKS
 
     def store(slot, turned):
@@ -240,47 +310,36 @@
                 block * count : (block + 1) * count
             ]
 
-    filter_copy.wait()
-    for order in range(2):
-        store(3 + order, held_filter[order].T)
-    total = [jnp.zeros((tokens, chans), F32)] * 3
+    total = jnp.zeros((tokens, columns), F32)
     for z in range(n_z):
-        copies_in[z].wait()
-        for rows_ref, apart in ((own, 0), (right, 1), (far, 2), (left, 3)):
-            start = weight_start(place_ref, z, apart, ring, feats)
-            for which in range(3):
-                total[which] = total[which] + jnp.dot(
-                    rows_ref[z], held[which, pl.ds(start, feats), :], preferred_element_type=F32
-                )
+        total = total + jnp.dot(
+            side_by_side(own, right, far[z], left, z),
+            weight_ref[z].reshape((-1, columns)),
+            preferred_element_type=F32,
+        )
     for which in range(3):
-        store(which, total[which].T)
-
-
-def project_grad_kernel(
-    ring, place_ref, weight_ref, own, left, right, far, given_ref, out_ref, held, sems
-):
-    n_z, tokens, feats = own.shape
-    copies_in = started(chunks(weight_ref, n_z, 1), chunks(held, n_z, 1), sems)
+        store(which, total[:, which * chans : (which + 1) * chans].T)
+
+
+def project_grad_kernel(weight_ref, own, left, right, far, given_ref, out_ref):
+    n_z, tokens, _ = own.shape
+    wide = weight_ref.shape[1] // n_z
     total = jnp.zeros((weight_ref.shape[0], tokens), F32)
     for z in range(n_z):
-        copies_in[z].wait()
-        for rows_ref, apart in ((own, 0), (right, 1), (far, 2), (left, 3)):
-            start = weight_start(place_ref, z, apart, ring, feats)
-            total = total + lax.dot_general(
-                held[:, pl.ds(start, feats)],
-                rows_ref[z],
-                (((1,), (1,)), ((), ())),
-                preferred_element_type=F32,
-            )
-    count = out_ref.shape[1] // 6
-    out_ref[:, : 5 * count] = given_ref[...]
-    out_ref[:, 5 * count :] = total.reshape((BLOCKS, count, tokens))
+        total = total + lax.dot_general(
+            weight_ref[:, z * wide : (z + 1) * wide],
+            side_by_side(own, right, far[z], left, z),
+            (((1,), (1,)), ((), ())),
+            preferred_element_type=F32,
+        )
+    count = out_ref.shape[1] // 4
+    out_ref[:, : 3 * count] = given_ref[...]
+    out_ref[:, 3 * count :] = total.reshape((BLOCKS, count, tokens))
 
 
 def partial_kernel(
-    ring,
     place_ref,
-    out_weight_ref,
+    out_hbm,
     in_weight_ref,
     channels_ref,
     own_ref,
@@ -288,46 +347,49 @@
     left_ref,
     keep_r_ref,
     keep_l_ref,
-    held_out,
-    held_in,
-    sems,
+    out_weight_ref,
+    out_sems,
 ):
     n_z, _, feats, tokens = own_ref.shape
     half = n_z // 2
-    out_copies = started(chunks(out_weight_ref, n_z, 1), chunks(held_out, n_z, 1), sems.at[0])
-    in_copies = started(chunks(in_weight_ref, n_z, 1), chunks(held_in, n_z, 1), sems.at[1])
+    ring = out_sems.shape[0]
+    weight_copies = out_weight_copies(place_ref, out_hbm, out_weight_ref, out_sems)
     count = channels_ref.shape[1] // 4
     second, *grads = [
         channels_ref[:, slot * count : (slot + 1) * count].reshape((BLOCKS * count, tokens))
         for slot in range(4)
     ]
     second = second.astype(F32).T.astype(BF16)
-    dot = functools.partial(jnp.dot, preferred_element_type=F32)
-
-    def mixed(z, apart):
-        start = weight_start(place_ref, z, apart, ring, feats)
-        return dot(second, held_out[:, pl.ds(start, feats)])
-
-    def token_grad(z, apart):
-        start = weight_start(place_ref, z, apart, ring, feats)
-        total = dot(held_in[0, pl.ds(start, feats), :], grads[0])
-        for which in (1, 2):
-            total = total + dot(held_in[which, pl.ds(start, feats), :], grads[which])
-        return total
-
-    for copy in out_copies + in_copies:
-        copy.wait()
-    for output, product in ((0, mixed), (1, token_grad)):
+    grads = jnp.concatenate(grads, axis=0)
+    wide = out_weight_ref.shape[1] // n_z
+    columns = in_weight_ref.shape[3]
+
+    def mixed(z):
+        for copy in weight_copies[z * ring : (z + 1) * ring]:
+            copy.wait()
+        product = jnp.dot(
+            second, out_weight_ref[:, z * wide : (z + 1) * wide], preferred_element_type=F32
+        )
+        return [product[:, at : at + feats].astype(BF16) for at in range(0, wide, feats)]
+
+    def token_grad(z):
+        product = jnp.dot(
+            in_weight_ref[z].reshape((-1, columns)), grads, preferred_element_type=F32
+        )
+        return [product[at : at + feats].astype(BF16) for at in range(0, wide, feats)]
+
+    for output, pieces in ((1, token_grad), (0, mixed)):
         for z in range(n_z):
-            own_ref[z, output] = product(z, 0).astype(BF16)
+            own, ahead, far, behind = pieces(z)
+            own_ref[z, output] = own
             if z < half:
-                right_ref[z, output] = product(z, 2).astype(BF16)
-                keep_r_ref[z, output] = product(z, 1).astype(BF16)
-                left_ref[z, output] = product(z, 3).astype(BF16)
+                right_ref[z, output] = far
+                keep_r_ref[z, output] = ahead
+                left_ref[z, output] = behind
             else:
-                right_ref[z, output] = product(z, 1).astype(BF16)
-                left_ref[z, output] = product(z, 2).astype(BF16)
-                keep_l_ref[z - half, output] = product(z, 3).astype(BF16)
+                right_ref[z, output] = ahead
+                left_ref[z, output] = far
+                keep_l_ref[z - half, output] = behind
 
 
 def merge_kernel(keep_r_ref, keep_l_ref, from_l_ref, from_r_ref, right_ref, left_ref):
@@ -358,20 +420,18 @@
     token_grad_ref[...] = totals[1].T.astype(BF16)
 
 
-def run(kernel, out_shape, *args, flops=0, place=None, weights=()):
+def run(kernel, out_shape, *args, flops=0, place=None, far=(), scratch=()):
     single = not isinstance(out_shape, (list, tuple))
     outs = (out_shape,) if single else out_shape
     in_vmem = pl.BlockSpec(memory_space=pltpu.VMEM)
-    specs, scratch = [in_vmem] * len(args), []
-    if weights:
-        held = (pltpu.with_memory_space_constraint(weight, pltpu.HBM) for weight in weights)
-        places = () if place is None else (place,)
-        args = (*places, *held, *args)
-        in_hbm = [pl.BlockSpec(memory_space=pltpu.HBM)] * len(weights)
-        specs = [pl.BlockSpec(memory_space=pltpu.SMEM)] * len(places) + in_hbm + specs
-        scratch = [pltpu.VMEM(weight.shape, weight.dtype) for weight in weights]
-        shape = (BLOCKS,) if len(weights) == 1 else (len(weights), BLOCKS)
-        scratch.append(pltpu.SemaphoreType.DMA(shape))
+    places = () if place is None else (place,)
+    specs = [
+        *[pl.BlockSpec(memory_space=pltpu.SMEM)] * len(places),
+        *[pl.BlockSpec(memory_space=pltpu.HBM)] * len(far),
+        *[in_vmem] * len(args),
+    ]
+    held = (pltpu.with_memory_space_constraint(array, pltpu.HBM) for array in far)
+    args = (*places, *held, *args)
     moved = sum(int(np.prod(a.shape)) * a.dtype.itemsize for a in (*args, *outs))
     return pl.pallas_call(
         kernel,
@@ -392,10 +452,6 @@
     return lax.all_to_all(value, axis, 0, 0, tiled=True)
 
 
-def copies(value, count):
-    return jnp.broadcast_to(value[None], (count, *value.shape))
-
-
 def shifted(value, steps):
     ring = lax.axis_size("x")
     return lax.ppermute(value, "x", [(at, (at + steps) % ring) for at in range(ring)])
@@ -403,11 +459,6 @@
 
 def after(value, *others):
     return lax.optimization_barrier((value, *others))[0]
-
-
-def gathered(own, steps):
-    left, right = shifted(own, 1), shifted(own, -1)
-    return left, right, shifted(left if steps > 0 else right, steps)
 
 
 def on_device(tokens, in_weight, short_kernel, filters, skip_gain, out_weight, cotangent):
@@ -416,56 +467,89 @@
     n_z, ring = lax.axis_size("z"), lax.axis_size("x")
     half = n_z // 2
     count = chans // BLOCKS
-    seq_index = lax.axis_index(SEQ)
+    seq_place = lax.axis_index(SEQ).reshape((1,)).astype(jnp.int32)
     place = lax.axis_index("x").reshape((1,)).astype(jnp.int32)
     table = jnp.asarray(fine_table())
     twiddles = jnp.asarray(twiddle_table())
-    split_in = in_weight.transpose((1, 0, 2))
-
-    taps = lax.dynamic_slice_in_dim(short_kernel, seq_index * count, count, 2)
-    gains = lax.dynamic_slice_in_dim(skip_gain, seq_index * count, count, 1)
-    coef = jnp.concatenate([taps.reshape((9, count)), gains], axis=0)
-    coef = jnp.broadcast_to(coef[:, :, None], (11, count, LANES))
-
-    own_rows = exchanged(copies(tokens, n_z), "z")
-    own_grads = exchanged(after(copies(cotangent, n_z), own_rows), "z")
-    other_rows = gathered(own_rows, 1)
-    other_grads = gathered(after(own_grads, *other_rows[:2]), -1)
-
+    split_in = in_weight.transpose((1, 0, 2)).reshape((3, n_z, ring, LANES, chans))
+
+    sent = run(
+        copies_kernel,
+        shape_of((n_z, 2, rows, LANES), BF16),
+        far=(tokens, cotangent),
+        scratch=[pltpu.VMEM((2, rows, LANES), BF16), pltpu.SemaphoreType.DMA((2,))],
+    )
+    both = exchanged(sent, "z")
+    one = shape_of((n_z, rows, LANES), BF16)
+    own_rows, own_grads = run(apart_kernel, (one, one), both)
+    left_rows = shifted(own_rows, 1)
+    right_rows = shifted(own_rows, -1)
+    left_grads = shifted(own_grads, 1)
+    right_grads = shifted(own_grads, -1)
+    far_rows = shifted(left_rows, 1)
+    far_grads = shifted(right_grads, -1)
+
+    turned_filters = run(
+        turned_filters_kernel, shape_of((BLOCKS, 2 * count, rows), F32), after(filters, own_rows)
+    )
+    turned_filters = exchanged(turned_filters, SEQ)
+    weight_sems = pltpu.SemaphoreType.DMA((ring, n_z))
+    in_turned, out_turned = run(
+        weights_kernel,
+        (shape_of((n_z, ring, LANES, 3 * chans), BF16), shape_of(out_weight.shape, BF16)),
+        far=(after(split_in, own_rows), out_weight),
+        place=place,
+        scratch=[pltpu.SemaphoreType.DMA((ring, 3)), weight_sems],
+    )
     given = run(
-        functools.partial(project_kernel, ring),
-        shape_of((BLOCKS, 5 * count, rows), F32),
+        project_kernel,
+        shape_of((BLOCKS, 3 * count, rows), F32),
+        in_turned,
         own_rows,
-        *other_rows,
+        left_rows,
+        right_rows,
+        far_rows,
         flops=2 * rows * width * 3 * chans,
-        place=place,
-        weights=(split_in, filters),
     )
     given = run(
-        functools.partial(project_grad_kernel, ring),
-        shape_of((BLOCKS, 6 * count, rows), F32),
+        project_grad_kernel,
+        shape_of((BLOCKS, 4 * count, rows), F32),
+        out_turned,
         own_grads,
-        *other_grads,
+        left_grads,
+        right_grads,
+        far_grads,
         given,
         flops=2 * rows * width * chans,
-        place=place,
-        weights=(out_weight,),
     )
     channels = run(
         operator_kernel,
         shape_of((BLOCKS, 4 * count, LANES), BF16),
         exchanged(given, SEQ),
-        coef,
-        weights=(table, twiddles),
+        turned_filters,
+        place=seq_place,
+        far=(table, twiddles, short_kernel, skip_gain),
+        scratch=[
+            pltpu.VMEM(table.shape, BF16),
+            pltpu.VMEM(twiddles.shape, F32),
+            pltpu.VMEM(short_kernel.shape, F32),
+            pltpu.VMEM(skip_gain.shape, F32),
+            pltpu.VMEM((16, chans), F32),
+            pltpu.VMEM((chans, 16), F32),
+            pltpu.VMEM((11, count, LANES), F32),
+            pltpu.SemaphoreType.DMA((4, 1)),
+        ],
     )
     whole, part = (n_z, 2, LANES, rows), (half, 2, LANES, rows)
     own, to_right, to_left, keep_r, keep_l = run(
-        functools.partial(partial_kernel, ring),
+        partial_kernel,
         tuple(shape_of(shape, BF16) for shape in (whole, whole, whole, part, part)),
+        in_turned,
         exchanged(channels, SEQ),
         flops=2 * rows * width * 4 * chans,
         place=place,
-        weights=(out_weight, split_in),
+        far=(out_weight,),
+        scratch=[pltpu.VMEM(out_weight.shape, BF16), weight_sems],
     )
     from_l, from_r = shifted(to_right, 1), shifted(to_left, -1)
     to_right, to_left = run(

time: 131 us -> 125 us (0.954)
  waiting for transfers between devices: 36.8 us -> 26.7 us
  Pallas kernels: 13.9 us -> 16.4 us
  blocking collectives: 50.4 us -> 52.5 us
  local copies, waits for them, and re-layouts: 2.52 us -> 0.9 us
    ppermute x10, waiting for transfers between devices: 29.5 us -> 20.6 us  [shifted(): lax.ppermute(value, 'x', [(at, (at + steps) % ring) for at in range(ring)])]
    pallas_call x7 -> x11, Pallas kernels: 13.9 us -> 16.4 us  [run(): pl.pallas_call(kernel, out_shape=out_shape, in_specs=specs, out_specs=in_...]
    broadcast_in_dim x3 -> x0, local copies, waits for them, and re-layouts: 2.36 us -> none  [the longest x2 2.28 us: copies(): return jnp.broadcast_to(value[None], (count, *value.shape))]
    all_to_all x3, blocking collectives: 50.4 us -> 52.5 us  [exchanged(): return lax.all_to_all(value, axis, 0, 0, tiled=True)]
    all_to_all x2, starting transfers between devices: 8.33 us -> 9.72 us  [exchanged(): return lax.all_to_all(value, axis, 0, 0, tiled=True)]
  transfers between devices with their start and end apart: 12 -> 12, of which waited for: 7 -> 5; matrix products, arithmetic and copies ran while one was open for 0% -> 0% of each run, Pallas kernels for 2% -> 6%
where the time goes in v2:
time: 125 us; the launch traced here: 123 us
  blocking collectives  52.5 us (42%)
  waiting for transfers between devices  26.7 us (21%)
  starting transfers between devices  25.8 us (21%)
  Pallas kernels  16.4 us (13%)
    all_to_all x3, blocking collectives, exchanged(): return lax.all_to_all(value, axis, 0, 0, tiled=True)  52.5 us
    ppermute x10, waiting for transfers between devices, shifted(): lax.ppermute(value, 'x', [(at, (at + steps) % ring) for at in range(ring)])  20.6 us
    pallas_call x11, Pallas kernels, run(): pl.pallas_call(kernel, out_shape=out_shape, in_specs=specs, out_specs=in_...  16.4 us
    ppermute x10, starting transfers between devices, shifted(): lax.ppermute(value, 'x', [(at, (at + steps) % ring) for at in range(ring)])  16.1 us
    all_to_all x2, starting transfers between devices, exchanged(): return lax.all_to_all(value, axis, 0, 0, tiled=True)  9.72 us
    all_to_all x2, waiting for transfers between devices, exchanged(): return lax.all_to_all(value, axis, 0, 0, tiled=True)  6.05 us
  transfers between devices with their start and end apart: 12, of which 5 were waited for; matrix products, arithmetic and copies ran while one was open for 0% of the time, Pallas kernels for 6%

profile of v2, /device:TPU:8, one launch (start us, length us, event | category | flops | bytes accessed | tf_op | source)
XLA Modules:
  0.0 123.1 jit_solution(6971469841402366198)
XLA Ops:
  0.6 0.9 shard_map.104
  1.5 25.8 %all_to_all.25.both_ref = bf16[8,2,128,128]{3,2,1,0:T(8,128)(2,1)S(1)} all-to-all(bf16[8,2,128,128]{3,2,1,0:T(8,128)(2,1)S(1)} %shard_map.104), channel_id=1, replica_groups=mesh['y'=4,'core'=2,'z'=8,'x'=4] {'z'}, dimensions={0} | all-to-all | bytes 1048576 | tf_op jit(solution)/shard_map/all_to_all | solution.py:452
  27.3 0.7 shard_map.105
  28.0 1.5 %collective-permute-start.3 = (bf16[8,128,128]{2,1,0:T(8,128)(2,1)}, bf16[8,128,128]{2,1,0:T(8,128)(2,1)}, u32[]{:S(2)}, u32[]{:S(2)}) collective-permute-start(bf16[8,128,128]{2,1,0:T(8,128)(2,1)} %get-tuple-element.15.own), channel_id=1, source_target_pairs={{0,1},{1,2},{2,3},{3,0},{4,5},{5,6},{6,7},{7,4},{8,9},{9,10},{10,1... | collective-permute-start | bytes 786440 | tf_op jit(solution)/shard_map/ppermute | solution.py:457
  29.5 1.7 %collective-permute-start.1 = (bf16[8,128,128]{2,1,0:T(8,128)(2,1)S(1)}, bf16[8,128,128]{2,1,0:T(8,128)(2,1)}, u32[]{:S(2)}, u32[]{:S(2)}) collective-permute-start(bf16[8,128,128]{2,1,0:T(8,128)(2,1)S(1)} %get-tuple-element.19.own), channel_id=1, source_target_pairs={{0,3},{1,0},{2,1},{3,2},{4,7},{5,4},{6,5},{7,6},{8,11},{9,8},{10,9... | collective-permute-start | bytes 786440 | tf_op jit(solution)/shard_map/ppermute | solution.py:457
  31.2 1.5 %collective-permute-start.4 = (bf16[8,128,128]{2,1,0:T(8,128)(2,1)}, bf16[8,128,128]{2,1,0:T(8,128)(2,1)}, u32[]{:S(2)}, u32[]{:S(2)}) collective-permute-start(bf16[8,128,128]{2,1,0:T(8,128)(2,1)} %get-tuple-element.15.own), channel_id=1, source_target_pairs={{0,3},{1,0},{2,1},{3,2},{4,7},{5,4},{6,5},{7,6},{8,11},{9,8},{10,9... | collective-permute-start | bytes 786440 | tf_op jit(solution)/shard_map/ppermute | solution.py:457
  32.8 3.1 %collective-permute-done.3.left = bf16[8,128,128]{2,1,0:T(8,128)(2,1)} collective-permute-done((bf16[8,128,128]{2,1,0:T(8,128)(2,1)}, bf16[8,128,128]{2,1,0:T(8,128)(2,1)}, u32[]{:S(2)}, u32[]{:S(2)}) %collective-permute-start.3) | collective-permute-done | bytes 262176 | tf_op jit(solution)/shard_map/ppermute | solution.py:457
  35.9 0.3 collective-permute-start.5
  36.2 1.5 %collective-permute-start = (bf16[8,128,128]{2,1,0:T(8,128)(2,1)S(1)}, bf16[8,128,128]{2,1,0:T(8,128)(2,1)}, u32[]{:S(2)}, u32[]{:S(2)}) collective-permute-start(bf16[8,128,128]{2,1,0:T(8,128)(2,1)S(1)} %get-tuple-element.19.own), channel_id=1, source_target_pairs={{0,1},{1,2},{2,3},{3,0},{4,5},{5,6},{6,7},{7,4},{8,9},{9,10},{10,1... | collective-permute-start | bytes 786440 | tf_op jit(solution)/shard_map/ppermute | solution.py:457
  37.7 1.1 collective-permute-done.1.right
  38.8 3.0 %collective-permute-start.2 = (bf16[8,128,128]{2,1,0:T(8,128)(2,1)}, bf16[8,128,128]{2,1,0:T(8,128)(2,1)}, u32[]{:S(2)}, u32[]{:S(2)}) collective-permute-start(bf16[8,128,128]{2,1,0:T(8,128)(2,1)} %collective-permute-done.1.right), channel_id=1, source_target_pairs={{0,3},{1,0},{2,1},{3,2},{4,7},{5,4},{6,5},{7,6},{8,11},{9,8},{10,9... | collective-permute-start | bytes 786440 | tf_op jit(solution)/shard_map/ppermute | solution.py:457
  41.7 0.0 copy-start
  41.7 0.9 copy-done
  42.6 0.8 shard_map.109
  43.4 4.9 %all-to-all-start.2 = ((f32[8,32,128]{2,1,0:T(8,128)}), f32[8,32,128]{2,1,0:T(8,128)S(1)}, u32[]{:S(2)}, u32[]{:S(2)}) async-start(f32[8,32,128]{2,1,0:T(8,128)} %shard_map.109), calls=%async_computation.2 | async-start | bytes 262144 | tf_op jit(solution)/shard_map/all_to_all | solution.py:452
  48.3 2.4 %shard_map.106 = (bf16[8,4,128,384]{3,2,1,0:T(8,128)(2,1)S(1)}, bf16[128,4096]{1,0:T(8,128)(2,1)S(1)}) custom-call(s32[1]{0:T(128)} %bitcast.place_ref, bf16[3,8,4,128,128]{4,3,2,1,0:T(8,128)(2,1)} %bitcast.5, bf16[128,4096]{1,0:T(8,128)(2,1)} %out_hbm.3), custom_call_target="tpu_custom_call" | custom-call | bytes 8388612 | tf_op jit(solution)/shard_map/pallas_call | solution.py:436
  50.7 0.0 collective-permute-done.4.right
  50.8 0.0 collective-permute-done.5.far
  50.8 2.0 %shard_map.107.given_ref = f32[8,48,128]{2,1,0:T(8,128)S(1)} custom-call(bf16[8,4,128,384]{3,2,1,0:T(8,128)(2,1)S(1)} %get-tuple-element.17.weight_ref.in_weight_ref, bf16[8,128,128]{2,1,0:T(8,128)(2,1)} %get-tuple-element.15.own, bf16[8,128,128]{2,1,0:T(8,128)(2,1)} %collective-permute-done.3.left, bf16[8,128,128]{2,1,0:T(8,128)(2,1)} %collective-permute-done.4.right, ...), custom_call_target="tpu_custom_call" | custom-call | flops 402653184 | bytes 4390912 | tf_op jit(solution)/shard_map/pallas_call | solution.py:436
  52.8 0.0 collective-permute-done.left
  52.8 0.0 collective-permute-done.2.far
  52.8 2.2 %shard_map.108 = f32[8,64,128]{2,1,0:T(8,128)} custom-call(bf16[128,4096]{1,0:T(8,128)(2,1)S(1)} %get-tuple-element.18.weight_ref, bf16[8,128,128]{2,1,0:T(8,128)(2,1)S(1)} %get-tuple-element.19.own, bf16[8,128,128]{2,1,0:T(8,128)(2,1)} %collective-permute-done.left, bf16[8,128,128]{2,1,0:T(8,128)(2,1)} %collective-permute-done.1.right, ...), custom_call_target="tpu_custom_call" | custom-call | flops 134217728 | bytes 2555904 | tf_op jit(solution)/shard_map/pallas_call | solution.py:436
  55.0 0.0 all-to-all-done.2.filter_ref
  55.0 4.8 %all-to-all-start.1 = ((f32[8,64,128]{2,1,0:T(8,128)}), f32[8,64,128]{2,1,0:T(8,128)S(1)}, u32[]{:S(2)}, u32[]{:S(2)}) async-start(f32[8,64,128]{2,1,0:T(8,128)} %shard_map.108), calls=%async_computation.1 | async-start | bytes 524288 | tf_op jit(solution)/shard_map/all_to_all | solution.py:452
  59.8 6.0 %all-to-all-done.1.given_ref = f32[8,64,128]{2,1,0:T(8,128)S(1)} async-done(((f32[8,64,128]{2,1,0:T(8,128)}), f32[8,64,128]{2,1,0:T(8,128)S(1)}, u32[]{:S(2)}, u32[]{:S(2)}) %all-to-all-start.1) | async-done | bytes 262176 | tf_op jit(solution)/shard_map/all_to_all | solution.py:452
  65.9 3.0 %shard_map.110 = bf16[8,64,128]{2,1,0:T(8,128)(2,1)S(1)} custom-call(s32[1]{0:T(128)} %bitcast.3.place_ref, bf16[2,2,128,128]{3,2,1,0:T(8,128)(2,1)} %constant.20.clone.table_hbm, f32[2,9,128]{2,1,0:T(8,128)} %constant.21.clone.twiddle_hbm, f32[3,3,128]{2,1,0:T(4,128)} %taps_hbm.1, f32[2,128]{1,0:T(2,128)} %gains_hbm.1, ...), custom_call_target="tpu_custom_call" | custom-call | bytes 670212 | tf_op jit(solution)/shard_map/pallas_call | solution.py:436
  68.9 8.5 %all_to_all.26.channels_ref = bf16[8,64,128]{2,1,0:T(8,128)(2,1)S(1)} all-to-all(bf16[8,64,128]{2,1,0:T(8,128)(2,1)S(1)} %shard_map.110), channel_id=1, replica_groups=mesh['y'=4,'core'=2,'z'=8,'x'=4] {'y','core'}, dimensions={0} | all-to-all | bytes 262144 | tf_op jit(solution)/shard_map/all_to_all | solution.py:452
  77.4 3.4 %shard_map.111 = (bf16[8,2,128,128]{3,2,1,0:T(8,128)(2,1)S(1)}, bf16[8,2,128,128]{3,2,1,0:T(8,128)(2,1)S(1)}, bf16[8,2,128,128]{3,2,1,0:T(8,128)(2,1)S(1)}, bf16...) custom-call(s32[1]{0:T(128)} %bitcast.place_ref, bf16[128,4096]{1,0:T(8,128)(2,1)} %out_hbm.3, ...), custom_call_target="tpu_custom_call" | custom-call | flops 536870912 | bytes 6422532 | tf_op jit(solution)/shard_map/pallas_call | solution.py:436
  80.8 0.1 collective-permute-start.6
  80.8 3.2 %collective-permute-start.7 = (bf16[8,2,128,128]{3,2,1,0:T(8,128)(2,1)S(1)}, bf16[8,2,128,128]{3,2,1,0:T(8,128)(2,1)S(1)}, u32[]{:S(2)}, u32[]{:S(2)}) collective-permute-start(bf16[8,2,128,128]{3,2,1,0:T(8,128)(2,1)S(1)} %get-tuple-element.23), channel_id=1, source_target_pairs={{0,3},{1,0},{2,1},{3,2},{4,7},{5,4},{6,5},{7,6},{8,11},{9,8},{10,9... | collective-permute-start | bytes 1572872 | tf_op jit(solution)/shard_map/ppermute | solution.py:457
  84.1 11.4 %collective-permute-done.6.from_l_ref = bf16[8,2,128,128]{3,2,1,0:T(8,128)(2,1)S(1)} collective-permute-done((bf16[8,2,128,128]{3,2,1,0:T(8,128)(2,1)S(1)}, bf16[8,2,128,128]{3,2,1,0:T(8,128)(2,1)S(1)}, u32[]{:S(2)}, u32[]{:S(2)}) %collective-permute-start.6) | collective-permute-done | bytes 524320 | tf_op jit(solution)/shard_map/ppermute | solution.py:457
  95.5 0.0 collective-permute-done.7.from_r_ref
  95.5 0.1 shard_map.112
  95.6 0.1 collective-permute-start.8
  95.7 3.2 %collective-permute-start.9 = (bf16[4,2,128,128]{3,2,1,0:T(8,128)(2,1)S(1)}, bf16[4,2,128,128]{3,2,1,0:T(8,128)(2,1)S(1)}, u32[]{:S(2)}, u32[]{:S(2)}) collective-permute-start(bf16[4,2,128,128]{3,2,1,0:T(8,128)(2,1)S(1)} %get-tuple-element.27), channel_id=1, source_target_pairs={{0,3},{1,0},{2,1},{3,2},{4,7},{5,4},{6,5},{7,6},{8,11},{9,8},{10,9... | collective-permute-start | bytes 786440 | tf_op jit(solution)/shard_map/ppermute | solution.py:457
  98.9 5.0 %collective-permute-done.8.last_l_ref = bf16[4,2,128,128]{3,2,1,0:T(8,128)(2,1)S(1)} collective-permute-done((bf16[4,2,128,128]{3,2,1,0:T(8,128)(2,1)S(1)}, bf16[4,2,128,128]{3,2,1,0:T(8,128)(2,1)S(1)}, u32[]{:S(2)}, u32[]{:S(2)}) %collective-permute-start.8) | collective-permute-done | bytes 262176 | tf_op jit(solution)/shard_map/ppermute | solution.py:457
  103.9 0.0 collective-permute-done.9.last_r_ref
  103.9 0.2 shard_map.113
  104.1 18.3 %all_to_all.27.parts_ref = bf16[8,2,128,128]{3,2,1,0:T(8,128)(2,1)S(1)} all-to-all(bf16[8,2,128,128]{3,2,1,0:T(8,128)(2,1)S(1)} %shard_map.113), channel_id=1, replica_groups=mesh['y'=4,'core'=2,'z'=8,'x'=4] {'z'}, dimensions={0} | all-to-all | bytes 1048576 | tf_op jit(solution)/shard_map/all_to_all | solution.py:452
  122.4 0.7 shard_map.114
Async XLA Ops:
  28.0 7.9 %collective-permute-start.3 = (bf16[8,128,128]{2,1,0:T(8,128)(2,1)}, bf16[8,128,128]{2,1,0:T(8,128)(2,1)}, u32[]{:S(2)}, u32[]{:S(2)}) collective-permute-start(bf16[8,128,128]{2,1,0:T(8,128)(2,1)} %get-tuple-element.15.own), channel_id=1, source_target_pairs={{0,1},{1,2},{2,3},{3,0},{4,5},{5,6},{6,7},{7,4},{8,9},{9,10},{10,1... | collective-permute-start | bytes 786440 | tf_op jit(solution)/shard_map/ppermute | solution.py:457
  29.5 9.3 %collective-permute-start.1 = (bf16[8,128,128]{2,1,0:T(8,128)(2,1)S(1)}, bf16[8,128,128]{2,1,0:T(8,128)(2,1)}, u32[]{:S(2)}, u32[]{:S(2)}) collective-permute-start(bf16[8,128,128]{2,1,0:T(8,128)(2,1)S(1)} %get-tuple-element.19.own), channel_id=1, source_target_pairs={{0,3},{1,0},{2,1},{3,2},{4,7},{5,4},{6,5},{7,6},{8,11},{9,8},{10,9... | collective-permute-start | bytes 786440 | tf_op jit(solution)/shard_map/ppermute | solution.py:457
  31.2 19.5 %collective-permute-start.4 = (bf16[8,128,128]{2,1,0:T(8,128)(2,1)}, bf16[8,128,128]{2,1,0:T(8,128)(2,1)}, u32[]{:S(2)}, u32[]{:S(2)}) collective-permute-start(bf16[8,128,128]{2,1,0:T(8,128)(2,1)} %get-tuple-element.15.own), channel_id=1, source_target_pairs={{0,3},{1,0},{2,1},{3,2},{4,7},{5,4},{6,5},{7,6},{8,11},{9,8},{10,9... | collective-permute-start | bytes 786440 | tf_op jit(solution)/shard_map/ppermute | solution.py:457
  35.9 14.9 %collective-permute-start.5 = (bf16[8,128,128]{2,1,0:T(8,128)(2,1)}, bf16[8,128,128]{2,1,0:T(8,128)(2,1)}, u32[]{:S(2)}, u32[]{:S(2)}) collective-permute-start(bf16[8,128,128]{2,1,0:T(8,128)(2,1)} %collective-permute-done.3.left), channel_id=1, source_target_pairs={{0,1},{1,2},{2,3},{3,0},{4,5},{5,6},{6,7},{7,4},{8,9},{9,10},{10,1... | collective-permute-start | bytes 786440 | tf_op jit(solution)/shard_map/ppermute | solution.py:457
  36.2 16.6 %collective-permute-start = (bf16[8,128,128]{2,1,0:T(8,128)(2,1)S(1)}, bf16[8,128,128]{2,1,0:T(8,128)(2,1)}, u32[]{:S(2)}, u32[]{:S(2)}) collective-permute-start(bf16[8,128,128]{2,1,0:T(8,128)(2,1)S(1)} %get-tuple-element.19.own), channel_id=1, source_target_pairs={{0,1},{1,2},{2,3},{3,0},{4,5},{5,6},{6,7},{7,4},{8,9},{9,10},{10,1... | collective-permute-start | bytes 786440 | tf_op jit(solution)/shard_map/ppermute | solution.py:457
  38.8 14.0 %collective-permute-start.2 = (bf16[8,128,128]{2,1,0:T(8,128)(2,1)}, bf16[8,128,128]{2,1,0:T(8,128)(2,1)}, u32[]{:S(2)}, u32[]{:S(2)}) collective-permute-start(bf16[8,128,128]{2,1,0:T(8,128)(2,1)} %collective-permute-done.1.right), channel_id=1, source_target_pairs={{0,3},{1,0},{2,1},{3,2},{4,7},{5,4},{6,5},{7,6},{8,11},{9,8},{10,9... | collective-permute-start | bytes 786440 | tf_op jit(solution)/shard_map/ppermute | solution.py:457
  41.7 0.9 copy-start
  43.4 11.6 %all-to-all-start.2 = ((f32[8,32,128]{2,1,0:T(8,128)}), f32[8,32,128]{2,1,0:T(8,128)S(1)}, u32[]{:S(2)}, u32[]{:S(2)}) async-start(f32[8,32,128]{2,1,0:T(8,128)} %shard_map.109), calls=%async_computation.2 | async-start | bytes 262144 | tf_op jit(solution)/shard_map/all_to_all | solution.py:452
  55.0 10.9 %all-to-all-start.1 = ((f32[8,64,128]{2,1,0:T(8,128)}), f32[8,64,128]{2,1,0:T(8,128)S(1)}, u32[]{:S(2)}, u32[]{:S(2)}) async-start(f32[8,64,128]{2,1,0:T(8,128)} %shard_map.108), calls=%async_computation.1 | async-start | bytes 524288 | tf_op jit(solution)/shard_map/all_to_all | solution.py:452
  80.8 14.8 %collective-permute-start.6 = (bf16[8,2,128,128]{3,2,1,0:T(8,128)(2,1)S(1)}, bf16[8,2,128,128]{3,2,1,0:T(8,128)(2,1)S(1)}, u32[]{:S(2)}, u32[]{:S(2)}) collective-permute-start(bf16[8,2,128,128]{3,2,1,0:T(8,128)(2,1)S(1)} %get-tuple-element.22), channel_id=1, source_target_pairs={{0,1},{1,2},{2,3},{3,0},{4,5},{5,6},{6,7},{7,4},{8,9},{9,10},{10,1... | collective-permute-start | bytes 1572872 | tf_op jit(solution)/shard_map/ppermute | solution.py:457
  80.8 14.7 %collective-permute-start.7 = (bf16[8,2,128,128]{3,2,1,0:T(8,128)(2,1)S(1)}, bf16[8,2,128,128]{3,2,1,0:T(8,128)(2,1)S(1)}, u32[]{:S(2)}, u32[]{:S(2)}) collective-permute-start(bf16[8,2,128,128]{3,2,1,0:T(8,128)(2,1)S(1)} %get-tuple-element.23), channel_id=1, source_target_pairs={{0,3},{1,0},{2,1},{3,2},{4,7},{5,4},{6,5},{7,6},{8,11},{9,8},{10,9... | collective-permute-start | bytes 1572872 | tf_op jit(solution)/shard_map/ppermute | solution.py:457
  95.6 8.3 %collective-permute-start.8 = (bf16[4,2,128,128]{3,2,1,0:T(8,128)(2,1)S(1)}, bf16[4,2,128,128]{3,2,1,0:T(8,128)(2,1)S(1)}, u32[]{:S(2)}, u32[]{:S(2)}) collective-permute-start(bf16[4,2,128,128]{3,2,1,0:T(8,128)(2,1)S(1)} %get-tuple-element.26), channel_id=1, source_target_pairs={{0,1},{1,2},{2,3},{3,0},{4,5},{5,6},{6,7},{7,4},{8,9},{9,10},{10,1... | collective-permute-start | bytes 786440 | tf_op jit(solution)/shard_map/ppermute | solution.py:457
  95.7 8.2 %collective-permute-start.9 = (bf16[4,2,128,128]{3,2,1,0:T(8,128)(2,1)S(1)}, bf16[4,2,128,128]{3,2,1,0:T(8,128)(2,1)S(1)}, u32[]{:S(2)}, u32[]{:S(2)}) collective-permute-start(bf16[4,2,128,128]{3,2,1,0:T(8,128)(2,1)S(1)} %get-tuple-element.27), channel_id=1, source_target_pairs={{0,3},{1,0},{2,1},{3,2},{4,7},{5,4},{6,5},{7,6},{8,11},{9,8},{10,9... | collective-permute-start | bytes 786440 | tf_op jit(solution)/shard_map/ppermute | solution.py:457

commit v3 on v2

--- a/solution.py
+++ b/solution.py
@@ -17,6 +17,7 @@
 COARSE = 2 * BLOCKS
 KEPT = COARSE // 2 + 1
 SEQ = ("y", "core")
+NEAR_FIRST = (0, 1, 3, 2)
 
 
 def fine_table():
@@ -243,9 +244,11 @@
         out_ref[at] = held[...]
 
 
-def apart_kernel(both_ref, rows_ref, grads_ref):
-    rows_ref[...] = both_ref[:, 0]
-    grads_ref[...] = both_ref[:, 1]
+def halves_kernel(left_hbm, right_hbm, low_ref, high_ref, sems):
+    half = low_ref.shape[0]
+    sources = [left_hbm.at[pl.ds(0, half)], right_hbm.at[pl.ds(half, half)]]
+    for copy in started(sources, [low_ref, high_ref], sems):
+        copy.wait()
 
 
 def turned_filters_kernel(filter_ref, out_ref):
@@ -258,51 +261,85 @@
             ]
 
 
-def out_weight_copies(place_ref, out_hbm, out_ref, sems):
-    ring, n_z = sems.shape
-    feats = out_ref.shape[1] // (ring * n_z)
-    begun = []
-    for z in range(n_z):
-        for apart in range(ring):
-            source = lax.rem(place_ref[0] + apart, ring)
-            start = pl.multiple_of((z * ring + source) * feats, feats)
-            copy = pltpu.make_async_copy(
-                out_hbm.at[:, pl.ds(start, feats)],
-                out_ref.at[:, pl.ds((z * ring + apart) * feats, feats)],
-                sems.at[apart, z],
-            )
-            copy.start()
-            begun.append(copy)
-    return begun
-
-
-def weights_kernel(place_ref, in_hbm, out_hbm, in_ref, out_ref, in_sems, out_sems):
+def weights_kernel(place_ref, in_hbm, in_ref, sems):
     parts, _, ring, _, chans = in_hbm.shape
     begun = []
-    for apart in range(ring):
+    for slot, apart in enumerate(NEAR_FIRST):
         source = lax.rem(place_ref[0] + apart, ring)
         for part in range(parts):
             copy = pltpu.make_async_copy(
                 in_hbm.at[part, :, source],
-                in_ref.at[:, apart, :, pl.ds(part * chans, chans)],
-                in_sems.at[apart, part],
+                in_ref.at[:, slot, :, pl.ds(part * chans, chans)],
+                sems.at[slot, part],
             )
             copy.start()
             begun.append(copy)
-    begun += out_weight_copies(place_ref, out_hbm, out_ref, out_sems)
     for copy in begun:
         copy.wait()
 
 
-def side_by_side(own, right, far, left, z):
-    return jnp.concatenate([own[z], right[z], far, left[z]], axis=1)
-
-
-def project_kernel(weight_ref, own, left, right, far, out_ref):
-    n_z, tokens, _ = own.shape
-    columns = weight_ref.shape[3]
-    chans = columns // 3
+def ring_columns(place_ref, weight_ref, ring, feats, z):
+    found = []
+    for apart in NEAR_FIRST:
+        block = z * ring + lax.rem(place_ref[0] + apart, ring)
+        found.append(weight_ref[:, pl.ds(pl.multiple_of(block * feats, feats), feats)])
+    return jnp.concatenate(found, axis=1)
+
+
+def near_kernel(
+    place_ref,
+    out_hbm,
+    weight_ref,
+    own,
+    left,
+    right,
+    rows_ref,
+    grads_ref,
+    far_weight_ref,
+    out_weight_ref,
+    sems,
+):
+    (weight_copy,) = started([out_hbm], [out_weight_ref], sems)
+    n_z, _, tokens, feats = own.shape
+    ring, columns = weight_ref.shape[1], weight_ref.shape[3]
+
+    def near(which, z):
+        return jnp.concatenate([ref[z, which] for ref in (own, right, left)], axis=1)
+
+    total = jnp.zeros((tokens, columns), F32)
+    for z in range(n_z):
+        total = total + jnp.dot(
+            near(0, z),
+            weight_ref[z, : ring - 1].reshape((-1, columns)),
+            preferred_element_type=F32,
+        )
+    rows_ref[...] = total
+    weight_copy.wait()
+    total = jnp.zeros((out_weight_ref.shape[0], tokens), F32)
+    for z in range(n_z):
+        turned = ring_columns(place_ref, out_weight_ref, ring, feats, z)
+        far_weight_ref[z] = turned[:, (ring - 1) * feats :]
+        total = total + lax.dot_general(
+            turned[:, : (ring - 1) * feats],
+            near(1, z),
+            (((1,), (1,)), ((), ())),
+            preferred_element_type=F32,
+        )
+    grads_ref[...] = total
+
+
+def far_kernel(weight_ref, far_weight_ref, rows_ref, grads_ref, low, high, out_ref):
+    n_z, last = weight_ref.shape[0], weight_ref.shape[1] - 1
+    half = low.shape[0]
+    chans = far_weight_ref.shape[1]
     count = chans // BLOCKS
+    rows, grads = rows_ref[...], grads_ref[...]
+    for z in range(n_z):
+        far = low.at[z] if z < half else high.at[z - half]
+        rows = rows + jnp.dot(far[0], weight_ref[z, last], preferred_element_type=F32)
+        grads = grads + lax.dot_general(
+            far_weight_ref[z], far[1], (((1,), (1,)), ((), ())), preferred_element_type=F32
+        )
 
     def store(slot, turned):
         for block in range(BLOCKS):
@@ -310,31 +347,9 @@
                 block * count : (block + 1) * count
             ]
 
-    total = jnp.zeros((tokens, columns), F32)
-    for z in range(n_z):
-        total = total + jnp.dot(
-            side_by_side(own, right, far[z], left, z),
-            weight_ref[z].reshape((-1, columns)),
-            preferred_element_type=F32,
-        )
     for which in range(3):
-        store(which, total[:, which * chans : (which + 1) * chans].T)
-
-
-def project_grad_kernel(weight_ref, own, left, right, far, given_ref, out_ref):
-    n_z, tokens, _ = own.shape
-    wide = weight_ref.shape[1] // n_z
-    total = jnp.zeros((weight_ref.shape[0], tokens), F32)
-    for z in range(n_z):
-        total = total + lax.dot_general(
-            weight_ref[:, z * wide : (z + 1) * wide],
-            side_by_side(own, right, far[z], left, z),
-            (((1,), (1,)), ((), ())),
-            preferred_element_type=F32,
-        )
-    count = out_ref.shape[1] // 4
-    out_ref[:, : 3 * count] = given_ref[...]
-    out_ref[:, 3 * count :] = total.reshape((BLOCKS, count, tokens))
+        store(which, rows[:, which * chans : (which + 1) * chans].T)
+    store(3, grads)
 
 
 def partial_kernel(
@@ -348,12 +363,12 @@
     keep_r_ref,
     keep_l_ref,
     out_weight_ref,
-    out_sems,
+    sems,
 ):
     n_z, _, feats, tokens = own_ref.shape
     half = n_z // 2
-    ring = out_sems.shape[0]
-    weight_copies = out_weight_copies(place_ref, out_hbm, out_weight_ref, out_sems)
+    ring = in_weight_ref.shape[1]
+    (weight_copy,) = started([out_hbm], [out_weight_ref], sems)
     count = channels_ref.shape[1] // 4
     second, *grads = [
         channels_ref[:, slot * count : (slot + 1) * count].reshape((BLOCKS * count, tokens))
@@ -365,10 +380,10 @@
     columns = in_weight_ref.shape[3]
 
     def mixed(z):
-        for copy in weight_copies[z * ring : (z + 1) * ring]:
-            copy.wait()
         product = jnp.dot(
-            second, out_weight_ref[:, z * wide : (z + 1) * wide], preferred_element_type=F32
+            second,
+            ring_columns(place_ref, out_weight_ref, ring, feats, z),
+            preferred_element_type=F32,
         )
         return [product[:, at : at + feats].astype(BF16) for at in range(0, wide, feats)]
 
@@ -379,8 +394,10 @@
         return [product[at : at + feats].astype(BF16) for at in range(0, wide, feats)]
 
     for output, pieces in ((1, token_grad), (0, mixed)):
+        if output == 0:
+            weight_copy.wait()
         for z in range(n_z):
-            own, ahead, far, behind = pieces(z)
+            own, ahead, behind, far = pieces(z)
             own_ref[z, output] = own
             if z < half:
                 right_ref[z, output] = far
@@ -480,46 +497,49 @@
         scratch=[pltpu.VMEM((2, rows, LANES), BF16), pltpu.SemaphoreType.DMA((2,))],
     )
     both = exchanged(sent, "z")
-    one = shape_of((n_z, rows, LANES), BF16)
-    own_rows, own_grads = run(apart_kernel, (one, one), both)
-    left_rows = shifted(own_rows, 1)
-    right_rows = shifted(own_rows, -1)
-    left_grads = shifted(own_grads, 1)
-    right_grads = shifted(own_grads, -1)
-    far_rows = shifted(left_rows, 1)
-    far_grads = shifted(right_grads, -1)
+    left, right = shifted(both, 1), shifted(both, -1)
+    some = shape_of((half, 2, rows, LANES), BF16)
+    low, high = run(
+        halves_kernel, (some, some), far=(left, right), scratch=[pltpu.SemaphoreType.DMA((2,))]
+    )
+    low, high = shifted(low, 1), shifted(high, -1)
 
     turned_filters = run(
-        turned_filters_kernel, shape_of((BLOCKS, 2 * count, rows), F32), after(filters, own_rows)
+        turned_filters_kernel, shape_of((BLOCKS, 2 * count, rows), F32), after(filters, both)
     )
     turned_filters = exchanged(turned_filters, SEQ)
-    weight_sems = pltpu.SemaphoreType.DMA((ring, n_z))
-    in_turned, out_turned = run(
+    in_turned = run(
         weights_kernel,
-        (shape_of((n_z, ring, LANES, 3 * chans), BF16), shape_of(out_weight.shape, BF16)),
-        far=(after(split_in, own_rows), out_weight),
+        shape_of((n_z, ring, LANES, 3 * chans), BF16),
+        far=(after(split_in, both),),
         place=place,
-        scratch=[pltpu.SemaphoreType.DMA((ring, 3)), weight_sems],
+        scratch=[pltpu.SemaphoreType.DMA((ring, 3))],
+    )
+    out_scratch = [pltpu.VMEM(out_weight.shape, BF16), pltpu.SemaphoreType.DMA((1,))]
+    *near, far_weight = run(
+        near_kernel,
+        (
+            shape_of((rows, 3 * chans), F32),
+            shape_of((chans, rows), F32),
+            shape_of((n_z, chans, LANES), BF16),
+        ),
+        in_turned,
+        both,
+        left,
+        right,
+        flops=2 * rows * width * 3 * chans,
+        place=place,
+        far=(out_weight,),
+        scratch=out_scratch,
     )
     given = run(
-        project_kernel,
-        shape_of((BLOCKS, 3 * count, rows), F32),
+        far_kernel,
+        shape_of((BLOCKS, 4 * count, rows), F32),
         in_turned,
-        own_rows,
-        left_rows,
-        right_rows,
-        far_rows,
-        flops=2 * rows * width * 3 * chans,
-    )
-    given = run(
-        project_grad_kernel,
-        shape_of((BLOCKS, 4 * count, rows), F32),
-        out_turned,
-        own_grads,
-        left_grads,
-        right_grads,
-        far_grads,
-        given,
+        far_weight,
+        *near,
+        low,
+        high,
         flops=2 * rows * width * chans,
     )
     channels = run(
@@ -549,7 +569,7 @@
         flops=2 * rows * width * 4 * chans,
         place=place,
         far=(out_weight,),
-        scratch=[pltpu.VMEM(out_weight.shape, BF16), weight_sems],
+        scratch=out_scratch,
     )
     from_l, from_r = shifted(to_right, 1), shifted(to_left, -1)
     to_right, to_left = run(

time: 125 us -> 128 us (1.024)
  waiting for transfers between devices: 26.7 us -> 31.7 us
  starting transfers between devices: 25.8 us -> 22.9 us
  local copies, waits for them, and re-layouts: 0.9 us -> 3.53 us
    ppermute x10 -> x8, waiting for transfers between devices: 20.6 us -> 25.6 us  [shifted(): lax.ppermute(value, 'x', [(at, (at + steps) % ring) for at in range(ring)])]
    ppermute x10 -> x8, starting transfers between devices: 16.1 us -> 13.2 us  [shifted(): lax.ppermute(value, 'x', [(at, (at + steps) % ring) for at in range(ring)])]
    unnamed x2 -> x14, local copies, waits for them, and re-layouts: 0.9 us -> 3.53 us
  transfers between devices with their start and end apart: 12 -> 10, of which waited for: 5 -> 4; matrix products, arithmetic and copies ran while one was open for 0% -> 0% of each run, Pallas kernels for 6% -> 5%
where the time goes in v3:
time: 128 us; the launch traced here: 127 us
  blocking collectives  52.5 us (41%)
  waiting for transfers between devices  31.7 us (25%)
  starting transfers between devices  22.9 us (18%)
  Pallas kernels  15.2 us (12%)
  local copies, waits for them, and re-layouts  3.53 us (3%)
    all_to_all x3, blocking collectives, exchanged(): return lax.all_to_all(value, axis, 0, 0, tiled=True)  52.5 us
    ppermute x8, waiting for transfers between devices, shifted(): lax.ppermute(value, 'x', [(at, (at + steps) % ring) for at in range(ring)])  25.6 us
    pallas_call x11, Pallas kernels, run(): pl.pallas_call(kernel, out_shape=out_shape, in_specs=specs, out_specs=in_...  15.2 us
    ppermute x8, starting transfers between devices, shifted(): lax.ppermute(value, 'x', [(at, (at + steps) % ring) for at in range(ring)])  13.2 us
    all_to_all x2, starting transfers between devices, exchanged(): return lax.all_to_all(value, axis, 0, 0, tiled=True)  9.72 us
    all_to_all x2, waiting for transfers between devices, exchanged(): return lax.all_to_all(value, axis, 0, 0, tiled=True)  6.05 us
    unnamed x14, local copies, waits for them, and re-layouts  3.53 us
  transfers between devices with their start and end apart: 10, of which 4 were waited for; matrix products, arithmetic and copies ran while one was open for 0% of the time, Pallas kernels for 5%

profile of v3, /device:TPU:8, one launch (start us, length us, event | category | flops | bytes accessed | tf_op | source)
XLA Modules:
  0.0 126.5 jit_solution(5879940019721504725)
XLA Ops:
  0.6 0.9 shard_map.104
  1.5 25.8 %all_to_all.25.own = bf16[8,2,128,128]{3,2,1,0:T(8,128)(2,1)S(1)} all-to-all(bf16[8,2,128,128]{3,2,1,0:T(8,128)(2,1)S(1)} %shard_map.104), channel_id=1, replica_groups=mesh['y'=4,'core'=2,'z'=8,'x'=4] {'z'}, dimensions={0} | all-to-all | bytes 1048576 | tf_op jit(solution)/shard_map/all_to_all | solution.py:469
  27.3 1.5 %collective-permute-start = (bf16[8,2,128,128]{3,2,1,0:T(8,128)(2,1)S(1)}, bf16[8,2,128,128]{3,2,1,0:T(8,128)(2,1)S(1)}, u32[]{:S(2)}, u32[]{:S(2)}) collective-permute-start(bf16[8,2,128,128]{3,2,1,0:T(8,128)(2,1)S(1)} %all_to_all.25.own), channel_id=1, source_target_pairs={{0,1},{1,2},{2,3},{3,0},{4,5},{5,6},{6,7},{7,4},{8,9},{9,10},{10,1... | collective-permute-start | bytes 1572872 | tf_op jit(solution)/shard_map/ppermute | solution.py:474
  28.7 1.7 %collective-permute-start.1 = (bf16[8,2,128,128]{3,2,1,0:T(8,128)(2,1)S(1)}, bf16[8,2,128,128]{3,2,1,0:T(8,128)(2,1)S(1)}, u32[]{:S(2)}, u32[]{:S(2)}) collective-permute-start(bf16[8,2,128,128]{3,2,1,0:T(8,128)(2,1)S(1)} %all_to_all.25.own), channel_id=1, source_target_pairs={{0,3},{1,0},{2,1},{3,2},{4,7},{5,4},{6,5},{7,6},{8,11},{9,8},{10,9... | collective-permute-start | bytes 1572872 | tf_op jit(solution)/shard_map/ppermute | solution.py:474
  30.5 0.0 copy-start
  30.5 0.8 copy-done
  31.3 9.2 %collective-permute-done.left.left_hbm = bf16[8,2,128,128]{3,2,1,0:T(8,128)(2,1)S(1)} collective-permute-done((bf16[8,2,128,128]{3,2,1,0:T(8,128)(2,1)S(1)}, bf16[8,2,128,128]{3,2,1,0:T(8,128)(2,1)S(1)}, u32[]{:S(2)}, u32[]{:S(2)}) %collective-permute-start) | collective-permute-done | bytes 524320 | tf_op jit(solution)/shard_map/ppermute | solution.py:474
  40.5 0.0 copy-start.2
  40.5 0.0 collective-permute-done.1.right.right_hbm
  40.5 0.8 copy-done.2
  41.3 0.0 copy-start.4
  41.3 0.8 copy-done.4
  42.1 1.8 %shard_map.107 = (bf16[4,2,128,128]{3,2,1,0:T(8,128)(2,1)}, bf16[4,2,128,128]{3,2,1,0:T(8,128)(2,1)}) custom-call(bf16[8,2,128,128]{3,2,1,0:T(8,128)(2,1)} %copy-done.2, bf16[8,2,128,128]{3,2,1,0:T(8,128)(2,1)} %copy-done.4), custom_call_target="tpu_custom_call" | custom-call | bytes 1572864 | tf_op jit(solution)/shard_map/pallas_call | solution.py:453
  43.9 0.8 collective-permute-start.2
  44.7 2.5 %collective-permute-start.3 = (bf16[4,2,128,128]{3,2,1,0:T(8,128)(2,1)}, bf16[4,2,128,128]{3,2,1,0:T(8,128)(2,1)}, u32[]{:S(2)}, u32[]{:S(2)}) collective-permute-start(bf16[4,2,128,128]{3,2,1,0:T(8,128)(2,1)} %get-tuple-element.21), channel_id=1, source_target_pairs={{0,3},{1,0},{2,1},{3,2},{4,7},{5,4},{6,5},{7,6},{8,11},{9,8},{10,9... | collective-permute-start | bytes 786440 | tf_op jit(solution)/shard_map/ppermute | solution.py:474
  47.2 0.0 copy-start.6
  47.2 0.9 copy-done.6
  48.1 0.8 shard_map.109
  48.9 4.9 %all-to-all-start.2 = ((f32[8,32,128]{2,1,0:T(8,128)}), f32[8,32,128]{2,1,0:T(8,128)S(1)}, u32[]{:S(2)}, u32[]{:S(2)}) async-start(f32[8,32,128]{2,1,0:T(8,128)} %shard_map.109), calls=%async_computation.2 | async-start | bytes 262144 | tf_op jit(solution)/shard_map/all_to_all | solution.py:469
  53.8 0.0 copy-start.1
  53.8 0.0 copy-start.3
  53.8 0.0 copy-start.5
  53.8 2.1 %shard_map.105.weight_ref.in_weight_ref = bf16[8,4,128,384]{3,2,1,0:T(8,128)(2,1)S(1)} custom-call(s32[1]{0:T(128)} %bitcast.place_ref, bf16[3,8,4,128,128]{4,3,2,1,0:T(8,128)(2,1)} %bitcast.5), custom_call_target="tpu_custom_call" | custom-call | bytes 6291460 | tf_op jit(solution)/shard_map/pallas_call | solution.py:453
  55.9 0.0 copy-done.1
  55.9 0.1 copy-done.3
  56.0 0.2 copy-done.5
  56.1 1.8 %shard_map.106 = (f32[128,384]{1,0:T(8,128)S(1)}, f32[128,128]{1,0:T(8,128)S(1)}, bf16[8,128,128]{2,1,0:T(8,128)(2,1)S(1)}) custom-call(s32[1]{0:T(128)} %bitcast.place_ref, bf16[128,4096]{1,0:T(8,128)(2,1)} %out_hbm.3, bf16[8,4,128,384]{3,2,1,0:T(8,128)(2,1)S(1)} %shard_map.105.weight_ref.in_weight_ref, bf16[8,2,128,128]{3,2,1,0:T(8,128)(2,1)S(1)} %copy-done.1, ...), custom_call_target="tpu_custom_call" | custom-call | flops 402653184 | bytes 6291460 | tf_op jit(solution)/shard_map/pallas_call | solution.py:453
  57.9 0.0 collective-permute-done.2.low
  57.9 0.0 collective-permute-done.3.high
  57.9 2.2 %shard_map.108 = f32[8,64,128]{2,1,0:T(8,128)} custom-call(bf16[8,4,128,384]{3,2,1,0:T(8,128)(2,1)S(1)} %shard_map.105.weight_ref.in_weight_ref, bf16[8,128,128]{2,1,0:T(8,128)(2,1)S(1)} %get-tuple-element.17.far_weight_ref, f32[128,384]{1,0:T(8,128)S(1)} %get-tuple-element.18.rows_ref, f32[128,128]{1,0:T(8,128)S(1)} %get-tuple-element.19.grads_ref, ...), custom_call_target="tpu_custom_call" | custom-call | flops 134217728 | bytes 4456448 | tf_op jit(solution)/shard_map/pallas_call | solution.py:453
  60.2 0.0 all-to-all-done.2.filter_ref
  60.2 4.8 %all-to-all-start.1 = ((f32[8,64,128]{2,1,0:T(8,128)}), f32[8,64,128]{2,1,0:T(8,128)S(1)}, u32[]{:S(2)}, u32[]{:S(2)}) async-start(f32[8,64,128]{2,1,0:T(8,128)} %shard_map.108), calls=%async_computation.1 | async-start | bytes 524288 | tf_op jit(solution)/shard_map/all_to_all | solution.py:469
  65.0 6.0 %all-to-all-done.1.given_ref = f32[8,64,128]{2,1,0:T(8,128)S(1)} async-done(((f32[8,64,128]{2,1,0:T(8,128)}), f32[8,64,128]{2,1,0:T(8,128)S(1)}, u32[]{:S(2)}, u32[]{:S(2)}) %all-to-all-start.1) | async-done | bytes 262176 | tf_op jit(solution)/shard_map/all_to_all | solution.py:469
  71.0 3.0 %shard_map.110 = bf16[8,64,128]{2,1,0:T(8,128)(2,1)S(1)} custom-call(s32[1]{0:T(128)} %bitcast.3.place_ref, bf16[2,2,128,128]{3,2,1,0:T(8,128)(2,1)} %constant.20.clone.table_hbm, f32[2,9,128]{2,1,0:T(8,128)} %constant.21.clone.twiddle_hbm, f32[3,3,128]{2,1,0:T(4,128)} %taps_hbm.1, f32[2,128]{1,0:T(2,128)} %gains_hbm.1, ...), custom_call_target="tpu_custom_call" | custom-call | bytes 670212 | tf_op jit(solution)/shard_map/pallas_call | solution.py:453
  74.0 8.5 %all_to_all.26.channels_ref = bf16[8,64,128]{2,1,0:T(8,128)(2,1)S(1)} all-to-all(bf16[8,64,128]{2,1,0:T(8,128)(2,1)S(1)} %shard_map.110), channel_id=1, replica_groups=mesh['y'=4,'core'=2,'z'=8,'x'=4] {'y','core'}, dimensions={0} | all-to-all | bytes 262144 | tf_op jit(solution)/shard_map/all_to_all | solution.py:469
  82.5 1.7 %shard_map.111 = (bf16[8,2,128,128]{3,2,1,0:T(8,128)(2,1)S(1)}, bf16[8,2,128,128]{3,2,1,0:T(8,128)(2,1)S(1)}, bf16[8,2,128,128]{3,2,1,0:T(8,128)(2,1)S(1)}, bf16...) custom-call(s32[1]{0:T(128)} %bitcast.place_ref, bf16[128,4096]{1,0:T(8,128)(2,1)} %out_hbm.3, ...), custom_call_target="tpu_custom_call" | custom-call | flops 536870912 | bytes 6422532 | tf_op jit(solution)/shard_map/pallas_call | solution.py:453
  84.2 0.1 collective-permute-start.4
  84.3 3.2 %collective-permute-start.5 = (bf16[8,2,128,128]{3,2,1,0:T(8,128)(2,1)S(1)}, bf16[8,2,128,128]{3,2,1,0:T(8,128)(2,1)S(1)}, u32[]{:S(2)}, u32[]{:S(2)}) collective-permute-start(bf16[8,2,128,128]{3,2,1,0:T(8,128)(2,1)S(1)} %get-tuple-element.25), channel_id=1, source_target_pairs={{0,3},{1,0},{2,1},{3,2},{4,7},{5,4},{6,5},{7,6},{8,11},{9,8},{10,9... | collective-permute-start | bytes 1572872 | tf_op jit(solution)/shard_map/ppermute | solution.py:474
  87.5 11.4 %collective-permute-done.4.from_l_ref = bf16[8,2,128,128]{3,2,1,0:T(8,128)(2,1)S(1)} collective-permute-done((bf16[8,2,128,128]{3,2,1,0:T(8,128)(2,1)S(1)}, bf16[8,2,128,128]{3,2,1,0:T(8,128)(2,1)S(1)}, u32[]{:S(2)}, u32[]{:S(2)}) %collective-permute-start.4) | collective-permute-done | bytes 524320 | tf_op jit(solution)/shard_map/ppermute | solution.py:474
  98.9 0.0 collective-permute-done.5.from_r_ref
  98.9 0.1 shard_map.112
  99.1 0.1 collective-permute-start.6
  99.1 3.2 %collective-permute-start.7 = (bf16[4,2,128,128]{3,2,1,0:T(8,128)(2,1)S(1)}, bf16[4,2,128,128]{3,2,1,0:T(8,128)(2,1)S(1)}, u32[]{:S(2)}, u32[]{:S(2)}) collective-permute-start(bf16[4,2,128,128]{3,2,1,0:T(8,128)(2,1)S(1)} %get-tuple-element.29), channel_id=1, source_target_pairs={{0,3},{1,0},{2,1},{3,2},{4,7},{5,4},{6,5},{7,6},{8,11},{9,8},{10,9... | collective-permute-start | bytes 786440 | tf_op jit(solution)/shard_map/ppermute | solution.py:474
  102.4 5.0 %collective-permute-done.6.last_l_ref = bf16[4,2,128,128]{3,2,1,0:T(8,128)(2,1)S(1)} collective-permute-done((bf16[4,2,128,128]{3,2,1,0:T(8,128)(2,1)S(1)}, bf16[4,2,128,128]{3,2,1,0:T(8,128)(2,1)S(1)}, u32[]{:S(2)}, u32[]{:S(2)}) %collective-permute-start.6) | collective-permute-done | bytes 262176 | tf_op jit(solution)/shard_map/ppermute | solution.py:474
  107.3 0.0 collective-permute-done.7.last_r_ref
  107.3 0.2 shard_map.113
  107.5 18.3 %all_to_all.27.parts_ref = bf16[8,2,128,128]{3,2,1,0:T(8,128)(2,1)S(1)} all-to-all(bf16[8,2,128,128]{3,2,1,0:T(8,128)(2,1)S(1)} %shard_map.113), channel_id=1, replica_groups=mesh['y'=4,'core'=2,'z'=8,'x'=4] {'z'}, dimensions={0} | all-to-all | bytes 1048576 | tf_op jit(solution)/shard_map/all_to_all | solution.py:469
  125.8 0.7 shard_map.114
Async XLA Ops:
  27.3 13.2 %collective-permute-start = (bf16[8,2,128,128]{3,2,1,0:T(8,128)(2,1)S(1)}, bf16[8,2,128,128]{3,2,1,0:T(8,128)(2,1)S(1)}, u32[]{:S(2)}, u32[]{:S(2)}) collective-permute-start(bf16[8,2,128,128]{3,2,1,0:T(8,128)(2,1)S(1)} %all_to_all.25.own), channel_id=1, source_target_pairs={{0,1},{1,2},{2,3},{3,0},{4,5},{5,6},{6,7},{7,4},{8,9},{9,10},{10,1... | collective-permute-start | bytes 1572872 | tf_op jit(solution)/shard_map/ppermute | solution.py:474
  28.7 11.7 %collective-permute-start.1 = (bf16[8,2,128,128]{3,2,1,0:T(8,128)(2,1)S(1)}, bf16[8,2,128,128]{3,2,1,0:T(8,128)(2,1)S(1)}, u32[]{:S(2)}, u32[]{:S(2)}) collective-permute-start(bf16[8,2,128,128]{3,2,1,0:T(8,128)(2,1)S(1)} %all_to_all.25.own), channel_id=1, source_target_pairs={{0,3},{1,0},{2,1},{3,2},{4,7},{5,4},{6,5},{7,6},{8,11},{9,8},{10,9... | collective-permute-start | bytes 1572872 | tf_op jit(solution)/shard_map/ppermute | solution.py:474
  30.5 0.8 copy-start
  40.5 0.8 copy-start.2
  41.3 0.8 copy-start.4
  43.9 14.0 %collective-permute-start.2 = (bf16[4,2,128,128]{3,2,1,0:T(8,128)(2,1)}, bf16[4,2,128,128]{3,2,1,0:T(8,128)(2,1)S(1)}, u32[]{:S(2)}, u32[]{:S(2)}) collective-permute-start(bf16[4,2,128,128]{3,2,1,0:T(8,128)(2,1)} %get-tuple-element.20), channel_id=1, source_target_pairs={{0,1},{1,2},{2,3},{3,0},{4,5},{5,6},{6,7},{7,4},{8,9},{9,10},{10,1... | collective-permute-start | bytes 786440 | tf_op jit(solution)/shard_map/ppermute | solution.py:474
  44.7 13.2 %collective-permute-start.3 = (bf16[4,2,128,128]{3,2,1,0:T(8,128)(2,1)}, bf16[4,2,128,128]{3,2,1,0:T(8,128)(2,1)}, u32[]{:S(2)}, u32[]{:S(2)}) collective-permute-start(bf16[4,2,128,128]{3,2,1,0:T(8,128)(2,1)} %get-tuple-element.21), channel_id=1, source_target_pairs={{0,3},{1,0},{2,1},{3,2},{4,7},{5,4},{6,5},{7,6},{8,11},{9,8},{10,9... | collective-permute-start | bytes 786440 | tf_op jit(solution)/shard_map/ppermute | solution.py:474
  47.2 0.9 copy-start.6
  48.9 11.3 %all-to-all-start.2 = ((f32[8,32,128]{2,1,0:T(8,128)}), f32[8,32,128]{2,1,0:T(8,128)S(1)}, u32[]{:S(2)}, u32[]{:S(2)}) async-start(f32[8,32,128]{2,1,0:T(8,128)} %shard_map.109), calls=%async_computation.2 | async-start | bytes 262144 | tf_op jit(solution)/shard_map/all_to_all | solution.py:469
  53.8 2.1 %copy-start.1 = (bf16[8,2,128,128]{3,2,1,0:T(8,128)(2,1)S(1)}, bf16[8,2,128,128]{3,2,1,0:T(8,128)(2,1)}, u32[]{:S(2)}) copy-start(bf16[8,2,128,128]{3,2,1,0:T(8,128)(2,1)} %copy-done) | copy-start | bytes 1572868
  53.8 2.1 %copy-start.3 = (bf16[8,2,128,128]{3,2,1,0:T(8,128)(2,1)S(1)}, bf16[8,2,128,128]{3,2,1,0:T(8,128)(2,1)}, u32[]{:S(2)}) copy-start(bf16[8,2,128,128]{3,2,1,0:T(8,128)(2,1)} %copy-done.2) | copy-start | bytes 1572868
  53.8 2.3 %copy-start.5 = (bf16[8,2,128,128]{3,2,1,0:T(8,128)(2,1)S(1)}, bf16[8,2,128,128]{3,2,1,0:T(8,128)(2,1)}, u32[]{:S(2)}) copy-start(bf16[8,2,128,128]{3,2,1,0:T(8,128)(2,1)} %copy-done.4) | copy-start | bytes 1572868
  60.2 10.9 %all-to-all-start.1 = ((f32[8,64,128]{2,1,0:T(8,128)}), f32[8,64,128]{2,1,0:T(8,128)S(1)}, u32[]{:S(2)}, u32[]{:S(2)}) async-start(f32[8,64,128]{2,1,0:T(8,128)} %shard_map.108), calls=%async_computation.1 | async-start | bytes 524288 | tf_op jit(solution)/shard_map/all_to_all | solution.py:469
  84.2 14.8 %collective-permute-start.4 = (bf16[8,2,128,128]{3,2,1,0:T(8,128)(2,1)S(1)}, bf16[8,2,128,128]{3,2,1,0:T(8,128)(2,1)S(1)}, u32[]{:S(2)}, u32[]{:S(2)}) collective-permute-start(bf16[8,2,128,128]{3,2,1,0:T(8,128)(2,1)S(1)} %get-tuple-element.24), channel_id=1, source_target_pairs={{0,1},{1,2},{2,3},{3,0},{4,5},{5,6},{6,7},{7,4},{8,9},{9,10},{10,1... | collective-permute-start | bytes 1572872 | tf_op jit(solution)/shard_map/ppermute | solution.py:474
  84.3 14.7 %collective-permute-start.5 = (bf16[8,2,128,128]{3,2,1,0:T(8,128)(2,1)S(1)}, bf16[8,2,128,128]{3,2,1,0:T(8,128)(2,1)S(1)}, u32[]{:S(2)}, u32[]{:S(2)}) collective-permute-start(bf16[8,2,128,128]{3,2,1,0:T(8,128)(2,1)S(1)} %get-tuple-element.25), channel_id=1, source_target_pairs={{0,3},{1,0},{2,1},{3,2},{4,7},{5,4},{6,5},{7,6},{8,11},{9,8},{10,9... | collective-permute-start | bytes 1572872 | tf_op jit(solution)/shard_map/ppermute | solution.py:474
  99.1 8.3 %collective-permute-start.6 = (bf16[4,2,128,128]{3,2,1,0:T(8,128)(2,1)S(1)}, bf16[4,2,128,128]{3,2,1,0:T(8,128)(2,1)S(1)}, u32[]{:S(2)}, u32[]{:S(2)}) collective-permute-start(bf16[4,2,128,128]{3,2,1,0:T(8,128)(2,1)S(1)} %get-tuple-element.28), channel_id=1, source_target_pairs={{0,1},{1,2},{2,3},{3,0},{4,5},{5,6},{6,7},{7,4},{8,9},{9,10},{10,1... | collective-permute-start | bytes 786440 | tf_op jit(solution)/shard_map/ppermute | solution.py:474
  99.1 8.2 %collective-permute-start.7 = (bf16[4,2,128,128]{3,2,1,0:T(8,128)(2,1)S(1)}, bf16[4,2,128,128]{3,2,1,0:T(8,128)(2,1)S(1)}, u32[]{:S(2)}, u32[]{:S(2)}) collective-permute-start(bf16[4,2,128,128]{3,2,1,0:T(8,128)(2,1)S(1)} %get-tuple-element.29), channel_id=1, source_target_pairs={{0,3},{1,0},{2,1},{3,2},{4,7},{5,4},{6,5},{7,6},{8,11},{9,8},{10,9... | collective-permute-start | bytes 786440 | tf_op jit(solution)/shard_map/ppermute | solution.py:474

commit v4 on v3

--- a/solution.py
+++ b/solution.py
@@ -358,8 +358,10 @@
     in_weight_ref,
     channels_ref,
     own_ref,
-    right_ref,
-    left_ref,
+    far_r_ref,
+    far_l_ref,
+    near_r_ref,
+    near_l_ref,
     keep_r_ref,
     keep_l_ref,
     out_weight_ref,
@@ -400,29 +402,28 @@
             own, ahead, behind, far = pieces(z)
             own_ref[z, output] = own
             if z < half:
-                right_ref[z, output] = far
+                far_r_ref[z, output] = far
                 keep_r_ref[z, output] = ahead
-                left_ref[z, output] = behind
+                near_l_ref[z, output] = behind
             else:
-                right_ref[z, output] = ahead
-                left_ref[z, output] = far
+                near_r_ref[z - half, output] = ahead
+                far_l_ref[z - half, output] = far
                 keep_l_ref[z - half, output] = behind
 
 
 def merge_kernel(keep_r_ref, keep_l_ref, from_l_ref, from_r_ref, right_ref, left_ref):
-    half = keep_r_ref.shape[0]
-    right_ref[...] = (keep_r_ref[...].astype(F32) + from_l_ref[:half].astype(F32)).astype(BF16)
-    left_ref[...] = (keep_l_ref[...].astype(F32) + from_r_ref[half:].astype(F32)).astype(BF16)
-
-
-def ring_sum_kernel(own_ref, from_l_ref, from_r_ref, last_l_ref, last_r_ref, out_ref):
+    right_ref[...] = (keep_r_ref[...].astype(F32) + from_l_ref[...].astype(F32)).astype(BF16)
+    left_ref[...] = (keep_l_ref[...].astype(F32) + from_r_ref[...].astype(F32)).astype(BF16)
+
+
+def ring_sum_kernel(own_ref, near_l_ref, near_r_ref, last_l_ref, last_r_ref, out_ref):
     half = last_l_ref.shape[0]
     own_low, own_high = own_ref[:half].astype(F32), own_ref[half:].astype(F32)
     out_ref[:half] = (
-        own_low + last_l_ref[...].astype(F32) + from_r_ref[:half].astype(F32)
+        own_low + last_l_ref[...].astype(F32) + near_r_ref[...].astype(F32)
     ).astype(BF16)
     out_ref[half:] = (
-        own_high + from_l_ref[half:].astype(F32) + last_r_ref[...].astype(F32)
+        own_high + near_l_ref[...].astype(F32) + last_r_ref[...].astype(F32)
     ).astype(BF16)
 
 
@@ -561,9 +562,9 @@
         ],
     )
     whole, part = (n_z, 2, LANES, rows), (half, 2, LANES, rows)
-    own, to_right, to_left, keep_r, keep_l = run(
+    own, far_r, far_l, near_r, near_l, keep_r, keep_l = run(
         partial_kernel,
-        tuple(shape_of(shape, BF16) for shape in (whole, whole, whole, part, part)),
+        tuple(shape_of(shape, BF16) for shape in (whole, *[part] * 6)),
         in_turned,
         exchanged(channels, SEQ),
         flops=2 * rows * width * 4 * chans,
@@ -571,12 +572,14 @@
         far=(out_weight,),
         scratch=out_scratch,
     )
-    from_l, from_r = shifted(to_right, 1), shifted(to_left, -1)
+    from_l, from_r = shifted(far_r, 1), shifted(far_l, -1)
+    near_l = shifted(near_l, -1)
+    near_r = shifted(near_r, 1)
     to_right, to_left = run(
         merge_kernel, (shape_of(part, BF16), shape_of(part, BF16)), keep_r, keep_l, from_l, from_r
     )
     last_l, last_r = shifted(to_right, 1), shifted(to_left, -1)
-    parts = run(ring_sum_kernel, shape_of(whole, BF16), own, from_l, from_r, last_l, last_r)
+    parts = run(ring_sum_kernel, shape_of(whole, BF16), own, near_r, near_l, last_l, last_r)
     out = shape_of((rows, LANES), BF16)
     return run(last_sum_kernel, (out, out), exchanged(parts, "z"))
 

time: 128 us -> 126 us (0.984)
  waiting for transfers between devices: 31.7 us -> 25.5 us
  starting transfers between devices: 22.9 us -> 26.2 us
    ppermute x8 -> x10, waiting for transfers between devices: 25.6 us -> 19.5 us  [shifted(): lax.ppermute(value, 'x', [(at, (at + steps) % ring) for at in range(ring)])]
    ppermute x8 -> x10, starting transfers between devices: 13.2 us -> 16.5 us  [shifted(): lax.ppermute(value, 'x', [(at, (at + steps) % ring) for at in range(ring)])]
  transfers between devices with their start and end apart: 10 -> 12, of which waited for: 4 -> 5; matrix products, arithmetic and copies ran while one was open for 0% -> 0% of each run, Pallas kernels for 5% -> 6%
where the time goes in v4:
time: 126 us; the launch traced here: 125 us
  blocking collectives  53.4 us (42%)
  starting transfers between devices  26.2 us (21%)
  waiting for transfers between devices  25.5 us (20%)
  Pallas kernels  15.2 us (12%)
  local copies, waits for them, and re-layouts  3.54 us (3%)
    all_to_all x3, blocking collectives, exchanged(): return lax.all_to_all(value, axis, 0, 0, tiled=True)  53.4 us
    ppermute x10, waiting for transfers between devices, shifted(): lax.ppermute(value, 'x', [(at, (at + steps) % ring) for at in range(ring)])  19.5 us
    ppermute x10, starting transfers between devices, shifted(): lax.ppermute(value, 'x', [(at, (at + steps) % ring) for at in range(ring)])  16.5 us
    pallas_call x11, Pallas kernels, run(): pl.pallas_call(kernel, out_shape=out_shape, in_specs=specs, out_specs=in_...  15.2 us
    all_to_all x2, starting transfers between devices, exchanged(): return lax.all_to_all(value, axis, 0, 0, tiled=True)  9.72 us
    all_to_all x2, waiting for transfers between devices, exchanged(): return lax.all_to_all(value, axis, 0, 0, tiled=True)  6.05 us
    unnamed x14, local copies, waits for them, and re-layouts  3.54 us
  transfers between devices with their start and end apart: 12, of which 5 were waited for; matrix products, arithmetic and copies ran while one was open for 0% of the time, Pallas kernels for 6%

profile of v4, /device:TPU:8, one launch (start us, length us, event | category | flops | bytes accessed | tf_op | source)
XLA Modules:
  0.0 124.6 jit_solution(17517704996990153562)
XLA Ops:
  0.6 0.9 shard_map.104
  1.5 25.8 %all_to_all.25.own = bf16[8,2,128,128]{3,2,1,0:T(8,128)(2,1)S(1)} all-to-all(bf16[8,2,128,128]{3,2,1,0:T(8,128)(2,1)S(1)} %shard_map.104), channel_id=1, replica_groups=mesh['y'=4,'core'=2,'z'=8,'x'=4] {'z'}, dimensions={0} | all-to-all | bytes 1048576 | tf_op jit(solution)/shard_map/all_to_all | solution.py:470
  27.3 1.5 %collective-permute-start = (bf16[8,2,128,128]{3,2,1,0:T(8,128)(2,1)S(1)}, bf16[8,2,128,128]{3,2,1,0:T(8,128)(2,1)S(1)}, u32[]{:S(2)}, u32[]{:S(2)}) collective-permute-start(bf16[8,2,128,128]{3,2,1,0:T(8,128)(2,1)S(1)} %all_to_all.25.own), channel_id=1, source_target_pairs={{0,1},{1,2},{2,3},{3,0},{4,5},{5,6},{6,7},{7,4},{8,9},{9,10},{10,1... | collective-permute-start | bytes 1572872 | tf_op jit(solution)/shard_map/ppermute | solution.py:475
  28.7 1.7 %collective-permute-start.1 = (bf16[8,2,128,128]{3,2,1,0:T(8,128)(2,1)S(1)}, bf16[8,2,128,128]{3,2,1,0:T(8,128)(2,1)S(1)}, u32[]{:S(2)}, u32[]{:S(2)}) collective-permute-start(bf16[8,2,128,128]{3,2,1,0:T(8,128)(2,1)S(1)} %all_to_all.25.own), channel_id=1, source_target_pairs={{0,3},{1,0},{2,1},{3,2},{4,7},{5,4},{6,5},{7,6},{8,11},{9,8},{10,9... | collective-permute-start | bytes 1572872 | tf_op jit(solution)/shard_map/ppermute | solution.py:475
  30.5 0.0 copy-start
  30.5 0.8 copy-done
  31.3 9.2 %collective-permute-done.left.left_hbm = bf16[8,2,128,128]{3,2,1,0:T(8,128)(2,1)S(1)} collective-permute-done((bf16[8,2,128,128]{3,2,1,0:T(8,128)(2,1)S(1)}, bf16[8,2,128,128]{3,2,1,0:T(8,128)(2,1)S(1)}, u32[]{:S(2)}, u32[]{:S(2)}) %collective-permute-start) | collective-permute-done | bytes 524320 | tf_op jit(solution)/shard_map/ppermute | solution.py:475
  40.5 0.0 copy-start.2
  40.5 0.0 collective-permute-done.1.right.right_hbm
  40.5 0.8 copy-done.2
  41.3 0.0 copy-start.4
  41.3 0.8 copy-done.4
  42.1 1.9 %shard_map.107 = (bf16[4,2,128,128]{3,2,1,0:T(8,128)(2,1)}, bf16[4,2,128,128]{3,2,1,0:T(8,128)(2,1)}) custom-call(bf16[8,2,128,128]{3,2,1,0:T(8,128)(2,1)} %copy-done.2, bf16[8,2,128,128]{3,2,1,0:T(8,128)(2,1)} %copy-done.4), custom_call_target="tpu_custom_call" | custom-call | bytes 1572864 | tf_op jit(solution)/shard_map/pallas_call | solution.py:454
  43.9 0.8 collective-permute-start.2
  44.7 2.6 %collective-permute-start.3 = (bf16[4,2,128,128]{3,2,1,0:T(8,128)(2,1)}, bf16[4,2,128,128]{3,2,1,0:T(8,128)(2,1)}, u32[]{:S(2)}, u32[]{:S(2)}) collective-permute-start(bf16[4,2,128,128]{3,2,1,0:T(8,128)(2,1)} %get-tuple-element.23), channel_id=1, source_target_pairs={{0,3},{1,0},{2,1},{3,2},{4,7},{5,4},{6,5},{7,6},{8,11},{9,8},{10,9... | collective-permute-start | bytes 786440 | tf_op jit(solution)/shard_map/ppermute | solution.py:475
  47.2 0.0 copy-start.6
  47.3 0.9 copy-done.6
  48.2 0.7 shard_map.109
  48.9 4.9 %all-to-all-start.2 = ((f32[8,32,128]{2,1,0:T(8,128)}), f32[8,32,128]{2,1,0:T(8,128)S(1)}, u32[]{:S(2)}, u32[]{:S(2)}) async-start(f32[8,32,128]{2,1,0:T(8,128)} %shard_map.109), calls=%async_computation.2 | async-start | bytes 262144 | tf_op jit(solution)/shard_map/all_to_all | solution.py:470
  53.8 0.0 copy-start.1
  53.8 0.0 copy-start.3
  53.8 0.0 copy-start.5
  53.8 2.1 %shard_map.105.weight_ref.in_weight_ref = bf16[8,4,128,384]{3,2,1,0:T(8,128)(2,1)S(1)} custom-call(s32[1]{0:T(128)} %bitcast.place_ref, bf16[3,8,4,128,128]{4,3,2,1,0:T(8,128)(2,1)} %bitcast.5), custom_call_target="tpu_custom_call" | custom-call | bytes 6291460 | tf_op jit(solution)/shard_map/pallas_call | solution.py:454
  55.9 0.0 copy-done.1
  55.9 0.1 copy-done.3
  56.0 0.2 copy-done.5
  56.1 1.8 %shard_map.106 = (f32[128,384]{1,0:T(8,128)S(1)}, f32[128,128]{1,0:T(8,128)S(1)}, bf16[8,128,128]{2,1,0:T(8,128)(2,1)S(1)}) custom-call(s32[1]{0:T(128)} %bitcast.place_ref, bf16[128,4096]{1,0:T(8,128)(2,1)} %out_hbm.3, bf16[8,4,128,384]{3,2,1,0:T(8,128)(2,1)S(1)} %shard_map.105.weight_ref.in_weight_ref, bf16[8,2,128,128]{3,2,1,0:T(8,128)(2,1)S(1)} %copy-done.1, ...), custom_call_target="tpu_custom_call" | custom-call | flops 402653184 | bytes 6291460 | tf_op jit(solution)/shard_map/pallas_call | solution.py:454
  57.9 0.0 collective-permute-done.2.low
  57.9 0.0 collective-permute-done.3.high
  58.0 2.2 %shard_map.108 = f32[8,64,128]{2,1,0:T(8,128)} custom-call(bf16[8,4,128,384]{3,2,1,0:T(8,128)(2,1)S(1)} %shard_map.105.weight_ref.in_weight_ref, bf16[8,128,128]{2,1,0:T(8,128)(2,1)S(1)} %get-tuple-element.19.far_weight_ref, f32[128,384]{1,0:T(8,128)S(1)} %get-tuple-element.20.rows_ref, f32[128,128]{1,0:T(8,128)S(1)} %get-tuple-element.21.grads_ref, ...), custom_call_target="tpu_custom_call" | custom-call | flops 134217728 | bytes 4456448 | tf_op jit(solution)/shard_map/pallas_call | solution.py:454
  60.2 0.0 all-to-all-done.2.filter_ref
  60.2 4.8 %all-to-all-start.1 = ((f32[8,64,128]{2,1,0:T(8,128)}), f32[8,64,128]{2,1,0:T(8,128)S(1)}, u32[]{:S(2)}, u32[]{:S(2)}) async-start(f32[8,64,128]{2,1,0:T(8,128)} %shard_map.108), calls=%async_computation.1 | async-start | bytes 524288 | tf_op jit(solution)/shard_map/all_to_all | solution.py:470
  65.0 6.0 %all-to-all-done.1.given_ref = f32[8,64,128]{2,1,0:T(8,128)S(1)} async-done(((f32[8,64,128]{2,1,0:T(8,128)}), f32[8,64,128]{2,1,0:T(8,128)S(1)}, u32[]{:S(2)}, u32[]{:S(2)}) %all-to-all-start.1) | async-done | bytes 262176 | tf_op jit(solution)/shard_map/all_to_all | solution.py:470
  71.0 3.0 %shard_map.110 = bf16[8,64,128]{2,1,0:T(8,128)(2,1)S(1)} custom-call(s32[1]{0:T(128)} %bitcast.3.place_ref, bf16[2,2,128,128]{3,2,1,0:T(8,128)(2,1)} %constant.20.clone.table_hbm, f32[2,9,128]{2,1,0:T(8,128)} %constant.21.clone.twiddle_hbm, f32[3,3,128]{2,1,0:T(4,128)} %taps_hbm.1, f32[2,128]{1,0:T(2,128)} %gains_hbm.1, ...), custom_call_target="tpu_custom_call" | custom-call | bytes 670212 | tf_op jit(solution)/shard_map/pallas_call | solution.py:454
  74.0 8.5 %all_to_all.26.channels_ref = bf16[8,64,128]{2,1,0:T(8,128)(2,1)S(1)} all-to-all(bf16[8,64,128]{2,1,0:T(8,128)(2,1)S(1)} %shard_map.110), channel_id=1, replica_groups=mesh['y'=4,'core'=2,'z'=8,'x'=4] {'y','core'}, dimensions={0} | all-to-all | bytes 262144 | tf_op jit(solution)/shard_map/all_to_all | solution.py:470
  82.5 1.7 %shard_map.111 = (bf16[8,2,128,128]{3,2,1,0:T(8,128)(2,1)S(1)}, bf16[4,2,128,128]{3,2,1,0:T(8,128)(2,1)S(1)}, bf16[4,2,128,128]{3,2,1,0:T(8,128)(2,1)S(1)}, bf16...) custom-call(s32[1]{0:T(128)} %bitcast.place_ref, ...), custom_call_target="tpu_custom_call" | custom-call | flops 536870912 | bytes 6422532 | tf_op jit(solution)/shard_map/pallas_call | solution.py:454
  84.2 0.1 collective-permute-start.6
  84.3 3.2 %collective-permute-start.7 = (bf16[4,2,128,128]{3,2,1,0:T(8,128)(2,1)S(1)}, bf16[4,2,128,128]{3,2,1,0:T(8,128)(2,1)S(1)}, u32[]{:S(2)}, u32[]{:S(2)}) collective-permute-start(bf16[4,2,128,128]{3,2,1,0:T(8,128)(2,1)S(1)} %get-tuple-element.31), channel_id=1, source_target_pairs={{0,3},{1,0},{2,1},{3,2},{4,7},{5,4},{6,5},{7,6},{8,11},{9,8},{10,9... | collective-permute-start | bytes 786440 | tf_op jit(solution)/shard_map/ppermute | solution.py:475
  87.5 0.0 collective-permute-start.4
  87.5 3.2 %collective-permute-start.5 = (bf16[4,2,128,128]{3,2,1,0:T(8,128)(2,1)S(1)}, bf16[4,2,128,128]{3,2,1,0:T(8,128)(2,1)S(1)}, u32[]{:S(2)}, u32[]{:S(2)}) collective-permute-start(bf16[4,2,128,128]{3,2,1,0:T(8,128)(2,1)S(1)} %get-tuple-element.27), channel_id=1, source_target_pairs={{0,3},{1,0},{2,1},{3,2},{4,7},{5,4},{6,5},{7,6},{8,11},{9,8},{10,9... | collective-permute-start | bytes 786440 | tf_op jit(solution)/shard_map/ppermute | solution.py:475
  90.7 3.9 %collective-permute-done.6.from_l_ref = bf16[4,2,128,128]{3,2,1,0:T(8,128)(2,1)S(1)} collective-permute-done((bf16[4,2,128,128]{3,2,1,0:T(8,128)(2,1)S(1)}, bf16[4,2,128,128]{3,2,1,0:T(8,128)(2,1)S(1)}, u32[]{:S(2)}, u32[]{:S(2)}) %collective-permute-start.6) | collective-permute-done | bytes 262176 | tf_op jit(solution)/shard_map/ppermute | solution.py:475
  94.6 0.0 collective-permute-done.7.from_r_ref
  94.7 0.1 shard_map.112
  94.8 0.1 collective-permute-start.8
  94.9 3.3 %collective-permute-start.9 = (bf16[4,2,128,128]{3,2,1,0:T(8,128)(2,1)S(1)}, bf16[4,2,128,128]{3,2,1,0:T(8,128)(2,1)S(1)}, u32[]{:S(2)}, u32[]{:S(2)}) collective-permute-start(bf16[4,2,128,128]{3,2,1,0:T(8,128)(2,1)S(1)} %get-tuple-element.33), channel_id=1, source_target_pairs={{0,3},{1,0},{2,1},{3,2},{4,7},{5,4},{6,5},{7,6},{8,11},{9,8},{10,9... | collective-permute-start | bytes 786440 | tf_op jit(solution)/shard_map/ppermute | solution.py:475
  98.2 2.1 %collective-permute-done.4.near_l_ref = bf16[4,2,128,128]{3,2,1,0:T(8,128)(2,1)S(1)} collective-permute-done((bf16[4,2,128,128]{3,2,1,0:T(8,128)(2,1)S(1)}, bf16[4,2,128,128]{3,2,1,0:T(8,128)(2,1)S(1)}, u32[]{:S(2)}, u32[]{:S(2)}) %collective-permute-start.4) | collective-permute-done | bytes 262176 | tf_op jit(solution)/shard_map/ppermute | solution.py:475
  100.3 0.0 collective-permute-done.5.near_r_ref
  100.3 4.3 %collective-permute-done.8.last_l_ref = bf16[4,2,128,128]{3,2,1,0:T(8,128)(2,1)S(1)} collective-permute-done((bf16[4,2,128,128]{3,2,1,0:T(8,128)(2,1)S(1)}, bf16[4,2,128,128]{3,2,1,0:T(8,128)(2,1)S(1)}, u32[]{:S(2)}, u32[]{:S(2)}) %collective-permute-start.8) | collective-permute-done | bytes 262176 | tf_op jit(solution)/shard_map/ppermute | solution.py:475
  104.6 0.0 collective-permute-done.9.last_r_ref
  104.6 0.2 shard_map.113
  104.8 19.1 %all_to_all.27.parts_ref = bf16[8,2,128,128]{3,2,1,0:T(8,128)(2,1)S(1)} all-to-all(bf16[8,2,128,128]{3,2,1,0:T(8,128)(2,1)S(1)} %shard_map.113), channel_id=1, replica_groups=mesh['y'=4,'core'=2,'z'=8,'x'=4] {'z'}, dimensions={0} | all-to-all | bytes 1048576 | tf_op jit(solution)/shard_map/all_to_all | solution.py:470
  123.9 0.7 shard_map.114
Async XLA Ops:
  27.3 13.2 %collective-permute-start = (bf16[8,2,128,128]{3,2,1,0:T(8,128)(2,1)S(1)}, bf16[8,2,128,128]{3,2,1,0:T(8,128)(2,1)S(1)}, u32[]{:S(2)}, u32[]{:S(2)}) collective-permute-start(bf16[8,2,128,128]{3,2,1,0:T(8,128)(2,1)S(1)} %all_to_all.25.own), channel_id=1, source_target_pairs={{0,1},{1,2},{2,3},{3,0},{4,5},{5,6},{6,7},{7,4},{8,9},{9,10},{10,1... | collective-permute-start | bytes 1572872 | tf_op jit(solution)/shard_map/ppermute | solution.py:475
  28.7 11.7 %collective-permute-start.1 = (bf16[8,2,128,128]{3,2,1,0:T(8,128)(2,1)S(1)}, bf16[8,2,128,128]{3,2,1,0:T(8,128)(2,1)S(1)}, u32[]{:S(2)}, u32[]{:S(2)}) collective-permute-start(bf16[8,2,128,128]{3,2,1,0:T(8,128)(2,1)S(1)} %all_to_all.25.own), channel_id=1, source_target_pairs={{0,3},{1,0},{2,1},{3,2},{4,7},{5,4},{6,5},{7,6},{8,11},{9,8},{10,9... | collective-permute-start | bytes 1572872 | tf_op jit(solution)/shard_map/ppermute | solution.py:475
  30.5 0.8 copy-start
  40.5 0.8 copy-start.2
  41.3 0.8 copy-start.4
  43.9 14.0 %collective-permute-start.2 = (bf16[4,2,128,128]{3,2,1,0:T(8,128)(2,1)}, bf16[4,2,128,128]{3,2,1,0:T(8,128)(2,1)S(1)}, u32[]{:S(2)}, u32[]{:S(2)}) collective-permute-start(bf16[4,2,128,128]{3,2,1,0:T(8,128)(2,1)} %get-tuple-element.22), channel_id=1, source_target_pairs={{0,1},{1,2},{2,3},{3,0},{4,5},{5,6},{6,7},{7,4},{8,9},{9,10},{10,1... | collective-permute-start | bytes 786440 | tf_op jit(solution)/shard_map/ppermute | solution.py:475
  44.7 13.2 %collective-permute-start.3 = (bf16[4,2,128,128]{3,2,1,0:T(8,128)(2,1)}, bf16[4,2,128,128]{3,2,1,0:T(8,128)(2,1)}, u32[]{:S(2)}, u32[]{:S(2)}) collective-permute-start(bf16[4,2,128,128]{3,2,1,0:T(8,128)(2,1)} %get-tuple-element.23), channel_id=1, source_target_pairs={{0,3},{1,0},{2,1},{3,2},{4,7},{5,4},{6,5},{7,6},{8,11},{9,8},{10,9... | collective-permute-start | bytes 786440 | tf_op jit(solution)/shard_map/ppermute | solution.py:475
  47.2 0.9 copy-start.6
  48.9 11.3 %all-to-all-start.2 = ((f32[8,32,128]{2,1,0:T(8,128)}), f32[8,32,128]{2,1,0:T(8,128)S(1)}, u32[]{:S(2)}, u32[]{:S(2)}) async-start(f32[8,32,128]{2,1,0:T(8,128)} %shard_map.109), calls=%async_computation.2 | async-start | bytes 262144 | tf_op jit(solution)/shard_map/all_to_all | solution.py:470
  53.8 2.1 %copy-start.1 = (bf16[8,2,128,128]{3,2,1,0:T(8,128)(2,1)S(1)}, bf16[8,2,128,128]{3,2,1,0:T(8,128)(2,1)}, u32[]{:S(2)}) copy-start(bf16[8,2,128,128]{3,2,1,0:T(8,128)(2,1)} %copy-done) | copy-start | bytes 1572868
  53.8 2.1 %copy-start.3 = (bf16[8,2,128,128]{3,2,1,0:T(8,128)(2,1)S(1)}, bf16[8,2,128,128]{3,2,1,0:T(8,128)(2,1)}, u32[]{:S(2)}) copy-start(bf16[8,2,128,128]{3,2,1,0:T(8,128)(2,1)} %copy-done.2) | copy-start | bytes 1572868
  53.8 2.3 %copy-start.5 = (bf16[8,2,128,128]{3,2,1,0:T(8,128)(2,1)S(1)}, bf16[8,2,128,128]{3,2,1,0:T(8,128)(2,1)}, u32[]{:S(2)}) copy-start(bf16[8,2,128,128]{3,2,1,0:T(8,128)(2,1)} %copy-done.4) | copy-start | bytes 1572868
  60.2 10.9 %all-to-all-start.1 = ((f32[8,64,128]{2,1,0:T(8,128)}), f32[8,64,128]{2,1,0:T(8,128)S(1)}, u32[]{:S(2)}, u32[]{:S(2)}) async-start(f32[8,64,128]{2,1,0:T(8,128)} %shard_map.108), calls=%async_computation.1 | async-start | bytes 524288 | tf_op jit(solution)/shard_map/all_to_all | solution.py:470
  84.2 10.5 %collective-permute-start.6 = (bf16[4,2,128,128]{3,2,1,0:T(8,128)(2,1)S(1)}, bf16[4,2,128,128]{3,2,1,0:T(8,128)(2,1)S(1)}, u32[]{:S(2)}, u32[]{:S(2)}) collective-permute-start(bf16[4,2,128,128]{3,2,1,0:T(8,128)(2,1)S(1)} %get-tuple-element.30), channel_id=1, source_target_pairs={{0,1},{1,2},{2,3},{3,0},{4,5},{5,6},{6,7},{7,4},{8,9},{9,10},{10,1... | collective-permute-start | bytes 786440 | tf_op jit(solution)/shard_map/ppermute | solution.py:475
  84.3 10.4 %collective-permute-start.7 = (bf16[4,2,128,128]{3,2,1,0:T(8,128)(2,1)S(1)}, bf16[4,2,128,128]{3,2,1,0:T(8,128)(2,1)S(1)}, u32[]{:S(2)}, u32[]{:S(2)}) collective-permute-start(bf16[4,2,128,128]{3,2,1,0:T(8,128)(2,1)S(1)} %get-tuple-element.31), channel_id=1, source_target_pairs={{0,3},{1,0},{2,1},{3,2},{4,7},{5,4},{6,5},{7,6},{8,11},{9,8},{10,9... | collective-permute-start | bytes 786440 | tf_op jit(solution)/shard_map/ppermute | solution.py:475
  87.5 12.8 %collective-permute-start.4 = (bf16[4,2,128,128]{3,2,1,0:T(8,128)(2,1)S(1)}, bf16[4,2,128,128]{3,2,1,0:T(8,128)(2,1)S(1)}, u32[]{:S(2)}, u32[]{:S(2)}) collective-permute-start(bf16[4,2,128,128]{3,2,1,0:T(8,128)(2,1)S(1)} %get-tuple-element.26), channel_id=1, source_target_pairs={{0,1},{1,2},{2,3},{3,0},{4,5},{5,6},{6,7},{7,4},{8,9},{9,10},{10,1... | collective-permute-start | bytes 786440 | tf_op jit(solution)/shard_map/ppermute | solution.py:475
  87.5 12.8 %collective-permute-start.5 = (bf16[4,2,128,128]{3,2,1,0:T(8,128)(2,1)S(1)}, bf16[4,2,128,128]{3,2,1,0:T(8,128)(2,1)S(1)}, u32[]{:S(2)}, u32[]{:S(2)}) collective-permute-start(bf16[4,2,128,128]{3,2,1,0:T(8,128)(2,1)S(1)} %get-tuple-element.27), channel_id=1, source_target_pairs={{0,3},{1,0},{2,1},{3,2},{4,7},{5,4},{6,5},{7,6},{8,11},{9,8},{10,9... | collective-permute-start | bytes 786440 | tf_op jit(solution)/shard_map/ppermute | solution.py:475
  94.8 9.8 %collective-permute-start.8 = (bf16[4,2,128,128]{3,2,1,0:T(8,128)(2,1)S(1)}, bf16[4,2,128,128]{3,2,1,0:T(8,128)(2,1)S(1)}, u32[]{:S(2)}, u32[]{:S(2)}) collective-permute-start(bf16[4,2,128,128]{3,2,1,0:T(8,128)(2,1)S(1)} %get-tuple-element.32), channel_id=1, source_target_pairs={{0,1},{1,2},{2,3},{3,0},{4,5},{5,6},{6,7},{7,4},{8,9},{9,10},{10,1... | collective-permute-start | bytes 786440 | tf_op jit(solution)/shard_map/ppermute | solution.py:475
  94.9 9.7 %collective-permute-start.9 = (bf16[4,2,128,128]{3,2,1,0:T(8,128)(2,1)S(1)}, bf16[4,2,128,128]{3,2,1,0:T(8,128)(2,1)S(1)}, u32[]{:S(2)}, u32[]{:S(2)}) collective-permute-start(bf16[4,2,128,128]{3,2,1,0:T(8,128)(2,1)S(1)} %get-tuple-element.33), channel_id=1, source_target_pairs={{0,3},{1,0},{2,1},{3,2},{4,7},{5,4},{6,5},{7,6},{8,11},{9,8},{10,9... | collective-permute-start | bytes 786440 | tf_op jit(solution)/shard_map/ppermute | solution.py:475

commit v5 on v4

--- a/solution.py
+++ b/solution.py
@@ -352,14 +352,50 @@
     store(3, grads)
 
 
+def far_partial_kernel(
+    place_ref,
+    out_hbm,
+    in_weight_ref,
+    channels_ref,
+    far_r_ref,
+    far_l_ref,
+    out_weight_ref,
+    sems,
+):
+    half, _, feats, tokens = far_r_ref.shape
+    n_z = 2 * half
+    ring = in_weight_ref.shape[1]
+    (weight_copy,) = started([out_hbm], [out_weight_ref], sems)
+    count = channels_ref.shape[1] // 4
+    second, *grads = [
+        channels_ref[:, slot * count : (slot + 1) * count].reshape((BLOCKS * count, tokens))
+        for slot in range(4)
+    ]
+    second = second.astype(F32).T.astype(BF16)
+    grads = jnp.concatenate(grads, axis=0)
+    wide = out_weight_ref.shape[1] // n_z
+
+    def mixed(z):
+        columns_of = ring_columns(place_ref, out_weight_ref, ring, feats, z)
+        return jnp.dot(second, columns_of[:, wide - feats :], preferred_element_type=F32)
+
+    def token_grad(z):
+        return jnp.dot(in_weight_ref[z, ring - 1], grads, preferred_element_type=F32)
+
+    for output, product in ((1, token_grad), (0, mixed)):
+        if output == 0:
+            weight_copy.wait()
+        for z in range(n_z):
+            far_ref = far_r_ref.at[z] if z < half else far_l_ref.at[z - half]
+            far_ref[output] = product(z).astype(BF16)
+
+
 def partial_kernel(
     place_ref,
     out_hbm,
     in_weight_ref,
     channels_ref,
     own_ref,
-    far_r_ref,
-    far_l_ref,
     near_r_ref,
     near_l_ref,
     keep_r_ref,
@@ -399,15 +435,13 @@
         if output == 0:
             weight_copy.wait()
         for z in range(n_z):
-            own, ahead, behind, far = pieces(z)
+            own, ahead, behind, _ = pieces(z)
             own_ref[z, output] = own
             if z < half:
-                far_r_ref[z, output] = far
                 keep_r_ref[z, output] = ahead
                 near_l_ref[z, output] = behind
             else:
                 near_r_ref[z - half, output] = ahead
-                far_l_ref[z - half, output] = far
                 keep_l_ref[z - half, output] = behind
 
 
@@ -562,17 +596,28 @@
         ],
     )
     whole, part = (n_z, 2, LANES, rows), (half, 2, LANES, rows)
-    own, far_r, far_l, near_r, near_l, keep_r, keep_l = run(
-        partial_kernel,
-        tuple(shape_of(shape, BF16) for shape in (whole, *[part] * 6)),
+    channels = exchanged(channels, SEQ)
+    far_r, far_l = run(
+        far_partial_kernel,
+        (shape_of(part, BF16),) * 2,
         in_turned,
-        exchanged(channels, SEQ),
-        flops=2 * rows * width * 4 * chans,
+        channels,
+        flops=rows * width * 2 * chans,
         place=place,
         far=(out_weight,),
         scratch=out_scratch,
     )
     from_l, from_r = shifted(far_r, 1), shifted(far_l, -1)
+    own, near_r, near_l, keep_r, keep_l = run(
+        partial_kernel,
+        tuple(shape_of(shape, BF16) for shape in (whole, *[part] * 4)),
+        in_turned,
+        channels,
+        flops=rows * width * 6 * chans,
+        place=place,
+        far=(out_weight,),
+        scratch=out_scratch,
+    )
     near_l = shifted(near_l, -1)
     near_r = shifted(near_r, 1)
     to_right, to_left = run(

time: 126 us -> 127 us (level)
  Pallas kernels: 15.2 us -> 16.9 us
  waiting for transfers between devices: 25.5 us -> 23.9 us
    pallas_call x11 -> x12, Pallas kernels: 15.2 us -> 16.9 us  [run(): pl.pallas_call(kernel, out_shape=out_shape, in_specs=specs, out_specs=in_...]
    ppermute x10, waiting for transfers between devices: 19.5 us -> 17.8 us  [shifted(): lax.ppermute(value, 'x', [(at, (at + steps) % ring) for at in range(ring)])]
  transfers between devices with their start and end apart: 12 -> 12, of which waited for: 5 -> 5; matrix products, arithmetic and copies ran while one was open for 0% -> 0% of each run, Pallas kernels for 6% -> 7%
where the time goes in v5:
time: 127 us; the launch traced here: 125 us
  blocking collectives  53.5 us (42%)
  starting transfers between devices  26.2 us (21%)
  waiting for transfers between devices  23.9 us (19%)
  Pallas kernels  16.9 us (13%)
  local copies, waits for them, and re-layouts  3.54 us (3%)
    all_to_all x3, blocking collectives, exchanged(): return lax.all_to_all(value, axis, 0, 0, tiled=True)  53.5 us
    ppermute x10, waiting for transfers between devices, shifted(): lax.ppermute(value, 'x', [(at, (at + steps) % ring) for at in range(ring)])  17.8 us
    pallas_call x12, Pallas kernels, run(): pl.pallas_call(kernel, out_shape=out_shape, in_specs=specs, out_specs=in_...  16.9 us
    ppermute x10, starting transfers between devices, shifted(): lax.ppermute(value, 'x', [(at, (at + steps) % ring) for at in range(ring)])  16.5 us
    all_to_all x2, starting transfers between devices, exchanged(): return lax.all_to_all(value, axis, 0, 0, tiled=True)  9.71 us
    all_to_all x2, waiting for transfers between devices, exchanged(): return lax.all_to_all(value, axis, 0, 0, tiled=True)  6.05 us
    unnamed x14, local copies, waits for them, and re-layouts  3.54 us
  transfers between devices with their start and end apart: 12, of which 5 were waited for; matrix products, arithmetic and copies ran while one was open for 0% of the time, Pallas kernels for 7%

profile of v5, /device:TPU:8, one launch (start us, length us, event | category | flops | bytes accessed | tf_op | source)
XLA Modules:
  0.0 124.8 jit_solution(7548572291633996765)
XLA Ops:
  0.6 0.9 shard_map.104
  1.5 25.8 %all_to_all.25.own = bf16[8,2,128,128]{3,2,1,0:T(8,128)(2,1)S(1)} all-to-all(bf16[8,2,128,128]{3,2,1,0:T(8,128)(2,1)S(1)} %shard_map.104), channel_id=1, replica_groups=mesh['y'=4,'core'=2,'z'=8,'x'=4] {'z'}, dimensions={0} | all-to-all | bytes 1048576 | tf_op jit(solution)/shard_map/all_to_all | solution.py:504
  27.3 1.5 %collective-permute-start = (bf16[8,2,128,128]{3,2,1,0:T(8,128)(2,1)S(1)}, bf16[8,2,128,128]{3,2,1,0:T(8,128)(2,1)S(1)}, u32[]{:S(2)}, u32[]{:S(2)}) collective-permute-start(bf16[8,2,128,128]{3,2,1,0:T(8,128)(2,1)S(1)} %all_to_all.25.own), channel_id=1, source_target_pairs={{0,1},{1,2},{2,3},{3,0},{4,5},{5,6},{6,7},{7,4},{8,9},{9,10},{10,1... | collective-permute-start | bytes 1572872 | tf_op jit(solution)/shard_map/ppermute | solution.py:509
  28.7 1.7 %collective-permute-start.1 = (bf16[8,2,128,128]{3,2,1,0:T(8,128)(2,1)S(1)}, bf16[8,2,128,128]{3,2,1,0:T(8,128)(2,1)S(1)}, u32[]{:S(2)}, u32[]{:S(2)}) collective-permute-start(bf16[8,2,128,128]{3,2,1,0:T(8,128)(2,1)S(1)} %all_to_all.25.own), channel_id=1, source_target_pairs={{0,3},{1,0},{2,1},{3,2},{4,7},{5,4},{6,5},{7,6},{8,11},{9,8},{10,9... | collective-permute-start | bytes 1572872 | tf_op jit(solution)/shard_map/ppermute | solution.py:509
  30.5 0.0 copy-start
  30.5 0.8 copy-done
  31.3 9.2 %collective-permute-done.left.left_hbm = bf16[8,2,128,128]{3,2,1,0:T(8,128)(2,1)S(1)} collective-permute-done((bf16[8,2,128,128]{3,2,1,0:T(8,128)(2,1)S(1)}, bf16[8,2,128,128]{3,2,1,0:T(8,128)(2,1)S(1)}, u32[]{:S(2)}, u32[]{:S(2)}) %collective-permute-start) | collective-permute-done | bytes 524320 | tf_op jit(solution)/shard_map/ppermute | solution.py:509
  40.5 0.0 copy-start.2
  40.5 0.0 collective-permute-done.1.right.right_hbm
  40.5 0.8 copy-done.2
  41.3 0.0 copy-start.4
  41.3 0.8 copy-done.4
  42.1 1.9 %shard_map.107 = (bf16[4,2,128,128]{3,2,1,0:T(8,128)(2,1)}, bf16[4,2,128,128]{3,2,1,0:T(8,128)(2,1)}) custom-call(bf16[8,2,128,128]{3,2,1,0:T(8,128)(2,1)} %copy-done.2, bf16[8,2,128,128]{3,2,1,0:T(8,128)(2,1)} %copy-done.4), custom_call_target="tpu_custom_call" | custom-call | bytes 1572864 | tf_op jit(solution)/shard_map/pallas_call | solution.py:488
  43.9 0.8 collective-permute-start.2
  44.7 2.5 %collective-permute-start.3 = (bf16[4,2,128,128]{3,2,1,0:T(8,128)(2,1)}, bf16[4,2,128,128]{3,2,1,0:T(8,128)(2,1)}, u32[]{:S(2)}, u32[]{:S(2)}) collective-permute-start(bf16[4,2,128,128]{3,2,1,0:T(8,128)(2,1)} %get-tuple-element.23), channel_id=1, source_target_pairs={{0,3},{1,0},{2,1},{3,2},{4,7},{5,4},{6,5},{7,6},{8,11},{9,8},{10,9... | collective-permute-start | bytes 786440 | tf_op jit(solution)/shard_map/ppermute | solution.py:509
  47.2 0.0 copy-start.6
  47.3 0.9 copy-done.6
  48.2 0.8 shard_map.109
  48.9 4.9 %all-to-all-start.2 = ((f32[8,32,128]{2,1,0:T(8,128)}), f32[8,32,128]{2,1,0:T(8,128)S(1)}, u32[]{:S(2)}, u32[]{:S(2)}) async-start(f32[8,32,128]{2,1,0:T(8,128)} %shard_map.109), calls=%async_computation.2 | async-start | bytes 262144 | tf_op jit(solution)/shard_map/all_to_all | solution.py:504
  53.8 0.0 copy-start.1
  53.8 0.0 copy-start.3
  53.8 0.0 copy-start.5
  53.8 2.1 %shard_map.105.weight_ref.in_weight_ref = bf16[8,4,128,384]{3,2,1,0:T(8,128)(2,1)S(1)} custom-call(s32[1]{0:T(128)} %bitcast.place_ref, bf16[3,8,4,128,128]{4,3,2,1,0:T(8,128)(2,1)} %bitcast.5), custom_call_target="tpu_custom_call" | custom-call | bytes 6291460 | tf_op jit(solution)/shard_map/pallas_call | solution.py:488
  55.9 0.0 copy-done.1
  55.9 0.1 copy-done.3
  56.0 0.2 copy-done.5
  56.1 1.8 %shard_map.106 = (f32[128,384]{1,0:T(8,128)S(1)}, f32[128,128]{1,0:T(8,128)S(1)}, bf16[8,128,128]{2,1,0:T(8,128)(2,1)S(1)}) custom-call(s32[1]{0:T(128)} %bitcast.place_ref, bf16[128,4096]{1,0:T(8,128)(2,1)} %out_hbm.5, bf16[8,4,128,384]{3,2,1,0:T(8,128)(2,1)S(1)} %shard_map.105.weight_ref.in_weight_ref, bf16[8,2,128,128]{3,2,1,0:T(8,128)(2,1)S(1)} %copy-done.1, ...), custom_call_target="tpu_custom_call" | custom-call | flops 402653184 | bytes 6291460 | tf_op jit(solution)/shard_map/pallas_call | solution.py:488
  57.9 0.0 collective-permute-done.2.low
  58.0 0.0 collective-permute-done.3.high
  58.0 2.2 %shard_map.108 = f32[8,64,128]{2,1,0:T(8,128)} custom-call(bf16[8,4,128,384]{3,2,1,0:T(8,128)(2,1)S(1)} %shard_map.105.weight_ref.in_weight_ref, bf16[8,128,128]{2,1,0:T(8,128)(2,1)S(1)} %get-tuple-element.19.far_weight_ref, f32[128,384]{1,0:T(8,128)S(1)} %get-tuple-element.20.rows_ref, f32[128,128]{1,0:T(8,128)S(1)} %get-tuple-element.21.grads_ref, ...), custom_call_target="tpu_custom_call" | custom-call | flops 134217728 | bytes 4456448 | tf_op jit(solution)/shard_map/pallas_call | solution.py:488
  60.2 0.0 all-to-all-done.2.filter_ref
  60.2 4.8 %all-to-all-start.1 = ((f32[8,64,128]{2,1,0:T(8,128)}), f32[8,64,128]{2,1,0:T(8,128)S(1)}, u32[]{:S(2)}, u32[]{:S(2)}) async-start(f32[8,64,128]{2,1,0:T(8,128)} %shard_map.108), calls=%async_computation.1 | async-start | bytes 524288 | tf_op jit(solution)/shard_map/all_to_all | solution.py:504
  65.0 6.0 %all-to-all-done.1.given_ref = f32[8,64,128]{2,1,0:T(8,128)S(1)} async-done(((f32[8,64,128]{2,1,0:T(8,128)}), f32[8,64,128]{2,1,0:T(8,128)S(1)}, u32[]{:S(2)}, u32[]{:S(2)}) %all-to-all-start.1) | async-done | bytes 262176 | tf_op jit(solution)/shard_map/all_to_all | solution.py:504
  71.0 3.0 %shard_map.110 = bf16[8,64,128]{2,1,0:T(8,128)(2,1)S(1)} custom-call(s32[1]{0:T(128)} %bitcast.3.place_ref, bf16[2,2,128,128]{3,2,1,0:T(8,128)(2,1)} %constant.20.clone.table_hbm, f32[2,9,128]{2,1,0:T(8,128)} %constant.21.clone.twiddle_hbm, f32[3,3,128]{2,1,0:T(4,128)} %taps_hbm.1, f32[2,128]{1,0:T(2,128)} %gains_hbm.1, ...), custom_call_target="tpu_custom_call" | custom-call | bytes 670212 | tf_op jit(solution)/shard_map/pallas_call | solution.py:488
  74.0 8.5 %all_to_all.26.channels_ref = bf16[8,64,128]{2,1,0:T(8,128)(2,1)S(1)} all-to-all(bf16[8,64,128]{2,1,0:T(8,128)(2,1)S(1)} %shard_map.110), channel_id=1, replica_groups=mesh['y'=4,'core'=2,'z'=8,'x'=4] {'y','core'}, dimensions={0} | all-to-all | bytes 262144 | tf_op jit(solution)/shard_map/all_to_all | solution.py:504
  82.5 1.7 %shard_map.112 = (bf16[4,2,128,128]{3,2,1,0:T(8,128)(2,1)S(1)}, bf16[4,2,128,128]{3,2,1,0:T(8,128)(2,1)S(1)}) custom-call(s32[1]{0:T(128)} %bitcast.place_ref, bf16[128,4096]{1,0:T(8,128)(2,1)} %out_hbm.5, bf16[8,4,128,384]{3,2,1,0:T(8,128)(2,1)S(1)} %shard_map.105.weight_ref.in_weight_ref, bf16[8,64,128]{2,1,0:T(8,128)(2,1)S(1)} %all_to_all.26.channels_ref), custom_call_target="tpu_custom_call" | custom-call | flops 134217728 | bytes 4849668 | tf_op jit(solution)/shard_map/pallas_call | solution.py:488
  84.2 0.1 collective-permute-start.6
  84.3 3.2 %collective-permute-start.7 = (bf16[4,2,128,128]{3,2,1,0:T(8,128)(2,1)S(1)}, bf16[4,2,128,128]{3,2,1,0:T(8,128)(2,1)S(1)}, u32[]{:S(2)}, u32[]{:S(2)}) collective-permute-start(bf16[4,2,128,128]{3,2,1,0:T(8,128)(2,1)S(1)} %get-tuple-element.31), channel_id=1, source_target_pairs={{0,3},{1,0},{2,1},{3,2},{4,7},{5,4},{6,5},{7,6},{8,11},{9,8},{10,9... | collective-permute-start | bytes 786440 | tf_op jit(solution)/shard_map/ppermute | solution.py:509
  87.5 1.7 %shard_map.111 = (bf16[8,2,128,128]{3,2,1,0:T(8,128)(2,1)S(1)}, bf16[4,2,128,128]{3,2,1,0:T(8,128)(2,1)S(1)}, bf16[4,2,128,128]{3,2,1,0:T(8,128)(2,1)S(1)}, bf16...) custom-call(s32[1]{0:T(128)} %bitcast.place_ref, bf16[128,4096]{1,0:T(8,128)(2,1)} %out_hbm.5, ...), custom_call_target="tpu_custom_call" | custom-call | flops 402653184 | bytes 5898244 | tf_op jit(solution)/shard_map/pallas_call | solution.py:488
  89.2 0.1 collective-permute-start.4
  89.3 3.2 %collective-permute-start.5 = (bf16[4,2,128,128]{3,2,1,0:T(8,128)(2,1)S(1)}, bf16[4,2,128,128]{3,2,1,0:T(8,128)(2,1)S(1)}, u32[]{:S(2)}, u32[]{:S(2)}) collective-permute-start(bf16[4,2,128,128]{3,2,1,0:T(8,128)(2,1)S(1)} %get-tuple-element.27), channel_id=1, source_target_pairs={{0,3},{1,0},{2,1},{3,2},{4,7},{5,4},{6,5},{7,6},{8,11},{9,8},{10,9... | collective-permute-start | bytes 786440 | tf_op jit(solution)/shard_map/ppermute | solution.py:509
  92.5 2.0 %collective-permute-done.6.from_l_ref = bf16[4,2,128,128]{3,2,1,0:T(8,128)(2,1)S(1)} collective-permute-done((bf16[4,2,128,128]{3,2,1,0:T(8,128)(2,1)S(1)}, bf16[4,2,128,128]{3,2,1,0:T(8,128)(2,1)S(1)}, u32[]{:S(2)}, u32[]{:S(2)}) %collective-permute-start.6) | collective-permute-done | bytes 262176 | tf_op jit(solution)/shard_map/ppermute | solution.py:509
  94.5 0.0 collective-permute-done.7.from_r_ref
  94.5 0.1 shard_map.113
  94.7 0.1 collective-permute-start.8
  94.8 3.2 %collective-permute-start.9 = (bf16[4,2,128,128]{3,2,1,0:T(8,128)(2,1)S(1)}, bf16[4,2,128,128]{3,2,1,0:T(8,128)(2,1)S(1)}, u32[]{:S(2)}, u32[]{:S(2)}) collective-permute-start(bf16[4,2,128,128]{3,2,1,0:T(8,128)(2,1)S(1)} %get-tuple-element.33), channel_id=1, source_target_pairs={{0,3},{1,0},{2,1},{3,2},{4,7},{5,4},{6,5},{7,6},{8,11},{9,8},{10,9... | collective-permute-start | bytes 786440 | tf_op jit(solution)/shard_map/ppermute | solution.py:509
  98.0 2.2 %collective-permute-done.4.near_l_ref = bf16[4,2,128,128]{3,2,1,0:T(8,128)(2,1)S(1)} collective-permute-done((bf16[4,2,128,128]{3,2,1,0:T(8,128)(2,1)S(1)}, bf16[4,2,128,128]{3,2,1,0:T(8,128)(2,1)S(1)}, u32[]{:S(2)}, u32[]{:S(2)}) %collective-permute-start.4) | collective-permute-done | bytes 262176 | tf_op jit(solution)/shard_map/ppermute | solution.py:509
  100.2 0.0 collective-permute-done.5.near_r_ref
  100.2 4.4 %collective-permute-done.8.last_l_ref = bf16[4,2,128,128]{3,2,1,0:T(8,128)(2,1)S(1)} collective-permute-done((bf16[4,2,128,128]{3,2,1,0:T(8,128)(2,1)S(1)}, bf16[4,2,128,128]{3,2,1,0:T(8,128)(2,1)S(1)}, u32[]{:S(2)}, u32[]{:S(2)}) %collective-permute-start.8) | collective-permute-done | bytes 262176 | tf_op jit(solution)/shard_map/ppermute | solution.py:509
  104.6 0.0 collective-permute-done.9.last_r_ref
  104.6 0.2 shard_map.114
  104.8 19.3 %all_to_all.27.parts_ref = bf16[8,2,128,128]{3,2,1,0:T(8,128)(2,1)S(1)} all-to-all(bf16[8,2,128,128]{3,2,1,0:T(8,128)(2,1)S(1)} %shard_map.114), channel_id=1, replica_groups=mesh['y'=4,'core'=2,'z'=8,'x'=4] {'z'}, dimensions={0} | all-to-all | bytes 1048576 | tf_op jit(solution)/shard_map/all_to_all | solution.py:504
  124.1 0.7 shard_map.115
Async XLA Ops:
  27.3 13.2 %collective-permute-start = (bf16[8,2,128,128]{3,2,1,0:T(8,128)(2,1)S(1)}, bf16[8,2,128,128]{3,2,1,0:T(8,128)(2,1)S(1)}, u32[]{:S(2)}, u32[]{:S(2)}) collective-permute-start(bf16[8,2,128,128]{3,2,1,0:T(8,128)(2,1)S(1)} %all_to_all.25.own), channel_id=1, source_target_pairs={{0,1},{1,2},{2,3},{3,0},{4,5},{5,6},{6,7},{7,4},{8,9},{9,10},{10,1... | collective-permute-start | bytes 1572872 | tf_op jit(solution)/shard_map/ppermute | solution.py:509
  28.7 11.7 %collective-permute-start.1 = (bf16[8,2,128,128]{3,2,1,0:T(8,128)(2,1)S(1)}, bf16[8,2,128,128]{3,2,1,0:T(8,128)(2,1)S(1)}, u32[]{:S(2)}, u32[]{:S(2)}) collective-permute-start(bf16[8,2,128,128]{3,2,1,0:T(8,128)(2,1)S(1)} %all_to_all.25.own), channel_id=1, source_target_pairs={{0,3},{1,0},{2,1},{3,2},{4,7},{5,4},{6,5},{7,6},{8,11},{9,8},{10,9... | collective-permute-start | bytes 1572872 | tf_op jit(solution)/shard_map/ppermute | solution.py:509
  30.5 0.8 copy-start
  40.5 0.8 copy-start.2
  41.3 0.8 copy-start.4
  43.9 14.0 %collective-permute-start.2 = (bf16[4,2,128,128]{3,2,1,0:T(8,128)(2,1)}, bf16[4,2,128,128]{3,2,1,0:T(8,128)(2,1)S(1)}, u32[]{:S(2)}, u32[]{:S(2)}) collective-permute-start(bf16[4,2,128,128]{3,2,1,0:T(8,128)(2,1)} %get-tuple-element.22), channel_id=1, source_target_pairs={{0,1},{1,2},{2,3},{3,0},{4,5},{5,6},{6,7},{7,4},{8,9},{9,10},{10,1... | collective-permute-start | bytes 786440 | tf_op jit(solution)/shard_map/ppermute | solution.py:509
  44.7 13.2 %collective-permute-start.3 = (bf16[4,2,128,128]{3,2,1,0:T(8,128)(2,1)}, bf16[4,2,128,128]{3,2,1,0:T(8,128)(2,1)}, u32[]{:S(2)}, u32[]{:S(2)}) collective-permute-start(bf16[4,2,128,128]{3,2,1,0:T(8,128)(2,1)} %get-tuple-element.23), channel_id=1, source_target_pairs={{0,3},{1,0},{2,1},{3,2},{4,7},{5,4},{6,5},{7,6},{8,11},{9,8},{10,9... | collective-permute-start | bytes 786440 | tf_op jit(solution)/shard_map/ppermute | solution.py:509
  47.2 0.9 copy-start.6
  48.9 11.3 %all-to-all-start.2 = ((f32[8,32,128]{2,1,0:T(8,128)}), f32[8,32,128]{2,1,0:T(8,128)S(1)}, u32[]{:S(2)}, u32[]{:S(2)}) async-start(f32[8,32,128]{2,1,0:T(8,128)} %shard_map.109), calls=%async_computation.2 | async-start | bytes 262144 | tf_op jit(solution)/shard_map/all_to_all | solution.py:504
  53.8 2.1 %copy-start.1 = (bf16[8,2,128,128]{3,2,1,0:T(8,128)(2,1)S(1)}, bf16[8,2,128,128]{3,2,1,0:T(8,128)(2,1)}, u32[]{:S(2)}) copy-start(bf16[8,2,128,128]{3,2,1,0:T(8,128)(2,1)} %copy-done) | copy-start | bytes 1572868
  53.8 2.1 %copy-start.3 = (bf16[8,2,128,128]{3,2,1,0:T(8,128)(2,1)S(1)}, bf16[8,2,128,128]{3,2,1,0:T(8,128)(2,1)}, u32[]{:S(2)}) copy-start(bf16[8,2,128,128]{3,2,1,0:T(8,128)(2,1)} %copy-done.2) | copy-start | bytes 1572868
  53.8 2.3 %copy-start.5 = (bf16[8,2,128,128]{3,2,1,0:T(8,128)(2,1)S(1)}, bf16[8,2,128,128]{3,2,1,0:T(8,128)(2,1)}, u32[]{:S(2)}) copy-start(bf16[8,2,128,128]{3,2,1,0:T(8,128)(2,1)} %copy-done.4) | copy-start | bytes 1572868
  60.2 10.8 %all-to-all-start.1 = ((f32[8,64,128]{2,1,0:T(8,128)}), f32[8,64,128]{2,1,0:T(8,128)S(1)}, u32[]{:S(2)}, u32[]{:S(2)}) async-start(f32[8,64,128]{2,1,0:T(8,128)} %shard_map.108), calls=%async_computation.1 | async-start | bytes 524288 | tf_op jit(solution)/shard_map/all_to_all | solution.py:504
  84.2 10.3 %collective-permute-start.6 = (bf16[4,2,128,128]{3,2,1,0:T(8,128)(2,1)S(1)}, bf16[4,2,128,128]{3,2,1,0:T(8,128)(2,1)S(1)}, u32[]{:S(2)}, u32[]{:S(2)}) collective-permute-start(bf16[4,2,128,128]{3,2,1,0:T(8,128)(2,1)S(1)} %get-tuple-element.30), channel_id=1, source_target_pairs={{0,1},{1,2},{2,3},{3,0},{4,5},{5,6},{6,7},{7,4},{8,9},{9,10},{10,1... | collective-permute-start | bytes 786440 | tf_op jit(solution)/shard_map/ppermute | solution.py:509
  84.3 10.2 %collective-permute-start.7 = (bf16[4,2,128,128]{3,2,1,0:T(8,128)(2,1)S(1)}, bf16[4,2,128,128]{3,2,1,0:T(8,128)(2,1)S(1)}, u32[]{:S(2)}, u32[]{:S(2)}) collective-permute-start(bf16[4,2,128,128]{3,2,1,0:T(8,128)(2,1)S(1)} %get-tuple-element.31), channel_id=1, source_target_pairs={{0,3},{1,0},{2,1},{3,2},{4,7},{5,4},{6,5},{7,6},{8,11},{9,8},{10,9... | collective-permute-start | bytes 786440 | tf_op jit(solution)/shard_map/ppermute | solution.py:509
  89.2 10.9 %collective-permute-start.4 = (bf16[4,2,128,128]{3,2,1,0:T(8,128)(2,1)S(1)}, bf16[4,2,128,128]{3,2,1,0:T(8,128)(2,1)S(1)}, u32[]{:S(2)}, u32[]{:S(2)}) collective-permute-start(bf16[4,2,128,128]{3,2,1,0:T(8,128)(2,1)S(1)} %get-tuple-element.26), channel_id=1, source_target_pairs={{0,1},{1,2},{2,3},{3,0},{4,5},{5,6},{6,7},{7,4},{8,9},{9,10},{10,1... | collective-permute-start | bytes 786440 | tf_op jit(solution)/shard_map/ppermute | solution.py:509
  89.3 10.9 %collective-permute-start.5 = (bf16[4,2,128,128]{3,2,1,0:T(8,128)(2,1)S(1)}, bf16[4,2,128,128]{3,2,1,0:T(8,128)(2,1)S(1)}, u32[]{:S(2)}, u32[]{:S(2)}) collective-permute-start(bf16[4,2,128,128]{3,2,1,0:T(8,128)(2,1)S(1)} %get-tuple-element.27), channel_id=1, source_target_pairs={{0,3},{1,0},{2,1},{3,2},{4,7},{5,4},{6,5},{7,6},{8,11},{9,8},{10,9... | collective-permute-start | bytes 786440 | tf_op jit(solution)/shard_map/ppermute | solution.py:509
  94.7 9.9 %collective-permute-start.8 = (bf16[4,2,128,128]{3,2,1,0:T(8,128)(2,1)S(1)}, bf16[4,2,128,128]{3,2,1,0:T(8,128)(2,1)S(1)}, u32[]{:S(2)}, u32[]{:S(2)}) collective-permute-start(bf16[4,2,128,128]{3,2,1,0:T(8,128)(2,1)S(1)} %get-tuple-element.32), channel_id=1, source_target_pairs={{0,1},{1,2},{2,3},{3,0},{4,5},{5,6},{6,7},{7,4},{8,9},{9,10},{10,1... | collective-permute-start | bytes 786440 | tf_op jit(solution)/shard_map/ppermute | solution.py:509
  94.8 9.8 %collective-permute-start.9 = (bf16[4,2,128,128]{3,2,1,0:T(8,128)(2,1)S(1)}, bf16[4,2,128,128]{3,2,1,0:T(8,128)(2,1)S(1)}, u32[]{:S(2)}, u32[]{:S(2)}) collective-permute-start(bf16[4,2,128,128]{3,2,1,0:T(8,128)(2,1)S(1)} %get-tuple-element.33), channel_id=1, source_target_pairs={{0,3},{1,0},{2,1},{3,2},{4,7},{5,4},{6,5},{7,6},{8,11},{9,8},{10,9... | collective-permute-start | bytes 786440 | tf_op jit(solution)/shard_map/ppermute | solution.py:509
